TPU v7x, 32 devices: a whole 2x2x4 slice. The times are simulated.
32 devices in a mesh: aux: 8 (over y, x, core), orb: 4 (over z).
Axes of the slice: x: 2, y: 2, z: 4, core: 2. Of those that a mesh axis runs over, the one named last changes fastest.
Arguments:
- band_pattern: int32 [64, 4], P('aux'), may hold values 0 or 1
- density_in: bfloat16 [64, 4, 128, 128], P('aux', 'orb')
- field_terms: bfloat16 [2, 64, 4, 128, 128], P(None, 'aux', 'orb'), may hold values from -3 to 3
- fit_blocks: int32 [1], replicated, may hold values from 0 to 63
- tensor: bfloat16 [1, 3072, 4, 16384], P(None, 'aux', 'orb'), may hold values from -0.0234375 to 0.0234375
- metric_inv: float32 [1, 3072, 3072], P(None, 'aux')
Outputs:
- response: bfloat16 [2, 64, 4, 128, 128], P(None, 'aux', 'orb')
- coefficients: float32 [1, 2, 3072], P(None, None, 'aux')
All inputs are finite; a program needn't handle non-finite values. No bound on the sum of `band_pattern` on one device may be relied on, other than what follows from the above.
Results may differ from a plain program's by a relative error of at most 0.0055.
Values may be sent and summed in bfloat16 or wider, within the bound.
No kernel may reach another device: no remote copies, remote signals or barrier semaphores. Data moves between devices by JAX's collectives and lax.ppermute only.
A program may use at most 192 MiB of HBM per device.

v0:
```python
import functools

import jax
import jax.numpy as jnp
from jax import lax
from jax.experimental import pallas as pl
from jax.experimental.pallas import tpu as pltpu
from jax.sharding import PartitionSpec as P


ANY = pl.BlockSpec(memory_space=pl.ANY)
SMEM = pl.BlockSpec(memory_space=pltpu.SMEM)
VMEM = pl.BlockSpec(memory_space=pltpu.VMEM)


def band_keep(band_pattern, first_row, total_rows):
    slot_count = band_pattern.shape[1]
    half_band = slot_count // 2
    row_ids = first_row + jnp.arange(band_pattern.shape[0], dtype=jnp.int32)[:, None]
    columns = row_ids + jnp.arange(slot_count, dtype=jnp.int32)[None, :] - half_band
    return (band_pattern == 1) & (columns >= 0) & (columns < total_rows)


def swap_pairs(count, distance):
    return [(i, i ^ distance) for i in range(count)]


def in_groups(count, group, step):
    group = min(group, count)
    trips = -(-count // group)
    if trips == 1:
        for place in range(count):
            step(place)
        return

    def body(trip, carry):
        start = jnp.minimum(trip * group, count - group)
        for place in range(group):
            step(start + place)
        return carry

    lax.fori_loop(0, trips, body, 0)


def mid_kernel(slots, count_rows, group, plan, scal, keep, *refs):
    half = slots // 2
    blk = refs[0].shape[-1]
    ins, rest = refs[: plan["inputs"]], refs[plan["inputs"] :]
    outs, fits, dens, pert, square, order, sems = rest
    mid_rows = count_rows + 2 * half - 1
    middle, is_a, fit_row, owner = scal[0], scal[1], scal[2], scal[3]

    def cols(slot, width=1):
        return pl.ds(slot * blk, width * blk)

    def wide(ref, row, low, high, head, tail):
        parts = [ref[row, :, cols(low, high - low)]]
        if head:
            parts.insert(0, jnp.zeros((blk, head * blk), jnp.bfloat16))
        if tail:
            parts.append(jnp.zeros((blk, tail * blk), jnp.bfloat16))
        return parts[0] if len(parts) == 1 else jnp.concatenate(parts, 1)

    def add_products(total, lefts, left_row, right, right_row):
        for first in range(0, slots, 2):
            rows, spans = [], []
            for t in (first, first + 1):
                low, high = max(0, t - half), min(slots - 1, slots - 1 + t - half)
                spans.append((t, low, high))
            start, stop = min(v[1] for v in spans), max(v[2] for v in spans)
            for t, low, high in spans:
                u = low - t + half
                rows.append(
                    wide(right, right_row + t, u, u + high - low + 1, low - start, stop - high)
                )
            lhs = [left[left_row, :, cols(first, 2)] for _, left in lefts]
            lhs = lhs[0] if len(lhs) == 1 else jnp.concatenate(lhs, 0)
            value = jnp.dot(lhs, jnp.concatenate(rows, 0), preferred_element_type=jnp.float32)
            for index, (key, _) in enumerate(lefts):
                for s in range(start, stop + 1):
                    part = value[index * blk : (index + 1) * blk, (s - start) * blk : (s - start + 1) * blk]
                    total[key, s] = total[key, s] + part if (key, s) in total else part

    def first_step(j):
        total = {}
        add_products(total, [("square", dens), ("order", pert)], j + half, dens, j)
        add_products(total, [("order", dens)], j + half, pert, j)
        for s in range(slots):
            kept = keep[j, s] != 0
            square[j, :, cols(s)] = jnp.where(kept, total["square", s], 0.0).astype(jnp.bfloat16)
            order[j, :, cols(s)] = jnp.where(kept, total["order", s], 0.0).astype(jnp.bfloat16)

    def second_step(i):
        j = i + half
        total = {}
        add_products(total, [("second", square)], j, order, i)
        add_products(total, [("second", order)], j, square, i)
        for s in range(slots):
            twice = 2.0 * order[j, :, cols(s)].astype(jnp.float32)
            value = jnp.where(keep[j, s] != 0, twice - total["second", s], 0.0).astype(jnp.bfloat16)
            outs[jnp.where(is_a != 0, (s - (half - 1)) % slots, (half - s) % slots), i] = value

    @pl.when(middle != 0)
    def _():
        copies = []
        for kind, field, distance, source, start, size, row in plan["moves"]:
            low, high = half - 1 - distance, half + distance
            slot = jnp.where((is_a != 0) == (kind == "near"), low, high)
            target = pert if field else dens
            copies.append(
                pltpu.make_async_copy(
                    ins[source].at[pl.ds(start, size)],
                    target.at[pl.ds(row, size), :, pl.ds(pl.multiple_of(slot * blk, blk), blk)],
                    sems.at[len(copies)],
                )
            )
        for copy in copies:
            copy.start()
        for copy in copies:
            copy.wait()
        in_groups(mid_rows, group, first_step)
        in_groups(count_rows, group, second_step)
        for step in range(slots):
            value = outs[step, fit_row].astype(jnp.float32)
            fits[step] = jnp.where(owner != 0, value, 0.0).astype(jnp.bfloat16)

    @pl.when(middle == 0)
    def _():
        outs[...] = jnp.zeros_like(outs)
        fits[...] = jnp.zeros_like(fits)


def preload_kernel(steps, *refs):
    count = len(refs) // 2
    sources, targets, sems = refs[:count], refs[count : 2 * count], refs[2 * count]
    copies = []
    for source, target in zip(sources, targets):
        height = source.shape[0] // steps
        for step in range(steps):
            rows = pl.ds(step * height, height)
            copies.append(pltpu.make_async_copy(source.at[rows], target.at[rows], sems.at[len(copies)]))
    for copy in copies:
        copy.start()
    for copy in copies:
        copy.wait()


def sums_kernel(place, *refs):
    pieces, (tensor, out) = refs[:-2], refs[-2:]
    pairs = pieces[0][...]
    for piece in pieces[1:]:
        pairs = pairs + piece[...]
    out[...] = jnp.zeros_like(out)
    flat = pairs.reshape(pairs.shape[0], -1)
    out[place[0]] = lax.dot_general(
        flat, tensor[...], (((1,), (1,)), ((), ())), preferred_element_type=jnp.float32
    )


def metric_kernel(*refs):
    pieces, (metric, out) = refs[:-2], refs[-2:]
    sums = pieces[0][...]
    for piece in pieces[1:]:
        sums = sums + piece[...]
    groups, fields, width = sums.shape
    lanes = 128
    totals = [jnp.zeros((out.shape[1], lanes), jnp.float32) for _ in range(fields)]
    full = [
        jnp.concatenate([sums[group, field : field + 1, :] for group in range(groups)], 1)
        for field in range(fields)
    ]
    for start in range(0, groups * width, lanes):
        tile = metric[:, start : start + lanes]
        for field in range(fields):
            totals[field] = totals[field] + tile * full[field][:, start : start + lanes]
    for field in range(fields):
        out[field, :] = jnp.sum(totals[field].T, axis=0)


def on_device(band_pattern, density_in, field_terms, fit_blocks, tensor, metric_inv):
    count_rows = density_in.shape[0]
    blk = density_in.shape[-1]
    fields = field_terms.shape[0]
    slots = lax.axis_size("orb")
    half = slots // 2
    aux_count = lax.axis_size("aux")
    total_rows = count_rows * aux_count
    my_aux = lax.axis_index("aux")
    my_slot = lax.axis_index("orb")
    first_row = my_aux * count_rows
    side_a, side_b = half - 1, half
    is_a = my_slot < half
    middle = (my_slot == side_a) | (my_slot == side_b)
    zero_half = jnp.zeros((), jnp.bfloat16)
    up_rows, down_rows = 2 * half, 2 * half - 2
    forward = [(i, i + 1) for i in range(aux_count - 1)]
    backward = [(i + 1, i) for i in range(aux_count - 1)]

    keep_rows = band_keep(band_pattern, first_row, total_rows)
    keep_own = lax.dynamic_index_in_dim(keep_rows, my_slot, 1, keepdims=False)[:, None, None]
    density = jnp.where(keep_own, density_in[:, 0], zero_half)

    def with_field(index):
        picked = lax.dynamic_index_in_dim(field_terms, index, 0, keepdims=False)[:, 0]
        return jnp.concatenate([density, jnp.where(keep_own, picked, zero_half)], 0)

    near = with_field(jnp.where(is_a, 0, 1))
    far = with_field(jnp.where(is_a, 1, 0))

    inputs, moves = [], []

    def stage_rims(pieces, extra=None):
        split = lambda rows: (rows[:count_rows], rows[count_rows:])
        low = [part[count_rows - up_rows :] for _, _, rows in pieces for part in split(rows)]
        high = [part[:down_rows] for _, _, rows in pieces for part in split(rows)]
        if extra is not None:
            low, high = low + [extra], high + [extra]
        low = lax.ppermute(jnp.concatenate(low, 0), "aux", forward)
        high = lax.ppermute(jnp.concatenate(high, 0), "aux", backward)
        for source, size, row in ((low, up_rows, 0), (high, down_rows, up_rows + count_rows)):
            for index, (kind, distance, _) in enumerate(pieces):
                for field in range(2):
                    start = (2 * index + field) * size
                    moves.append((kind, field, distance, len(inputs), start, size, row))
            inputs.append(source)
        for kind, distance, rows in pieces:
            for field in range(2):
                moves.append((kind, field, distance, len(inputs), field * count_rows, count_rows, up_rows))
            inputs.append(rows)
        return low, high

    near_got, far_got = {0: near}, {}
    for distance in range(half):
        if distance:
            near_got[distance] = lax.ppermute(near, "orb", [(side_a - distance, side_a), (side_b + distance, side_b)])
        far_got[distance] = lax.ppermute(
            far, "orb", [(side_a - distance, side_b), (side_b + distance, side_a)]
        )
    pattern = jnp.pad(
        band_pattern.astype(jnp.bfloat16), ((0, blk - count_rows), (0, blk - slots))
    )[None]
    low, high = stage_rims([("near", 0, near)], pattern)
    held = (tensor.reshape(tensor.shape[1], -1), metric_inv[0])
    steps = max(count for count in (1, 2, 4, 8) if held[0].shape[0] % (16 * count) == 0)
    held = pl.pallas_call(
        functools.partial(preload_kernel, steps),
        out_shape=[jax.ShapeDtypeStruct(value.shape, value.dtype) for value in held],
        in_specs=[pl.BlockSpec(memory_space=pltpu.HBM)] * 2,
        out_specs=[VMEM] * 2,
        scratch_shapes=[pltpu.SemaphoreType.DMA((2 * steps,))],
        compiler_params=pltpu.CompilerParams(vmem_limit_bytes=4 << 20),
        name="preload",
    )(*held)
    integrals, metric = (pltpu.with_memory_space_constraint(value, pltpu.VMEM) for value in held)
    pattern_low = low[-1, count_rows - half : count_rows, :slots].astype(jnp.int32)
    pattern_high = high[-1, : half - 1, :slots].astype(jnp.int32)
    for distance in range(1, half):
        stage_rims(
            [("near", distance, near_got[distance]), ("far", distance - 1, far_got[distance - 1])]
        )
    stage_rims([("far", half - 1, far_got[half - 1])])

    pattern_wide = jnp.concatenate([pattern_low, band_pattern, pattern_high], 0)
    keep_wide = band_keep(pattern_wide, first_row - half, total_rows).astype(jnp.int32)
    owner = fit_blocks[0] // count_rows == my_aux
    scal = jnp.stack(
        [middle.astype(jnp.int32), is_a.astype(jnp.int32), fit_blocks[0] % count_rows, owner.astype(jnp.int32)]
    )
    wide_rows = count_rows + up_rows + down_rows
    mid_rows = count_rows + 2 * half - 1
    plan = {"inputs": len(inputs), "moves": tuple(moves)}
    out_shape = [
        jax.ShapeDtypeStruct((slots, count_rows, blk, blk), jnp.bfloat16),
        jax.ShapeDtypeStruct((slots, blk, blk), jnp.bfloat16),
    ]
    blocks = 2 * (wide_rows + mid_rows) * slots + 2 * slots * (count_rows + 1)
    parts, fit_parts = pl.pallas_call(
        functools.partial(mid_kernel, slots, count_rows, 4 if slots <= 4 else 1, plan),
        out_shape=out_shape,
        in_specs=[SMEM, SMEM] + [ANY] * len(inputs),
        out_specs=[VMEM] * 2,
        scratch_shapes=[
            pltpu.VMEM((wide_rows, blk, slots * blk), jnp.bfloat16),
            pltpu.VMEM((wide_rows, blk, slots * blk), jnp.bfloat16),
            pltpu.VMEM((mid_rows, blk, slots * blk), jnp.bfloat16),
            pltpu.VMEM((mid_rows, blk, slots * blk), jnp.bfloat16),
            pltpu.SemaphoreType.DMA((len(moves),)),
        ],
        compiler_params=pltpu.CompilerParams(vmem_limit_bytes=blocks * blk * blk * 2 + (4 << 20)),
        name="mid_products",
    )(scal, keep_wide, *inputs)

    def scatter(blocks):
        got = [blocks[0]]
        for step in range(1, slots):
            pairs = [(side_a, (side_a + step) % slots), (side_b, (side_b - step) % slots)]
            got.append(lax.ppermute(blocks[step], "orb", pairs))
        picked = []
        for wanted in ((my_slot - side_a) % slots, (side_b - my_slot) % slots):
            value = got[0]
            for step in range(1, slots):
                value = jnp.where(wanted == step, got[step], value)
            picked.append(value)
        return jnp.stack(picked, 0)

    fit_own = scatter(fit_parts)
    response = scatter(parts)[:, :, None]
    fit_own = fit_own + lax.ppermute(fit_own, "aux", swap_pairs(aux_count, 1))
    fit_pieces = [fit_own] + [
        lax.ppermute(fit_own, "aux", swap_pairs(aux_count, distance)) for distance in range(2, aux_count, 2)
    ]

    aux_rows = integrals.shape[0]
    sums = pl.pallas_call(
        sums_kernel,
        out_shape=jax.ShapeDtypeStruct((aux_count, fields, aux_rows), jnp.float32),
        in_specs=[SMEM] + [VMEM] * (len(fit_pieces) + 1),
        out_specs=VMEM,
        compiler_params=pltpu.CompilerParams(vmem_limit_bytes=8 << 20),
        name="fit_sums",
    )(my_aux.astype(jnp.int32)[None], *fit_pieces, integrals)
    sums = sums + lax.ppermute(sums, "aux", swap_pairs(aux_count, 1))
    pieces = [sums] + [
        lax.ppermute(sums, "aux", swap_pairs(aux_count, distance)) for distance in range(2, aux_count, 2)
    ]
    part = pl.pallas_call(
        metric_kernel,
        out_shape=jax.ShapeDtypeStruct((fields, metric.shape[0]), jnp.float32),
        in_specs=[VMEM] * (len(pieces) + 1),
        out_specs=VMEM,
        compiler_params=pltpu.CompilerParams(vmem_limit_bytes=8 << 20),
        name="metric",
    )(*pieces, metric)
    got = [part] + [
        lax.ppermute(part, "orb", [(i, (i + step) % slots) for i in range(slots)]) for step in range(1, slots)
    ]
    coefficients = None
    for plane in range(slots):
        value = got[0]
        for step in range(1, slots):
            value = jnp.where((my_slot - plane) % slots == step, got[step], value)
        coefficients = value if coefficients is None else coefficients + value
    return (response, coefficients[None])


def solution(mesh):
    in_specs = (
        P("aux", None),
        P("aux", "orb", None, None),
        P(None, "aux", "orb", None, None),
        P(),
        P(None, "aux", "orb", None),
        P(None, "aux", None),
    )
    out_specs = (P(None, "aux", "orb", None, None), P(None, None, "aux"))

    return jax.shard_map(on_device, mesh=mesh, in_specs=in_specs, out_specs=out_specs, check_vma=False)
```

profile of v0, /device:TPU:0, one launch (start us, length us, event | category | flops | bytes accessed | tf_op | source)
XLA Modules:
  0.0 112.3 jit_solution(10972058072543107733)
XLA Ops:
  0.7 0.7 fusion.20
  1.4 1.2 %bitcast_select_fusion.2 = (bf16[8,128,128]{2,1,0:T(8,128)(2,1)S(1)}, bf16[8,128,128]{2,1,0:T(8,128)(2,1)S(1)}, bf16[8,128,128]{2,1,0:T(8,128)(2,1)S(1)}) fusion(bf16[2,8,1,128,128]{4,3,2,1,0:T(8,128)(2,1)} %param.8, s32[]{:T(128)S(6)} %select_n.235, pred[8]{0:T(512)(128)(4,1)S(1)} %dynamic-slice_bitcast_fusion, s32[]{:T(128)S(6)} %select_n.233, ...), kind=kLoop, calls=%fused_computation.15 | loop fusion | flops 393216 | bytes 1572880 | tf_op jit(solution)/shard_map/jit(_where)/select_n | solution.py:205
  2.6 0.9 pad_maximum_fusion
  3.5 0.7 collective-permute-start.3
  4.2 7.7 %collective-permute-start.6 = (bf16[16,128,128]{2,1,0:T(8,128)(2,1)}, bf16[16,128,128]{2,1,0:T(8,128)(2,1)S(1)}, u32[]{:S(2)}, u32[]{:S(2)}) collective-permute-start(bf16[16,128,128]{2,1,0:T(8,128)(2,1)} %get-tuple-element.37), channel_id=1, source_target_pairs={{0,2},{3,1},{4,6},{7,5},{8,10},{11,9},{12,14},{15,13},{16,18},{19,... | collective-permute-start | bytes 1572872 | tf_op jit(solution)/shard_map/ppermute | solution.py:236
  11.8 0.7 convert_element_type.31
  12.6 0.7 pad_maximum_fusion.6
  13.3 1.3 %collective-permute-start.1 = (bf16[5,128,128]{2,1,0:T(8,128)(2,1)}, bf16[5,128,128]{2,1,0:T(8,128)(2,1)S(1)}, u32[]{:S(2)}, u32[]{:S(2)}) collective-permute-start(bf16[5,128,128]{2,1,0:T(8,128)(2,1)} %pad_maximum_fusion.6), channel_id=1, source_target_pairs={{4,0},{8,4},{12,8},{16,12},{20,16},{24,20},{28,24},{5,1},{9,5},{13... | collective-permute-start | bytes 491528 | tf_op jit(solution)/shard_map/ppermute | solution.py:219
  14.7 3.0 %collective-permute-start = (bf16[9,128,128]{2,1,0:T(8,128)(2,1)S(1)}, bf16[9,128,128]{2,1,0:T(8,128)(2,1)S(1)}, u32[]{:S(2)}, u32[]{:S(2)}) collective-permute-start(bf16[9,128,128]{2,1,0:T(8,128)(2,1)S(1)} %pad_maximum_fusion.3), channel_id=1, source_target_pairs={{0,4},{4,8},{8,12},{12,16},{16,20},{20,24},{24,28},{1,5},{5,9},{9,... | collective-permute-start | bytes 884744 | tf_op jit(solution)/shard_map/ppermute | solution.py:218
  17.8 1.4 %collective-permute-start.2 = (bf16[16,128,128]{2,1,0:T(8,128)(2,1)S(1)}, bf16[16,128,128]{2,1,0:T(8,128)(2,1)S(1)}, u32[]{:S(2)}, u32[]{:S(2)}) collective-permute-start(bf16[16,128,128]{2,1,0:T(8,128)(2,1)S(1)} %get-tuple-element.38.refs_2_), channel_id=1, source_target_pairs={{0,1},{3,2},{4,5},{7,6},{8,9},{11,10},{12,13},{15,14},{16,17},{19,... | collective-permute-start | bytes 1572872 | tf_op jit(solution)/shard_map/ppermute | solution.py:235
  19.9 0.8 copy.20
  20.8 13.4 %collective-permute-done.2.refs_5_ = bf16[16,128,128]{2,1,0:T(8,128)(2,1)S(1)} collective-permute-done((bf16[16,128,128]{2,1,0:T(8,128)(2,1)S(1)}, bf16[16,128,128]{2,1,0:T(8,128)(2,1)S(1)}, u32[]{:S(2)}, u32[]{:S(2)}) %collective-permute-start.2) | collective-permute-done | bytes 524320 | tf_op jit(solution)/shard_map/ppermute | solution.py:235
  34.3 1.3 %collective-permute-start.4 = (bf16[16,128,128]{2,1,0:T(8,128)(2,1)S(1)}, bf16[16,128,128]{2,1,0:T(8,128)(2,1)S(1)}, u32[]{:S(2)}, u32[]{:S(2)}) collective-permute-start(bf16[16,128,128]{2,1,0:T(8,128)(2,1)S(1)} %pad_maximum_fusion.2), channel_id=1, source_target_pairs={{0,4},{4,8},{8,12},{12,16},{16,20},{20,24},{24,28},{1,5},{5,9},{9,... | collective-permute-start | bytes 1572872 | tf_op jit(solution)/shard_map/ppermute | solution.py:218
  35.7 1.3 %collective-permute-start.5 = (bf16[8,128,128]{2,1,0:T(8,128)(2,1)S(1)}, bf16[8,128,128]{2,1,0:T(8,128)(2,1)S(1)}, u32[]{:S(2)}, u32[]{:S(2)}) collective-permute-start(bf16[8,128,128]{2,1,0:T(8,128)(2,1)S(1)} %pad_maximum_fusion.4), channel_id=1, source_target_pairs={{4,0},{8,4},{12,8},{16,12},{20,16},{24,20},{28,24},{5,1},{9,5},{13... | collective-permute-start | bytes 786440 | tf_op jit(solution)/shard_map/ppermute | solution.py:219
  37.1 4.7 %collective-permute-start.7 = (bf16[8,128,128]{2,1,0:T(8,128)(2,1)S(1)}, bf16[8,128,128]{2,1,0:T(8,128)(2,1)S(1)}, u32[]{:S(2)}, u32[]{:S(2)}) collective-permute-start(bf16[8,128,128]{2,1,0:T(8,128)(2,1)S(1)} %pad_maximum_fusion.5), channel_id=1, source_target_pairs={{0,4},{4,8},{8,12},{12,16},{16,20},{20,24},{24,28},{1,5},{5,9},{9,... | collective-permute-start | bytes 786440 | tf_op jit(solution)/shard_map/ppermute | solution.py:218
  41.9 1.3 %collective-permute-start.8 = (bf16[4,128,128]{2,1,0:T(8,128)(2,1)S(1)}, bf16[4,128,128]{2,1,0:T(8,128)(2,1)S(1)}, u32[]{:S(2)}, u32[]{:S(2)}) collective-permute-start(bf16[4,128,128]{2,1,0:T(8,128)(2,1)S(1)} %pad_maximum_fusion.7), channel_id=1, source_target_pairs={{4,0},{8,4},{12,8},{16,12},{20,16},{24,20},{28,24},{5,1},{9,5},{13... | collective-permute-start | bytes 393224 | tf_op jit(solution)/shard_map/ppermute | solution.py:219
  43.2 3.1 %collective-permute-done.8.refs_8_ = bf16[4,128,128]{2,1,0:T(8,128)(2,1)S(1)} collective-permute-done((bf16[4,128,128]{2,1,0:T(8,128)(2,1)S(1)}, bf16[4,128,128]{2,1,0:T(8,128)(2,1)S(1)}, u32[]{:S(2)}, u32[]{:S(2)}) %collective-permute-start.8) | collective-permute-done | bytes 131104 | tf_op jit(solution)/shard_map/ppermute | solution.py:219
  46.4 0.9 copy-done.3
  47.3 1.0 mid_products.1
  49.0 1.3 %collective-permute-start.12 = (bf16[128,128]{1,0:T(8,128)(2,1)S(1)}, bf16[128,128]{1,0:T(8,128)(2,1)S(1)}, u32[]{:S(2)}, u32[]{:S(2)}) collective-permute-start(bf16[128,128]{1,0:T(8,128)(2,1)S(1)} %get-tuple-element.43), channel_id=1, source_target_pairs={{1,0},{2,3},{5,4},{6,7},{9,8},{10,11},{13,12},{14,15},{17,16},{18,... | collective-permute-start | bytes 98312 | tf_op jit(solution)/shard_map/ppermute | solution.py:297
  50.3 1.3 %collective-permute-start.13 = (bf16[128,128]{1,0:T(8,128)(2,1)S(1)}, bf16[128,128]{1,0:T(8,128)(2,1)S(1)}, u32[]{:S(2)}, u32[]{:S(2)}) collective-permute-start(bf16[128,128]{1,0:T(8,128)(2,1)S(1)} %get-tuple-element.42), channel_id=1, source_target_pairs={{1,3},{2,0},{5,7},{6,4},{9,11},{10,8},{13,15},{14,12},{17,19},{18,... | collective-permute-start | bytes 98312 | tf_op jit(solution)/shard_map/ppermute | solution.py:297
  52.3 7.3 %collective-permute-done.12 = bf16[128,128]{1,0:T(8,128)(2,1)S(1)} collective-permute-done((bf16[128,128]{1,0:T(8,128)(2,1)S(1)}, bf16[128,128]{1,0:T(8,128)(2,1)S(1)}, u32[]{:S(2)}, u32[]{:S(2)}) %collective-permute-start.12) | collective-permute-done | bytes 32800 | tf_op jit(solution)/shard_map/ppermute | solution.py:297
  59.5 2.3 %collective-permute-done.13 = bf16[128,128]{1,0:T(8,128)(2,1)S(1)} collective-permute-done((bf16[128,128]{1,0:T(8,128)(2,1)S(1)}, bf16[128,128]{1,0:T(8,128)(2,1)S(1)}, u32[]{:S(2)}, u32[]{:S(2)}) %collective-permute-start.13) | collective-permute-done | bytes 32800 | tf_op jit(solution)/shard_map/ppermute | solution.py:297
  61.9 0.8 fusion.8
  62.7 4.1 %collective-permute-start.15 = (bf16[2,128,128]{2,1,0:T(8,128)(2,1)S(1)}, bf16[2,128,128]{2,1,0:T(8,128)(2,1)S(1)}, u32[]{:S(2)}, u32[]{:S(2)}) collective-permute-start(bf16[2,128,128]{2,1,0:T(8,128)(2,1)S(1)} %pad_maximum_fusion.8), channel_id=1, source_target_pairs={{0,4},{4,0},{8,12},{12,8},{16,20},{20,16},{24,28},{28,24},{1,5},{5... | collective-permute-start | bytes 196616 | tf_op jit(solution)/shard_map/ppermute | solution.py:308
  66.8 0.9 collective-permute-done.15
  67.7 3.2 %collective-permute-start.16 = (bf16[2,128,128]{2,1,0:T(8,128)(2,1)S(1)}, bf16[2,128,128]{2,1,0:T(8,128)(2,1)S(1)}, u32[]{:S(2)}, u32[]{:S(2)}) collective-permute-start(bf16[2,128,128]{2,1,0:T(8,128)(2,1)S(1)} %fusion.23.refs_0_), channel_id=1, source_target_pairs={{0,8},{4,12},{8,0},{12,4},{16,24},{20,28},{24,16},{28,20},{1,9},{5... | collective-permute-start | bytes 196616 | tf_op jit(solution)/shard_map/ppermute | solution.py:310
  70.9 1.1 %collective-permute-start.17 = (bf16[2,128,128]{2,1,0:T(8,128)(2,1)S(1)}, bf16[2,128,128]{2,1,0:T(8,128)(2,1)S(1)}, u32[]{:S(2)}, u32[]{:S(2)}) collective-permute-start(bf16[2,128,128]{2,1,0:T(8,128)(2,1)S(1)} %fusion.23.refs_0_), channel_id=1, source_target_pairs={{0,16},{4,20},{8,24},{12,28},{16,0},{20,4},{24,8},{28,12},{1,17},{... | collective-permute-start | bytes 196616 | tf_op jit(solution)/shard_map/ppermute | solution.py:310
  72.0 1.4 %collective-permute-start.18 = (bf16[2,128,128]{2,1,0:T(8,128)(2,1)S(1)}, bf16[2,128,128]{2,1,0:T(8,128)(2,1)S(1)}, u32[]{:S(2)}, u32[]{:S(2)}) collective-permute-start(bf16[2,128,128]{2,1,0:T(8,128)(2,1)S(1)} %fusion.23.refs_0_), channel_id=1, source_target_pairs={{0,24},{4,28},{8,16},{12,20},{16,8},{20,12},{24,0},{28,4},{1,25},{... | collective-permute-start | bytes 196616 | tf_op jit(solution)/shard_map/ppermute | solution.py:310
  73.4 4.6 %copy-done = bf16[1,384,1,16384]{3,1,2,0:T(8,128)(2,1)S(1)} copy-done((bf16[1,384,1,16384]{3,1,2,0:T(8,128)(2,1)S(1)}, bf16[1,384,1,16384]{3,1,2,0:T(8,128)(2,1)}, u32[]{:S(2)}) %copy-start) | copy-done | bytes 12582936
  78.0 2.3 %copy-done.1 = f32[1,384,3072]{2,1,0:T(8,128)S(1)} copy-done((f32[1,384,3072]{2,1,0:T(8,128)S(1)}, f32[1,384,3072]{2,1,0:T(8,128)}, u32[]{:S(2)}) %copy-start.1) | copy-done | bytes 4718616
  80.3 2.0 %preload.1 = (bf16[384,16384]{1,0:T(8,128)(2,1)S(1)}, f32[384,3072]{1,0:T(8,128)S(1)}) custom-call(bf16[384,16384]{1,0:T(8,128)(2,1)S(1)} %bitcast.88, f32[384,3072]{1,0:T(8,128)S(1)} %bitcast.89), custom_call_target="tpu_custom_call" | custom-call | tf_op jit(solution)/shard_map/preload/pallas_call | solution.py:245
  82.3 3.3 %fit_sums.1 = f32[8,2,384]{2,1,0:T(2,128)S(1)} custom-call(s32[1]{0:T(128)} %bitcast.20.place, bf16[2,128,128]{2,1,0:T(8,128)(2,1)S(1)} %fusion.23.refs_0_, bf16[2,128,128]{2,1,0:T(8,128)(2,1)S(1)} %collective-permute-done.16.refs_1_, bf16[2,128,128]{2,1,0:T(8,128)(2,1)S(1)} %collective-permute-done.17.refs_2_, ...), custom_call_target="tpu_custom_call" | custom-call | tf_op jit(solution)/shard_map/fit_sums/pallas_call | solution.py:314
  85.7 1.2 %collective-permute-done.19 = f32[8,2,384]{2,1,0:T(2,128)S(1)} collective-permute-done((f32[8,2,384]{2,1,0:T(2,128)S(1)}, f32[8,2,384]{2,1,0:T(2,128)S(1)}, u32[]{:S(2)}, u32[]{:S(2)}) %collective-permute-start.19) | collective-permute-done | bytes 24608 | tf_op jit(solution)/shard_map/ppermute | solution.py:322
  86.9 1.1 collective-permute-start.20
  88.0 1.3 %collective-permute-start.9 = (bf16[8,128,128]{2,1,0:T(8,128)(2,1)S(1)}, bf16[8,128,128]{2,1,0:T(8,128)(2,1)S(1)}, u32[]{:S(2)}, u32[]{:S(2)}) collective-permute-start(bf16[8,128,128]{2,1,0:T(8,128)(2,1)S(1)} %get-tuple-element.22), channel_id=1, source_target_pairs={{1,0},{2,3},{5,4},{6,7},{9,8},{10,11},{13,12},{14,15},{17,16},{18,... | collective-permute-start | bytes 786440 | tf_op jit(solution)/shard_map/ppermute | solution.py:297
  89.3 1.3 %collective-permute-start.10 = (bf16[8,128,128]{2,1,0:T(8,128)(2,1)S(1)}, bf16[8,128,128]{2,1,0:T(8,128)(2,1)S(1)}, u32[]{:S(2)}, u32[]{:S(2)}) collective-permute-start(bf16[8,128,128]{2,1,0:T(8,128)(2,1)S(1)} %get-tuple-element.21), channel_id=1, source_target_pairs={{1,3},{2,0},{5,7},{6,4},{9,11},{10,8},{13,15},{14,12},{17,19},{18,... | collective-permute-start | bytes 786440 | tf_op jit(solution)/shard_map/ppermute | solution.py:297
  90.6 0.7 collective-permute-start.11
  91.3 1.2 %collective-permute-start.21 = (f32[8,2,384]{2,1,0:T(2,128)S(1)}, f32[8,2,384]{2,1,0:T(2,128)S(1)}, u32[]{:S(2)}, u32[]{:S(2)}) collective-permute-start(f32[8,2,384]{2,1,0:T(2,128)S(1)} %add.125.refs_0_), channel_id=1, source_target_pairs={{0,16},{4,20},{8,24},{12,28},{16,0},{20,4},{24,8},{28,12},{1,17},{... | collective-permute-start | bytes 73736 | tf_op jit(solution)/shard_map/ppermute | solution.py:324
  92.5 1.4 %collective-permute-start.22 = (f32[8,2,384]{2,1,0:T(2,128)S(1)}, f32[8,2,384]{2,1,0:T(2,128)S(1)}, u32[]{:S(2)}, u32[]{:S(2)}) collective-permute-start(f32[8,2,384]{2,1,0:T(2,128)S(1)} %add.125.refs_0_), channel_id=1, source_target_pairs={{0,24},{4,28},{8,16},{12,20},{16,8},{20,12},{24,0},{28,4},{1,25},{... | collective-permute-start | bytes 73736 | tf_op jit(solution)/shard_map/ppermute | solution.py:324
  94.0 1.2 %collective-permute-done.21.refs_2_ = f32[8,2,384]{2,1,0:T(2,128)S(1)} collective-permute-done((f32[8,2,384]{2,1,0:T(2,128)S(1)}, f32[8,2,384]{2,1,0:T(2,128)S(1)}, u32[]{:S(2)}, u32[]{:S(2)}) %collective-permute-start.21) | collective-permute-done | bytes 24608 | tf_op jit(solution)/shard_map/ppermute | solution.py:324
  95.2 2.0 %collective-permute-done.22.refs_3_ = f32[8,2,384]{2,1,0:T(2,128)S(1)} collective-permute-done((f32[8,2,384]{2,1,0:T(2,128)S(1)}, f32[8,2,384]{2,1,0:T(2,128)S(1)}, u32[]{:S(2)}, u32[]{:S(2)}) %collective-permute-start.22) | collective-permute-done | bytes 24608 | tf_op jit(solution)/shard_map/ppermute | solution.py:324
  97.2 0.8 metric.1
  98.0 1.5 %collective-permute-start.23 = (f32[2,384]{1,0:T(2,128)S(1)}, f32[2,384]{1,0:T(2,128)S(1)}, u32[]{:S(2)}, u32[]{:S(2)}) collective-permute-start(f32[2,384]{1,0:T(2,128)S(1)} %metric.1), channel_id=1, source_target_pairs={{0,3},{1,0},{2,1},{3,2},{4,7},{5,4},{6,5},{7,6},{8,11},{9,8},{10,9... | collective-permute-start | bytes 9224 | tf_op jit(solution)/shard_map/ppermute | solution.py:335
  99.5 5.8 %collective-permute-start.24 = (f32[2,384]{1,0:T(2,128)S(1)}, f32[2,384]{1,0:T(2,128)S(1)}, u32[]{:S(2)}, u32[]{:S(2)}) collective-permute-start(f32[2,384]{1,0:T(2,128)S(1)} %metric.1), channel_id=1, source_target_pairs={{0,2},{1,3},{2,0},{3,1},{4,6},{5,7},{6,4},{7,5},{8,10},{9,11},{10,... | collective-permute-start | bytes 9224 | tf_op jit(solution)/shard_map/ppermute | solution.py:335
  105.4 2.0 %collective-permute-start.25 = (f32[2,384]{1,0:T(2,128)S(1)}, f32[2,384]{1,0:T(2,128)S(1)}, u32[]{:S(2)}, u32[]{:S(2)}) collective-permute-start(f32[2,384]{1,0:T(2,128)S(1)} %metric.1), channel_id=1, source_target_pairs={{0,1},{1,2},{2,3},{3,0},{4,5},{5,6},{6,7},{7,4},{8,9},{9,10},{10,1... | collective-permute-start | bytes 9224 | tf_op jit(solution)/shard_map/ppermute | solution.py:335
  107.4 3.4 %collective-permute-done.25 = f32[2,384]{1,0:T(2,128)S(1)} collective-permute-done((f32[2,384]{1,0:T(2,128)S(1)}, f32[2,384]{1,0:T(2,128)S(1)}, u32[]{:S(2)}, u32[]{:S(2)}) %collective-permute-start.25) | collective-permute-done | bytes 3104 | tf_op jit(solution)/shard_map/ppermute | solution.py:335
  111.5 0.8 maximum_bitcast_fusion
  (57 shorter events, 2.9 us)
Async XLA Ops:
  3.5 17.3 %collective-permute-start.3 = (bf16[16,128,128]{2,1,0:T(8,128)(2,1)}, bf16[16,128,128]{2,1,0:T(8,128)(2,1)S(1)}, u32[]{:S(2)}, u32[]{:S(2)}) collective-permute-start(bf16[16,128,128]{2,1,0:T(8,128)(2,1)} %get-tuple-element.37), channel_id=1, source_target_pairs={{1,2},{2,1},{5,6},{6,5},{9,10},{10,9},{13,14},{14,13},{17,18},{18,... | collective-permute-start | bytes 1572872 | tf_op jit(solution)/shard_map/ppermute | solution.py:236
  4.2 32.8 %collective-permute-start.6 = (bf16[16,128,128]{2,1,0:T(8,128)(2,1)}, bf16[16,128,128]{2,1,0:T(8,128)(2,1)S(1)}, u32[]{:S(2)}, u32[]{:S(2)}) collective-permute-start(bf16[16,128,128]{2,1,0:T(8,128)(2,1)} %get-tuple-element.37), channel_id=1, source_target_pairs={{0,2},{3,1},{4,6},{7,5},{8,10},{11,9},{12,14},{15,13},{16,18},{19,... | collective-permute-start | bytes 1572872 | tf_op jit(solution)/shard_map/ppermute | solution.py:236
  13.3 7.4 %collective-permute-start.1 = (bf16[5,128,128]{2,1,0:T(8,128)(2,1)}, bf16[5,128,128]{2,1,0:T(8,128)(2,1)S(1)}, u32[]{:S(2)}, u32[]{:S(2)}) collective-permute-start(bf16[5,128,128]{2,1,0:T(8,128)(2,1)} %pad_maximum_fusion.6), channel_id=1, source_target_pairs={{4,0},{8,4},{12,8},{16,12},{20,16},{24,20},{28,24},{5,1},{9,5},{13... | collective-permute-start | bytes 491528 | tf_op jit(solution)/shard_map/ppermute | solution.py:219
  14.7 6.0 %collective-permute-start = (bf16[9,128,128]{2,1,0:T(8,128)(2,1)S(1)}, bf16[9,128,128]{2,1,0:T(8,128)(2,1)S(1)}, u32[]{:S(2)}, u32[]{:S(2)}) collective-permute-start(bf16[9,128,128]{2,1,0:T(8,128)(2,1)S(1)} %pad_maximum_fusion.3), channel_id=1, source_target_pairs={{0,4},{4,8},{8,12},{12,16},{16,20},{20,24},{24,28},{1,5},{5,9},{9,... | collective-permute-start | bytes 884744 | tf_op jit(solution)/shard_map/ppermute | solution.py:218
  17.8 16.4 %collective-permute-start.2 = (bf16[16,128,128]{2,1,0:T(8,128)(2,1)S(1)}, bf16[16,128,128]{2,1,0:T(8,128)(2,1)S(1)}, u32[]{:S(2)}, u32[]{:S(2)}) collective-permute-start(bf16[16,128,128]{2,1,0:T(8,128)(2,1)S(1)} %get-tuple-element.38.refs_2_), channel_id=1, source_target_pairs={{0,1},{3,2},{4,5},{7,6},{8,9},{11,10},{12,13},{15,14},{16,17},{19,... | collective-permute-start | bytes 1572872 | tf_op jit(solution)/shard_map/ppermute | solution.py:235
  20.7 25.6 %copy-start.2 = (bf16[5,128,128]{2,1,0:T(8,128)(2,1)}, bf16[5,128,128]{2,1,0:T(8,128)(2,1)S(1)}, u32[]{:S(2)}) copy-start(bf16[5,128,128]{2,1,0:T(8,128)(2,1)S(1)} %collective-permute-done.1.refs_1_) | copy-start | bytes 491524
  34.3 12.1 %collective-permute-start.4 = (bf16[16,128,128]{2,1,0:T(8,128)(2,1)S(1)}, bf16[16,128,128]{2,1,0:T(8,128)(2,1)S(1)}, u32[]{:S(2)}, u32[]{:S(2)}) collective-permute-start(bf16[16,128,128]{2,1,0:T(8,128)(2,1)S(1)} %pad_maximum_fusion.2), channel_id=1, source_target_pairs={{0,4},{4,8},{8,12},{12,16},{16,20},{20,24},{24,28},{1,5},{5,9},{9,... | collective-permute-start | bytes 1572872 | tf_op jit(solution)/shard_map/ppermute | solution.py:218
  35.7 10.6 %collective-permute-start.5 = (bf16[8,128,128]{2,1,0:T(8,128)(2,1)S(1)}, bf16[8,128,128]{2,1,0:T(8,128)(2,1)S(1)}, u32[]{:S(2)}, u32[]{:S(2)}) collective-permute-start(bf16[8,128,128]{2,1,0:T(8,128)(2,1)S(1)} %pad_maximum_fusion.4), channel_id=1, source_target_pairs={{4,0},{8,4},{12,8},{16,12},{20,16},{24,20},{28,24},{5,1},{9,5},{13... | collective-permute-start | bytes 786440 | tf_op jit(solution)/shard_map/ppermute | solution.py:219
  37.1 9.3 %collective-permute-start.7 = (bf16[8,128,128]{2,1,0:T(8,128)(2,1)S(1)}, bf16[8,128,128]{2,1,0:T(8,128)(2,1)S(1)}, u32[]{:S(2)}, u32[]{:S(2)}) collective-permute-start(bf16[8,128,128]{2,1,0:T(8,128)(2,1)S(1)} %pad_maximum_fusion.5), channel_id=1, source_target_pairs={{0,4},{4,8},{8,12},{12,16},{16,20},{20,24},{24,28},{1,5},{5,9},{9,... | collective-permute-start | bytes 786440 | tf_op jit(solution)/shard_map/ppermute | solution.py:218
  41.9 4.5 %collective-permute-start.8 = (bf16[4,128,128]{2,1,0:T(8,128)(2,1)S(1)}, bf16[4,128,128]{2,1,0:T(8,128)(2,1)S(1)}, u32[]{:S(2)}, u32[]{:S(2)}) collective-permute-start(bf16[4,128,128]{2,1,0:T(8,128)(2,1)S(1)} %pad_maximum_fusion.7), channel_id=1, source_target_pairs={{4,0},{8,4},{12,8},{16,12},{20,16},{24,20},{28,24},{5,1},{9,5},{13... | collective-permute-start | bytes 393224 | tf_op jit(solution)/shard_map/ppermute | solution.py:219
  46.3 0.9 copy-start.3
  48.3 0.7 copy-start.4
  49.0 10.6 %collective-permute-start.12 = (bf16[128,128]{1,0:T(8,128)(2,1)S(1)}, bf16[128,128]{1,0:T(8,128)(2,1)S(1)}, u32[]{:S(2)}, u32[]{:S(2)}) collective-permute-start(bf16[128,128]{1,0:T(8,128)(2,1)S(1)} %get-tuple-element.43), channel_id=1, source_target_pairs={{1,0},{2,3},{5,4},{6,7},{9,8},{10,11},{13,12},{14,15},{17,16},{18,... | collective-permute-start | bytes 98312 | tf_op jit(solution)/shard_map/ppermute | solution.py:297
  50.3 11.6 %collective-permute-start.13 = (bf16[128,128]{1,0:T(8,128)(2,1)S(1)}, bf16[128,128]{1,0:T(8,128)(2,1)S(1)}, u32[]{:S(2)}, u32[]{:S(2)}) collective-permute-start(bf16[128,128]{1,0:T(8,128)(2,1)S(1)} %get-tuple-element.42), channel_id=1, source_target_pairs={{1,3},{2,0},{5,7},{6,4},{9,11},{10,8},{13,15},{14,12},{17,19},{18,... | collective-permute-start | bytes 98312 | tf_op jit(solution)/shard_map/ppermute | solution.py:297
  51.6 10.3 %collective-permute-start.14 = (bf16[128,128]{1,0:T(8,128)(2,1)S(1)}, bf16[128,128]{1,0:T(8,128)(2,1)S(1)}, u32[]{:S(2)}, u32[]{:S(2)}) collective-permute-start(bf16[128,128]{1,0:T(8,128)(2,1)S(1)} %get-tuple-element.41), channel_id=1, source_target_pairs={{1,2},{2,1},{5,6},{6,5},{9,10},{10,9},{13,14},{14,13},{17,18},{18,... | collective-permute-start | bytes 98312 | tf_op jit(solution)/shard_map/ppermute | solution.py:297
  62.7 5.0 %collective-permute-start.15 = (bf16[2,128,128]{2,1,0:T(8,128)(2,1)S(1)}, bf16[2,128,128]{2,1,0:T(8,128)(2,1)S(1)}, u32[]{:S(2)}, u32[]{:S(2)}) collective-permute-start(bf16[2,128,128]{2,1,0:T(8,128)(2,1)S(1)} %pad_maximum_fusion.8), channel_id=1, source_target_pairs={{0,4},{4,0},{8,12},{12,8},{16,20},{20,16},{24,28},{28,24},{1,5},{5... | collective-permute-start | bytes 196616 | tf_op jit(solution)/shard_map/ppermute | solution.py:308
  67.7 14.6 %collective-permute-start.16 = (bf16[2,128,128]{2,1,0:T(8,128)(2,1)S(1)}, bf16[2,128,128]{2,1,0:T(8,128)(2,1)S(1)}, u32[]{:S(2)}, u32[]{:S(2)}) collective-permute-start(bf16[2,128,128]{2,1,0:T(8,128)(2,1)S(1)} %fusion.23.refs_0_), channel_id=1, source_target_pairs={{0,8},{4,12},{8,0},{12,4},{16,24},{20,28},{24,16},{28,20},{1,9},{5... | collective-permute-start | bytes 196616 | tf_op jit(solution)/shard_map/ppermute | solution.py:310
  70.9 11.4 %collective-permute-start.17 = (bf16[2,128,128]{2,1,0:T(8,128)(2,1)S(1)}, bf16[2,128,128]{2,1,0:T(8,128)(2,1)S(1)}, u32[]{:S(2)}, u32[]{:S(2)}) collective-permute-start(bf16[2,128,128]{2,1,0:T(8,128)(2,1)S(1)} %fusion.23.refs_0_), channel_id=1, source_target_pairs={{0,16},{4,20},{8,24},{12,28},{16,0},{20,4},{24,8},{28,12},{1,17},{... | collective-permute-start | bytes 196616 | tf_op jit(solution)/shard_map/ppermute | solution.py:310
  72.0 10.3 %collective-permute-start.18 = (bf16[2,128,128]{2,1,0:T(8,128)(2,1)S(1)}, bf16[2,128,128]{2,1,0:T(8,128)(2,1)S(1)}, u32[]{:S(2)}, u32[]{:S(2)}) collective-permute-start(bf16[2,128,128]{2,1,0:T(8,128)(2,1)S(1)} %fusion.23.refs_0_), channel_id=1, source_target_pairs={{0,24},{4,28},{8,16},{12,20},{16,8},{20,12},{24,0},{28,4},{1,25},{... | collective-permute-start | bytes 196616 | tf_op jit(solution)/shard_map/ppermute | solution.py:310
  73.4 4.6 %copy-start = (bf16[1,384,1,16384]{3,1,2,0:T(8,128)(2,1)S(1)}, bf16[1,384,1,16384]{3,1,2,0:T(8,128)(2,1)}, u32[]{:S(2)}) copy-start(bf16[1,384,1,16384]{3,1,2,0:T(8,128)(2,1)} %param.10) | copy-start | bytes 37748740
  78.0 2.3 %copy-start.1 = (f32[1,384,3072]{2,1,0:T(8,128)S(1)}, f32[1,384,3072]{2,1,0:T(8,128)}, u32[]{:S(2)}) copy-start(f32[1,384,3072]{2,1,0:T(8,128)} %param.11) | copy-start | bytes 14155780
  85.7 1.2 %collective-permute-start.19 = (f32[8,2,384]{2,1,0:T(2,128)S(1)}, f32[8,2,384]{2,1,0:T(2,128)S(1)}, u32[]{:S(2)}, u32[]{:S(2)}) collective-permute-start(f32[8,2,384]{2,1,0:T(2,128)S(1)} %fit_sums.1), channel_id=1, source_target_pairs={{0,4},{4,0},{8,12},{12,8},{16,20},{20,16},{24,28},{28,24},{1,5},{5... | collective-permute-start | bytes 73736 | tf_op jit(solution)/shard_map/ppermute | solution.py:322
  86.9 5.6 %collective-permute-start.20 = (f32[8,2,384]{2,1,0:T(2,128)S(1)}, f32[8,2,384]{2,1,0:T(2,128)S(1)}, u32[]{:S(2)}, u32[]{:S(2)}) collective-permute-start(f32[8,2,384]{2,1,0:T(2,128)S(1)} %add.125.refs_0_), channel_id=1, source_target_pairs={{0,8},{4,12},{8,0},{12,4},{16,24},{20,28},{24,16},{28,20},{1,9},{5... | collective-permute-start | bytes 73736 | tf_op jit(solution)/shard_map/ppermute | solution.py:324
  88.0 23.4 %collective-permute-start.9 = (bf16[8,128,128]{2,1,0:T(8,128)(2,1)S(1)}, bf16[8,128,128]{2,1,0:T(8,128)(2,1)S(1)}, u32[]{:S(2)}, u32[]{:S(2)}) collective-permute-start(bf16[8,128,128]{2,1,0:T(8,128)(2,1)S(1)} %get-tuple-element.22), channel_id=1, source_target_pairs={{1,0},{2,3},{5,4},{6,7},{9,8},{10,11},{13,12},{14,15},{17,16},{18,... | collective-permute-start | bytes 786440 | tf_op jit(solution)/shard_map/ppermute | solution.py:297
  89.3 22.1 %collective-permute-start.10 = (bf16[8,128,128]{2,1,0:T(8,128)(2,1)S(1)}, bf16[8,128,128]{2,1,0:T(8,128)(2,1)S(1)}, u32[]{:S(2)}, u32[]{:S(2)}) collective-permute-start(bf16[8,128,128]{2,1,0:T(8,128)(2,1)S(1)} %get-tuple-element.21), channel_id=1, source_target_pairs={{1,3},{2,0},{5,7},{6,4},{9,11},{10,8},{13,15},{14,12},{17,19},{18,... | collective-permute-start | bytes 786440 | tf_op jit(solution)/shard_map/ppermute | solution.py:297
  90.6 20.8 %collective-permute-start.11 = (bf16[8,128,128]{2,1,0:T(8,128)(2,1)S(1)}, bf16[8,128,128]{2,1,0:T(8,128)(2,1)S(1)}, u32[]{:S(2)}, u32[]{:S(2)}) collective-permute-start(bf16[8,128,128]{2,1,0:T(8,128)(2,1)S(1)} %get-tuple-element.20), channel_id=1, source_target_pairs={{1,2},{2,1},{5,6},{6,5},{9,10},{10,9},{13,14},{14,13},{17,18},{18,... | collective-permute-start | bytes 786440 | tf_op jit(solution)/shard_map/ppermute | solution.py:297
  91.3 3.9 %collective-permute-start.21 = (f32[8,2,384]{2,1,0:T(2,128)S(1)}, f32[8,2,384]{2,1,0:T(2,128)S(1)}, u32[]{:S(2)}, u32[]{:S(2)}) collective-permute-start(f32[8,2,384]{2,1,0:T(2,128)S(1)} %add.125.refs_0_), channel_id=1, source_target_pairs={{0,16},{4,20},{8,24},{12,28},{16,0},{20,4},{24,8},{28,12},{1,17},{... | collective-permute-start | bytes 73736 | tf_op jit(solution)/shard_map/ppermute | solution.py:324
  92.5 4.7 %collective-permute-start.22 = (f32[8,2,384]{2,1,0:T(2,128)S(1)}, f32[8,2,384]{2,1,0:T(2,128)S(1)}, u32[]{:S(2)}, u32[]{:S(2)}) collective-permute-start(f32[8,2,384]{2,1,0:T(2,128)S(1)} %add.125.refs_0_), channel_id=1, source_target_pairs={{0,24},{4,28},{8,16},{12,20},{16,8},{20,12},{24,0},{28,4},{1,25},{... | collective-permute-start | bytes 73736 | tf_op jit(solution)/shard_map/ppermute | solution.py:324
  98.0 7.4 %collective-permute-start.23 = (f32[2,384]{1,0:T(2,128)S(1)}, f32[2,384]{1,0:T(2,128)S(1)}, u32[]{:S(2)}, u32[]{:S(2)}) collective-permute-start(f32[2,384]{1,0:T(2,128)S(1)} %metric.1), channel_id=1, source_target_pairs={{0,3},{1,0},{2,1},{3,2},{4,7},{5,4},{6,5},{7,6},{8,11},{9,8},{10,9... | collective-permute-start | bytes 9224 | tf_op jit(solution)/shard_map/ppermute | solution.py:335
  99.5 7.9 %collective-permute-start.24 = (f32[2,384]{1,0:T(2,128)S(1)}, f32[2,384]{1,0:T(2,128)S(1)}, u32[]{:S(2)}, u32[]{:S(2)}) collective-permute-start(f32[2,384]{1,0:T(2,128)S(1)} %metric.1), channel_id=1, source_target_pairs={{0,2},{1,3},{2,0},{3,1},{4,6},{5,7},{6,4},{7,5},{8,10},{9,11},{10,... | collective-permute-start | bytes 9224 | tf_op jit(solution)/shard_map/ppermute | solution.py:335
  105.4 5.4 %collective-permute-start.25 = (f32[2,384]{1,0:T(2,128)S(1)}, f32[2,384]{1,0:T(2,128)S(1)}, u32[]{:S(2)}, u32[]{:S(2)}) collective-permute-start(f32[2,384]{1,0:T(2,128)S(1)} %metric.1), channel_id=1, source_target_pairs={{0,1},{1,2},{2,3},{3,0},{4,5},{5,6},{6,7},{7,4},{8,9},{9,10},{10,1... | collective-permute-start | bytes 9224 | tf_op jit(solution)/shard_map/ppermute | solution.py:335
where the time goes:
time: 113 us; the launch traced here: 112 us
  starting transfers between devices  52.1 us (46%)
  waiting for transfers between devices  35 us (31%)
  local copies, waits for them, and re-layouts  9.54 us (8%)
  Pallas kernels  7.13 us (6%)
  other arithmetic  6.88 us (6%)
  between operations  1.76 us (2%)
    ppermute x1, waiting for transfers between devices, on_device(): lax.ppermute(near, 'orb', [(side_a - distance, side_a), (side_b + distanc...  13.4 us
    ppermute x6, waiting for transfers between devices, scatter(): got.append(lax.ppermute(blocks[step], 'orb', pairs))  9.58 us
    ppermute x3, starting transfers between devices, on_device(): lax.ppermute(part, 'orb', [(i, (i + step) % slots) for i in range(slots)])  9.29 us
    unnamed x11, local copies, waits for them, and re-layouts  9.23 us
    ppermute x3, starting transfers between devices, stage_rims(): low = lax.ppermute(jnp.concatenate(low, 0), 'aux', forward)  9.11 us
    ppermute x2, starting transfers between devices, on_device(): lax.ppermute(far, 'orb', [(side_a - distance, side_b), (side_b + distance...  8.35 us
    ppermute x6, starting transfers between devices, scatter(): got.append(lax.ppermute(blocks[step], 'orb', pairs))  6.5 us
    ppermute x3, starting transfers between devices, on_device(): lax.ppermute(fit_own, 'aux', swap_pairs(aux_count, distance))  5.69 us
  transfers between devices with their start and end apart: 26, of which 10 were waited for; matrix products, arithmetic and copies ran while one was open for 3% of the time, Pallas kernels for 2%

commit v1 on v0

--- a/solution.py
+++ b/solution.py
@@ -229,6 +229,10 @@
             inputs.append(rows)
         return low, high
 
+    wanted = [(my_slot - side_a) % slots, (side_b - my_slot) % slots]
+    wanted += [(my_slot - plane) % slots for plane in range(slots)]
+    wanted = [[index == step for step in range(slots)] for index in wanted]
+
     near_got, far_got = {0: near}, {}
     for distance in range(half):
         if distance:
@@ -240,7 +244,12 @@
         band_pattern.astype(jnp.bfloat16), ((0, blk - count_rows), (0, blk - slots))
     )[None]
     low, high = stage_rims([("near", 0, near)], pattern)
-    held = (tensor.reshape(tensor.shape[1], -1), metric_inv[0])
+    source, metric_source, *flags = lax.optimization_barrier(
+        [tensor, metric_inv] + [flag for group in wanted for flag in group]
+    )
+    wanted = [flags[index : index + slots] for index in range(0, len(flags), slots)]
+    held = (source.reshape(tensor.shape[1], -1), metric_source[0])
+    held = tuple(pltpu.with_memory_space_constraint(value, pltpu.HBM) for value in held)
     steps = max(count for count in (1, 2, 4, 8) if held[0].shape[0] % (16 * count) == 0)
     held = pl.pallas_call(
         functools.partial(preload_kernel, steps),
@@ -295,16 +304,20 @@
         for step in range(1, slots):
             pairs = [(side_a, (side_a + step) % slots), (side_b, (side_b - step) % slots)]
             got.append(lax.ppermute(blocks[step], "orb", pairs))
+        return got
+
+    def assemble(got):
         picked = []
-        for wanted in ((my_slot - side_a) % slots, (side_b - my_slot) % slots):
+        for flags in wanted[:fields]:
             value = got[0]
             for step in range(1, slots):
-                value = jnp.where(wanted == step, got[step], value)
+                value = jnp.where(flags[step], got[step], value)
             picked.append(value)
         return jnp.stack(picked, 0)
 
-    fit_own = scatter(fit_parts)
-    response = scatter(parts)[:, :, None]
+    fit_own = assemble(scatter(fit_parts))
+    got = scatter(parts)
+    response = assemble(got)[:, :, None]
     fit_own = fit_own + lax.ppermute(fit_own, "aux", swap_pairs(aux_count, 1))
     fit_pieces = [fit_own] + [
         lax.ppermute(fit_own, "aux", swap_pairs(aux_count, distance)) for distance in range(2, aux_count, 2)
@@ -338,7 +351,7 @@
     for plane in range(slots):
         value = got[0]
         for step in range(1, slots):
-            value = jnp.where((my_slot - plane) % slots == step, got[step], value)
+            value = jnp.where(wanted[fields + plane][step], got[step], value)
         coefficients = value if coefficients is None else coefficients + value
     return (response, coefficients[None])
 

time: 113 us -> 107 us (0.947)
  local copies, waits for them, and re-layouts: 9.54 us -> 2.63 us
  Pallas kernels: 7.13 us -> 11.2 us
  waiting for transfers between devices: 35 us -> 31.5 us
    unnamed x11 -> x7, local copies, waits for them, and re-layouts: 9.23 us -> 2.32 us
    ppermute x1, waiting for transfers between devices: 13.4 us -> 8.52 us  [on_device(): lax.ppermute(near, 'orb', [(side_a - distance, side_a), (side_b + distanc...]
    pallas_call x1, Pallas kernels: 1.97 us -> 6.04 us  [on_device(): pl.pallas_call(functools.partial(preload_kernel, steps), out_shape=[jax.S...]
    ppermute x6, waiting for transfers between devices: 9.58 us -> 12.1 us  [scatter(): got.append(lax.ppermute(blocks[step], 'orb', pairs))]
    ppermute x2, starting transfers between devices: 8.35 us -> 6.68 us  [on_device(): lax.ppermute(far, 'orb', [(side_a - distance, side_b), (side_b + distance...]
    ppermute x1, starting transfers between devices: 1.41 us -> 3.07 us  [on_device(): lax.ppermute(near, 'orb', [(side_a - distance, side_a), (side_b + distanc...]
    ppermute x3, starting transfers between devices: 5.69 us -> 6.98 us  [on_device(): lax.ppermute(fit_own, 'aux', swap_pairs(aux_count, distance))]
  transfers between devices with their start and end apart: 26 -> 26, of which waited for: 10 -> 11; matrix products, arithmetic and copies ran while one was open for 3% -> 3% of each run, Pallas kernels for 2% -> 6%
where the time goes in v1:
time: 107 us
  starting transfers between devices  52.8 us (49%)
  waiting for transfers between devices  31.5 us (29%)
  Pallas kernels  11.2 us (10%)
  other arithmetic  6.84 us (6%)
  local copies, waits for them, and re-layouts  2.63 us (2%)
  between operations  1.82 us (2%)
    ppermute x6, waiting for transfers between devices, scatter(): got.append(lax.ppermute(blocks[step], 'orb', pairs))  12.1 us
    ppermute x3, starting transfers between devices, on_device(): lax.ppermute(part, 'orb', [(i, (i + step) % slots) for i in range(slots)])  10 us
    ppermute x1, waiting for transfers between devices, on_device(): lax.ppermute(near, 'orb', [(side_a - distance, side_a), (side_b + distanc...  8.52 us
    ppermute x3, starting transfers between devices, stage_rims(): low = lax.ppermute(jnp.concatenate(low, 0), 'aux', forward)  8.09 us
    ppermute x3, starting transfers between devices, on_device(): lax.ppermute(fit_own, 'aux', swap_pairs(aux_count, distance))  6.98 us
    ppermute x2, starting transfers between devices, on_device(): lax.ppermute(far, 'orb', [(side_a - distance, side_b), (side_b + distance...  6.68 us
    ppermute x6, starting transfers between devices, scatter(): got.append(lax.ppermute(blocks[step], 'orb', pairs))  6.5 us
    pallas_call x1, Pallas kernels, on_device(): pl.pallas_call(functools.partial(preload_kernel, steps), out_shape=[jax.S...  6.04 us
  transfers between devices with their start and end apart: 26, of which 11 were waited for; matrix products, arithmetic and copies ran while one was open for 3% of the time, Pallas kernels for 6%

profile of v1, /device:TPU:0, one launch (start us, length us, event | category | flops | bytes accessed | tf_op | source)
XLA Modules:
  0.0 106.7 jit_solution(6176460765346408153)
XLA Ops:
  0.7 0.7 fusion.20
  1.4 1.2 %bitcast_select_fusion.2 = (bf16[8,128,128]{2,1,0:T(8,128)(2,1)S(1)}, bf16[8,128,128]{2,1,0:T(8,128)(2,1)S(1)}, bf16[8,128,128]{2,1,0:T(8,128)(2,1)S(1)}) fusion(bf16[2,8,1,128,128]{4,3,2,1,0:T(8,128)(2,1)} %param.8, s32[]{:T(128)S(6)} %select_n.219, pred[8]{0:T(512)(128)(4,1)S(1)} %dynamic-slice_bitcast_fusion, s32[]{:T(128)S(6)} %select_n.217, ...), kind=kLoop, calls=%fused_computation.15 | loop fusion | flops 393216 | bytes 1572880 | tf_op jit(solution)/shard_map/jit(_where)/select_n | solution.py:205
  2.6 0.9 pad_maximum_fusion
  3.5 6.0 %collective-permute-start.6 = (bf16[16,128,128]{2,1,0:T(8,128)(2,1)}, bf16[16,128,128]{2,1,0:T(8,128)(2,1)S(1)}, u32[]{:S(2)}, u32[]{:S(2)}) collective-permute-start(bf16[16,128,128]{2,1,0:T(8,128)(2,1)} %get-tuple-element.77), channel_id=1, source_target_pairs={{0,2},{3,1},{4,6},{7,5},{8,10},{11,9},{12,14},{15,13},{16,18},{19,... | collective-permute-start | bytes 1572872 | tf_op jit(solution)/shard_map/ppermute | solution.py:240
  9.5 0.7 collective-permute-start.3
  10.2 0.7 convert_element_type.31
  11.0 0.7 pad_maximum_fusion.6
  11.7 1.3 %collective-permute-start.1 = (bf16[5,128,128]{2,1,0:T(8,128)(2,1)}, bf16[5,128,128]{2,1,0:T(8,128)(2,1)S(1)}, u32[]{:S(2)}, u32[]{:S(2)}) collective-permute-start(bf16[5,128,128]{2,1,0:T(8,128)(2,1)} %pad_maximum_fusion.6), channel_id=1, source_target_pairs={{4,0},{8,4},{12,8},{16,12},{20,16},{24,20},{28,24},{5,1},{9,5},{13... | collective-permute-start | bytes 491528 | tf_op jit(solution)/shard_map/ppermute | solution.py:219
  13.0 3.0 %collective-permute-start = (bf16[9,128,128]{2,1,0:T(8,128)(2,1)S(1)}, bf16[9,128,128]{2,1,0:T(8,128)(2,1)S(1)}, u32[]{:S(2)}, u32[]{:S(2)}) collective-permute-start(bf16[9,128,128]{2,1,0:T(8,128)(2,1)S(1)} %pad_maximum_fusion.3), channel_id=1, source_target_pairs={{0,4},{4,8},{8,12},{12,16},{16,20},{20,24},{24,28},{1,5},{5,9},{9,... | collective-permute-start | bytes 884744 | tf_op jit(solution)/shard_map/ppermute | solution.py:218
  16.1 3.1 %collective-permute-start.2 = (bf16[16,128,128]{2,1,0:T(8,128)(2,1)S(1)}, bf16[16,128,128]{2,1,0:T(8,128)(2,1)S(1)}, u32[]{:S(2)}, u32[]{:S(2)}) collective-permute-start(bf16[16,128,128]{2,1,0:T(8,128)(2,1)S(1)} %get-tuple-element.78.refs_2_), channel_id=1, source_target_pairs={{0,1},{3,2},{4,5},{7,6},{8,9},{11,10},{12,13},{15,14},{16,17},{19,... | collective-permute-start | bytes 1572872 | tf_op jit(solution)/shard_map/ppermute | solution.py:239
  19.9 0.8 copy.20
  20.7 0.8 collective-permute-done.6.refs_9_
  21.6 2.0 %collective-permute-start.7 = (bf16[8,128,128]{2,1,0:T(8,128)(2,1)S(1)}, bf16[8,128,128]{2,1,0:T(8,128)(2,1)S(1)}, u32[]{:S(2)}, u32[]{:S(2)}) collective-permute-start(bf16[8,128,128]{2,1,0:T(8,128)(2,1)S(1)} %pad_maximum_fusion.5), channel_id=1, source_target_pairs={{0,4},{4,8},{8,12},{12,16},{16,20},{20,24},{24,28},{1,5},{5,9},{9,... | collective-permute-start | bytes 786440 | tf_op jit(solution)/shard_map/ppermute | solution.py:218
  23.6 8.5 %collective-permute-done.2.refs_5_ = bf16[16,128,128]{2,1,0:T(8,128)(2,1)S(1)} collective-permute-done((bf16[16,128,128]{2,1,0:T(8,128)(2,1)S(1)}, bf16[16,128,128]{2,1,0:T(8,128)(2,1)S(1)}, u32[]{:S(2)}, u32[]{:S(2)}) %collective-permute-start.2) | collective-permute-done | bytes 524320 | tf_op jit(solution)/shard_map/ppermute | solution.py:239
  32.2 1.3 %collective-permute-start.5 = (bf16[8,128,128]{2,1,0:T(8,128)(2,1)S(1)}, bf16[8,128,128]{2,1,0:T(8,128)(2,1)S(1)}, u32[]{:S(2)}, u32[]{:S(2)}) collective-permute-start(bf16[8,128,128]{2,1,0:T(8,128)(2,1)S(1)} %pad_maximum_fusion.4), channel_id=1, source_target_pairs={{4,0},{8,4},{12,8},{16,12},{20,16},{24,20},{28,24},{5,1},{9,5},{13... | collective-permute-start | bytes 786440 | tf_op jit(solution)/shard_map/ppermute | solution.py:219
  33.6 3.1 %collective-permute-start.4 = (bf16[16,128,128]{2,1,0:T(8,128)(2,1)S(1)}, bf16[16,128,128]{2,1,0:T(8,128)(2,1)S(1)}, u32[]{:S(2)}, u32[]{:S(2)}) collective-permute-start(bf16[16,128,128]{2,1,0:T(8,128)(2,1)S(1)} %pad_maximum_fusion.2), channel_id=1, source_target_pairs={{0,4},{4,8},{8,12},{12,16},{16,20},{20,24},{24,28},{1,5},{5,9},{9,... | collective-permute-start | bytes 1572872 | tf_op jit(solution)/shard_map/ppermute | solution.py:218
  36.7 1.3 %collective-permute-start.8 = (bf16[4,128,128]{2,1,0:T(8,128)(2,1)S(1)}, bf16[4,128,128]{2,1,0:T(8,128)(2,1)S(1)}, u32[]{:S(2)}, u32[]{:S(2)}) collective-permute-start(bf16[4,128,128]{2,1,0:T(8,128)(2,1)S(1)} %pad_maximum_fusion.7), channel_id=1, source_target_pairs={{4,0},{8,4},{12,8},{16,12},{20,16},{24,20},{28,24},{5,1},{9,5},{13... | collective-permute-start | bytes 393224 | tf_op jit(solution)/shard_map/ppermute | solution.py:219
  38.1 2.4 %collective-permute-done.8.refs_8_ = bf16[4,128,128]{2,1,0:T(8,128)(2,1)S(1)} collective-permute-done((bf16[4,128,128]{2,1,0:T(8,128)(2,1)S(1)}, bf16[4,128,128]{2,1,0:T(8,128)(2,1)S(1)}, u32[]{:S(2)}, u32[]{:S(2)}) %collective-permute-start.8) | collective-permute-done | bytes 131104 | tf_op jit(solution)/shard_map/ppermute | solution.py:219
  40.5 0.9 copy-done.1
  41.4 1.0 mid_products.1
  42.5 0.6 copy-done.2
  43.1 0.7 collective-permute-start.14
  43.8 1.3 %collective-permute-start.13 = (bf16[128,128]{1,0:T(8,128)(2,1)S(1)}, bf16[128,128]{1,0:T(8,128)(2,1)S(1)}, u32[]{:S(2)}, u32[]{:S(2)}) collective-permute-start(bf16[128,128]{1,0:T(8,128)(2,1)S(1)} %get-tuple-element.82), channel_id=1, source_target_pairs={{1,3},{2,0},{5,7},{6,4},{9,11},{10,8},{13,15},{14,12},{17,19},{18,... | collective-permute-start | bytes 98312 | tf_op jit(solution)/shard_map/ppermute | solution.py:306
  45.1 1.3 %collective-permute-start.12 = (bf16[128,128]{1,0:T(8,128)(2,1)S(1)}, bf16[128,128]{1,0:T(8,128)(2,1)S(1)}, u32[]{:S(2)}, u32[]{:S(2)}) collective-permute-start(bf16[128,128]{1,0:T(8,128)(2,1)S(1)} %get-tuple-element.83), channel_id=1, source_target_pairs={{1,0},{2,3},{5,4},{6,7},{9,8},{10,11},{13,12},{14,15},{17,16},{18,... | collective-permute-start | bytes 98312 | tf_op jit(solution)/shard_map/ppermute | solution.py:306
  46.5 10.6 %collective-permute-done.13 = bf16[128,128]{1,0:T(8,128)(2,1)S(1)} collective-permute-done((bf16[128,128]{1,0:T(8,128)(2,1)S(1)}, bf16[128,128]{1,0:T(8,128)(2,1)S(1)}, u32[]{:S(2)}, u32[]{:S(2)}) %collective-permute-start.13) | collective-permute-done | bytes 32800 | tf_op jit(solution)/shard_map/ppermute | solution.py:306
  57.1 1.4 %collective-permute-done.12 = bf16[128,128]{1,0:T(8,128)(2,1)S(1)} collective-permute-done((bf16[128,128]{1,0:T(8,128)(2,1)S(1)}, bf16[128,128]{1,0:T(8,128)(2,1)S(1)}, u32[]{:S(2)}, u32[]{:S(2)}) %collective-permute-start.12) | collective-permute-done | bytes 32800 | tf_op jit(solution)/shard_map/ppermute | solution.py:306
  58.6 0.8 fusion.8
  59.4 3.9 %collective-permute-start.15 = (bf16[2,128,128]{2,1,0:T(8,128)(2,1)S(1)}, bf16[2,128,128]{2,1,0:T(8,128)(2,1)S(1)}, u32[]{:S(2)}, u32[]{:S(2)}) collective-permute-start(bf16[2,128,128]{2,1,0:T(8,128)(2,1)S(1)} %pad_maximum_fusion.8), channel_id=1, source_target_pairs={{0,4},{4,0},{8,12},{12,8},{16,20},{20,16},{24,28},{28,24},{1,5},{5... | collective-permute-start | bytes 196616 | tf_op jit(solution)/shard_map/ppermute | solution.py:321
  63.2 0.9 collective-permute-done.15
  64.1 5.4 %collective-permute-start.18 = (bf16[2,128,128]{2,1,0:T(8,128)(2,1)S(1)}, bf16[2,128,128]{2,1,0:T(8,128)(2,1)S(1)}, u32[]{:S(2)}, u32[]{:S(2)}) collective-permute-start(bf16[2,128,128]{2,1,0:T(8,128)(2,1)S(1)} %fusion.23.refs_0_), channel_id=1, source_target_pairs={{0,24},{4,28},{8,16},{12,20},{16,8},{20,12},{24,0},{28,4},{1,25},{... | collective-permute-start | bytes 196616 | tf_op jit(solution)/shard_map/ppermute | solution.py:323
  69.7 1.4 %collective-permute-start.16 = (bf16[2,128,128]{2,1,0:T(8,128)(2,1)S(1)}, bf16[2,128,128]{2,1,0:T(8,128)(2,1)S(1)}, u32[]{:S(2)}, u32[]{:S(2)}) collective-permute-start(bf16[2,128,128]{2,1,0:T(8,128)(2,1)S(1)} %fusion.23.refs_0_), channel_id=1, source_target_pairs={{0,8},{4,12},{8,0},{12,4},{16,24},{20,28},{24,16},{28,20},{1,9},{5... | collective-permute-start | bytes 196616 | tf_op jit(solution)/shard_map/ppermute | solution.py:323
  71.1 6.0 %preload.1 = (bf16[384,16384]{1,0:T(8,128)(2,1)S(1)}, f32[384,3072]{1,0:T(8,128)S(1)}) custom-call(bf16[384,16384]{1,0:T(8,128)(2,1)} %bitcast.88, f32[384,3072]{1,0:T(8,128)} %bitcast.89), custom_call_target="tpu_custom_call" | custom-call | tf_op jit(solution)/shard_map/preload/pallas_call | solution.py:254
  77.2 3.3 %fit_sums.1 = f32[8,2,384]{2,1,0:T(2,128)S(1)} custom-call(s32[1]{0:T(128)} %bitcast.20.place, bf16[2,128,128]{2,1,0:T(8,128)(2,1)S(1)} %fusion.23.refs_0_, bf16[2,128,128]{2,1,0:T(8,128)(2,1)S(1)} %collective-permute-done.16.refs_1_, bf16[2,128,128]{2,1,0:T(8,128)(2,1)S(1)} %collective-permute-done.17.refs_2_, ...), custom_call_target="tpu_custom_call" | custom-call | tf_op jit(solution)/shard_map/fit_sums/pallas_call | solution.py:327
  80.5 1.2 %collective-permute-done.19 = f32[8,2,384]{2,1,0:T(2,128)S(1)} collective-permute-done((f32[8,2,384]{2,1,0:T(2,128)S(1)}, f32[8,2,384]{2,1,0:T(2,128)S(1)}, u32[]{:S(2)}, u32[]{:S(2)}) %collective-permute-start.19) | collective-permute-done | bytes 24608 | tf_op jit(solution)/shard_map/ppermute | solution.py:335
  81.8 2.0 %collective-permute-start.22 = (f32[8,2,384]{2,1,0:T(2,128)S(1)}, f32[8,2,384]{2,1,0:T(2,128)S(1)}, u32[]{:S(2)}, u32[]{:S(2)}) collective-permute-start(f32[8,2,384]{2,1,0:T(2,128)S(1)} %add.117.refs_0_), channel_id=1, source_target_pairs={{0,24},{4,28},{8,16},{12,20},{16,8},{20,12},{24,0},{28,4},{1,25},{... | collective-permute-start | bytes 73736 | tf_op jit(solution)/shard_map/ppermute | solution.py:337
  83.8 0.7 collective-permute-start.11
  84.5 1.3 %collective-permute-start.10 = (bf16[8,128,128]{2,1,0:T(8,128)(2,1)S(1)}, bf16[8,128,128]{2,1,0:T(8,128)(2,1)S(1)}, u32[]{:S(2)}, u32[]{:S(2)}) collective-permute-start(bf16[8,128,128]{2,1,0:T(8,128)(2,1)S(1)} %get-tuple-element.61), channel_id=1, source_target_pairs={{1,3},{2,0},{5,7},{6,4},{9,11},{10,8},{13,15},{14,12},{17,19},{18,... | collective-permute-start | bytes 786440 | tf_op jit(solution)/shard_map/ppermute | solution.py:306
  85.8 1.3 %collective-permute-start.9 = (bf16[8,128,128]{2,1,0:T(8,128)(2,1)S(1)}, bf16[8,128,128]{2,1,0:T(8,128)(2,1)S(1)}, u32[]{:S(2)}, u32[]{:S(2)}) collective-permute-start(bf16[8,128,128]{2,1,0:T(8,128)(2,1)S(1)} %get-tuple-element.62), channel_id=1, source_target_pairs={{1,0},{2,3},{5,4},{6,7},{9,8},{10,11},{13,12},{14,15},{17,16},{18,... | collective-permute-start | bytes 786440 | tf_op jit(solution)/shard_map/ppermute | solution.py:306
  87.4 1.5 %collective-permute-start.20 = (f32[8,2,384]{2,1,0:T(2,128)S(1)}, f32[8,2,384]{2,1,0:T(2,128)S(1)}, u32[]{:S(2)}, u32[]{:S(2)}) collective-permute-start(f32[8,2,384]{2,1,0:T(2,128)S(1)} %add.117.refs_0_), channel_id=1, source_target_pairs={{0,8},{4,12},{8,0},{12,4},{16,24},{20,28},{24,16},{28,20},{1,9},{5... | collective-permute-start | bytes 73736 | tf_op jit(solution)/shard_map/ppermute | solution.py:337
  88.8 2.1 %collective-permute-done.21.refs_2_ = f32[8,2,384]{2,1,0:T(2,128)S(1)} collective-permute-done((f32[8,2,384]{2,1,0:T(2,128)S(1)}, f32[8,2,384]{2,1,0:T(2,128)S(1)}, u32[]{:S(2)}, u32[]{:S(2)}) %collective-permute-start.21) | collective-permute-done | bytes 24608 | tf_op jit(solution)/shard_map/ppermute | solution.py:337
  91.2 0.8 metric.1
  92.0 2.8 %collective-permute-start.25 = (f32[2,384]{1,0:T(2,128)S(1)}, f32[2,384]{1,0:T(2,128)S(1)}, u32[]{:S(2)}, u32[]{:S(2)}) collective-permute-start(f32[2,384]{1,0:T(2,128)S(1)} %metric.1), channel_id=1, source_target_pairs={{0,1},{1,2},{2,3},{3,0},{4,5},{5,6},{6,7},{7,4},{8,9},{9,10},{10,1... | collective-permute-start | bytes 9224 | tf_op jit(solution)/shard_map/ppermute | solution.py:348
  94.7 0.9 collective-permute-start.24
  95.7 1.9 %collective-permute-done.25 = f32[2,384]{1,0:T(2,128)S(1)} collective-permute-done((f32[2,384]{1,0:T(2,128)S(1)}, f32[2,384]{1,0:T(2,128)S(1)}, u32[]{:S(2)}, u32[]{:S(2)}) %collective-permute-start.25) | collective-permute-done | bytes 3104 | tf_op jit(solution)/shard_map/ppermute | solution.py:348
  97.6 6.3 %collective-permute-start.23 = (f32[2,384]{1,0:T(2,128)S(1)}, f32[2,384]{1,0:T(2,128)S(1)}, u32[]{:S(2)}, u32[]{:S(2)}) collective-permute-start(f32[2,384]{1,0:T(2,128)S(1)} %metric.1), channel_id=1, source_target_pairs={{0,3},{1,0},{2,1},{3,2},{4,7},{5,4},{6,5},{7,6},{8,11},{9,8},{10,9... | collective-permute-start | bytes 9224 | tf_op jit(solution)/shard_map/ppermute | solution.py:348
  103.9 1.3 %collective-permute-done.23 = f32[2,384]{1,0:T(2,128)S(1)} collective-permute-done((f32[2,384]{1,0:T(2,128)S(1)}, f32[2,384]{1,0:T(2,128)S(1)}, u32[]{:S(2)}, u32[]{:S(2)}) %collective-permute-start.23) | collective-permute-done | bytes 3104 | tf_op jit(solution)/shard_map/ppermute | solution.py:348
  105.2 0.6 add_bitcast_fusion
  105.9 0.8 maximum_bitcast_fusion
  (53 shorter events, 1.5 us)
Async XLA Ops:
  3.5 18.0 %collective-permute-start.6 = (bf16[16,128,128]{2,1,0:T(8,128)(2,1)}, bf16[16,128,128]{2,1,0:T(8,128)(2,1)S(1)}, u32[]{:S(2)}, u32[]{:S(2)}) collective-permute-start(bf16[16,128,128]{2,1,0:T(8,128)(2,1)} %get-tuple-element.77), channel_id=1, source_target_pairs={{0,2},{3,1},{4,6},{7,5},{8,10},{11,9},{12,14},{15,13},{16,18},{19,... | collective-permute-start | bytes 1572872 | tf_op jit(solution)/shard_map/ppermute | solution.py:240
  9.5 14.1 %collective-permute-start.3 = (bf16[16,128,128]{2,1,0:T(8,128)(2,1)}, bf16[16,128,128]{2,1,0:T(8,128)(2,1)S(1)}, u32[]{:S(2)}, u32[]{:S(2)}) collective-permute-start(bf16[16,128,128]{2,1,0:T(8,128)(2,1)} %get-tuple-element.77), channel_id=1, source_target_pairs={{1,2},{2,1},{5,6},{6,5},{9,10},{10,9},{13,14},{14,13},{17,18},{18,... | collective-permute-start | bytes 1572872 | tf_op jit(solution)/shard_map/ppermute | solution.py:240
  11.7 9.0 %collective-permute-start.1 = (bf16[5,128,128]{2,1,0:T(8,128)(2,1)}, bf16[5,128,128]{2,1,0:T(8,128)(2,1)S(1)}, u32[]{:S(2)}, u32[]{:S(2)}) collective-permute-start(bf16[5,128,128]{2,1,0:T(8,128)(2,1)} %pad_maximum_fusion.6), channel_id=1, source_target_pairs={{4,0},{8,4},{12,8},{16,12},{20,16},{24,20},{28,24},{5,1},{9,5},{13... | collective-permute-start | bytes 491528 | tf_op jit(solution)/shard_map/ppermute | solution.py:219
  13.0 7.7 %collective-permute-start = (bf16[9,128,128]{2,1,0:T(8,128)(2,1)S(1)}, bf16[9,128,128]{2,1,0:T(8,128)(2,1)S(1)}, u32[]{:S(2)}, u32[]{:S(2)}) collective-permute-start(bf16[9,128,128]{2,1,0:T(8,128)(2,1)S(1)} %pad_maximum_fusion.3), channel_id=1, source_target_pairs={{0,4},{4,8},{8,12},{12,16},{16,20},{20,24},{24,28},{1,5},{5,9},{9,... | collective-permute-start | bytes 884744 | tf_op jit(solution)/shard_map/ppermute | solution.py:218
  16.1 16.0 %collective-permute-start.2 = (bf16[16,128,128]{2,1,0:T(8,128)(2,1)S(1)}, bf16[16,128,128]{2,1,0:T(8,128)(2,1)S(1)}, u32[]{:S(2)}, u32[]{:S(2)}) collective-permute-start(bf16[16,128,128]{2,1,0:T(8,128)(2,1)S(1)} %get-tuple-element.78.refs_2_), channel_id=1, source_target_pairs={{0,1},{3,2},{4,5},{7,6},{8,9},{11,10},{12,13},{15,14},{16,17},{19,... | collective-permute-start | bytes 1572872 | tf_op jit(solution)/shard_map/ppermute | solution.py:239
  20.7 19.8 %copy-start = (bf16[5,128,128]{2,1,0:T(8,128)(2,1)}, bf16[5,128,128]{2,1,0:T(8,128)(2,1)S(1)}, u32[]{:S(2)}) copy-start(bf16[5,128,128]{2,1,0:T(8,128)(2,1)S(1)} %collective-permute-done.1.refs_1_) | copy-start | bytes 491524
  21.6 18.9 %collective-permute-start.7 = (bf16[8,128,128]{2,1,0:T(8,128)(2,1)S(1)}, bf16[8,128,128]{2,1,0:T(8,128)(2,1)S(1)}, u32[]{:S(2)}, u32[]{:S(2)}) collective-permute-start(bf16[8,128,128]{2,1,0:T(8,128)(2,1)S(1)} %pad_maximum_fusion.5), channel_id=1, source_target_pairs={{0,4},{4,8},{8,12},{12,16},{16,20},{20,24},{24,28},{1,5},{5,9},{9,... | collective-permute-start | bytes 786440 | tf_op jit(solution)/shard_map/ppermute | solution.py:218
  32.2 8.3 %collective-permute-start.5 = (bf16[8,128,128]{2,1,0:T(8,128)(2,1)S(1)}, bf16[8,128,128]{2,1,0:T(8,128)(2,1)S(1)}, u32[]{:S(2)}, u32[]{:S(2)}) collective-permute-start(bf16[8,128,128]{2,1,0:T(8,128)(2,1)S(1)} %pad_maximum_fusion.4), channel_id=1, source_target_pairs={{4,0},{8,4},{12,8},{16,12},{20,16},{24,20},{28,24},{5,1},{9,5},{13... | collective-permute-start | bytes 786440 | tf_op jit(solution)/shard_map/ppermute | solution.py:219
  33.6 6.9 %collective-permute-start.4 = (bf16[16,128,128]{2,1,0:T(8,128)(2,1)S(1)}, bf16[16,128,128]{2,1,0:T(8,128)(2,1)S(1)}, u32[]{:S(2)}, u32[]{:S(2)}) collective-permute-start(bf16[16,128,128]{2,1,0:T(8,128)(2,1)S(1)} %pad_maximum_fusion.2), channel_id=1, source_target_pairs={{0,4},{4,8},{8,12},{12,16},{16,20},{20,24},{24,28},{1,5},{5,9},{9,... | collective-permute-start | bytes 1572872 | tf_op jit(solution)/shard_map/ppermute | solution.py:218
  36.7 3.8 %collective-permute-start.8 = (bf16[4,128,128]{2,1,0:T(8,128)(2,1)S(1)}, bf16[4,128,128]{2,1,0:T(8,128)(2,1)S(1)}, u32[]{:S(2)}, u32[]{:S(2)}) collective-permute-start(bf16[4,128,128]{2,1,0:T(8,128)(2,1)S(1)} %pad_maximum_fusion.7), channel_id=1, source_target_pairs={{4,0},{8,4},{12,8},{16,12},{20,16},{24,20},{28,24},{5,1},{9,5},{13... | collective-permute-start | bytes 393224 | tf_op jit(solution)/shard_map/ppermute | solution.py:219
  40.5 0.9 copy-start.1
  42.5 0.7 copy-start.2
  43.1 3.4 %collective-permute-start.14 = (bf16[128,128]{1,0:T(8,128)(2,1)S(1)}, bf16[128,128]{1,0:T(8,128)(2,1)S(1)}, u32[]{:S(2)}, u32[]{:S(2)}) collective-permute-start(bf16[128,128]{1,0:T(8,128)(2,1)S(1)} %get-tuple-element.81), channel_id=1, source_target_pairs={{1,2},{2,1},{5,6},{6,5},{9,10},{10,9},{13,14},{14,13},{17,18},{18,... | collective-permute-start | bytes 98312 | tf_op jit(solution)/shard_map/ppermute | solution.py:306
  43.8 13.3 %collective-permute-start.13 = (bf16[128,128]{1,0:T(8,128)(2,1)S(1)}, bf16[128,128]{1,0:T(8,128)(2,1)S(1)}, u32[]{:S(2)}, u32[]{:S(2)}) collective-permute-start(bf16[128,128]{1,0:T(8,128)(2,1)S(1)} %get-tuple-element.82), channel_id=1, source_target_pairs={{1,3},{2,0},{5,7},{6,4},{9,11},{10,8},{13,15},{14,12},{17,19},{18,... | collective-permute-start | bytes 98312 | tf_op jit(solution)/shard_map/ppermute | solution.py:306
  45.1 13.5 %collective-permute-start.12 = (bf16[128,128]{1,0:T(8,128)(2,1)S(1)}, bf16[128,128]{1,0:T(8,128)(2,1)S(1)}, u32[]{:S(2)}, u32[]{:S(2)}) collective-permute-start(bf16[128,128]{1,0:T(8,128)(2,1)S(1)} %get-tuple-element.83), channel_id=1, source_target_pairs={{1,0},{2,3},{5,4},{6,7},{9,8},{10,11},{13,12},{14,15},{17,16},{18,... | collective-permute-start | bytes 98312 | tf_op jit(solution)/shard_map/ppermute | solution.py:306
  59.4 4.8 %collective-permute-start.15 = (bf16[2,128,128]{2,1,0:T(8,128)(2,1)S(1)}, bf16[2,128,128]{2,1,0:T(8,128)(2,1)S(1)}, u32[]{:S(2)}, u32[]{:S(2)}) collective-permute-start(bf16[2,128,128]{2,1,0:T(8,128)(2,1)S(1)} %pad_maximum_fusion.8), channel_id=1, source_target_pairs={{0,4},{4,0},{8,12},{12,8},{16,20},{20,16},{24,28},{28,24},{1,5},{5... | collective-permute-start | bytes 196616 | tf_op jit(solution)/shard_map/ppermute | solution.py:321
  64.1 13.0 %collective-permute-start.18 = (bf16[2,128,128]{2,1,0:T(8,128)(2,1)S(1)}, bf16[2,128,128]{2,1,0:T(8,128)(2,1)S(1)}, u32[]{:S(2)}, u32[]{:S(2)}) collective-permute-start(bf16[2,128,128]{2,1,0:T(8,128)(2,1)S(1)} %fusion.23.refs_0_), channel_id=1, source_target_pairs={{0,24},{4,28},{8,16},{12,20},{16,8},{20,12},{24,0},{28,4},{1,25},{... | collective-permute-start | bytes 196616 | tf_op jit(solution)/shard_map/ppermute | solution.py:323
  69.5 7.7 %collective-permute-start.17 = (bf16[2,128,128]{2,1,0:T(8,128)(2,1)S(1)}, bf16[2,128,128]{2,1,0:T(8,128)(2,1)S(1)}, u32[]{:S(2)}, u32[]{:S(2)}) collective-permute-start(bf16[2,128,128]{2,1,0:T(8,128)(2,1)S(1)} %fusion.23.refs_0_), channel_id=1, source_target_pairs={{0,16},{4,20},{8,24},{12,28},{16,0},{20,4},{24,8},{28,12},{1,17},{... | collective-permute-start | bytes 196616 | tf_op jit(solution)/shard_map/ppermute | solution.py:323
  69.7 7.5 %collective-permute-start.16 = (bf16[2,128,128]{2,1,0:T(8,128)(2,1)S(1)}, bf16[2,128,128]{2,1,0:T(8,128)(2,1)S(1)}, u32[]{:S(2)}, u32[]{:S(2)}) collective-permute-start(bf16[2,128,128]{2,1,0:T(8,128)(2,1)S(1)} %fusion.23.refs_0_), channel_id=1, source_target_pairs={{0,8},{4,12},{8,0},{12,4},{16,24},{20,28},{24,16},{28,20},{1,9},{5... | collective-permute-start | bytes 196616 | tf_op jit(solution)/shard_map/ppermute | solution.py:323
  80.5 1.2 %collective-permute-start.19 = (f32[8,2,384]{2,1,0:T(2,128)S(1)}, f32[8,2,384]{2,1,0:T(2,128)S(1)}, u32[]{:S(2)}, u32[]{:S(2)}) collective-permute-start(f32[8,2,384]{2,1,0:T(2,128)S(1)} %fit_sums.1), channel_id=1, source_target_pairs={{0,4},{4,0},{8,12},{12,8},{16,20},{20,16},{24,28},{28,24},{1,5},{5... | collective-permute-start | bytes 73736 | tf_op jit(solution)/shard_map/ppermute | solution.py:335
  81.8 5.6 %collective-permute-start.22 = (f32[8,2,384]{2,1,0:T(2,128)S(1)}, f32[8,2,384]{2,1,0:T(2,128)S(1)}, u32[]{:S(2)}, u32[]{:S(2)}) collective-permute-start(f32[8,2,384]{2,1,0:T(2,128)S(1)} %add.117.refs_0_), channel_id=1, source_target_pairs={{0,24},{4,28},{8,16},{12,20},{16,8},{20,12},{24,0},{28,4},{1,25},{... | collective-permute-start | bytes 73736 | tf_op jit(solution)/shard_map/ppermute | solution.py:337
  83.8 22.0 %collective-permute-start.11 = (bf16[8,128,128]{2,1,0:T(8,128)(2,1)S(1)}, bf16[8,128,128]{2,1,0:T(8,128)(2,1)S(1)}, u32[]{:S(2)}, u32[]{:S(2)}) collective-permute-start(bf16[8,128,128]{2,1,0:T(8,128)(2,1)S(1)} %get-tuple-element.60), channel_id=1, source_target_pairs={{1,2},{2,1},{5,6},{6,5},{9,10},{10,9},{13,14},{14,13},{17,18},{18,... | collective-permute-start | bytes 786440 | tf_op jit(solution)/shard_map/ppermute | solution.py:306
  84.5 21.3 %collective-permute-start.10 = (bf16[8,128,128]{2,1,0:T(8,128)(2,1)S(1)}, bf16[8,128,128]{2,1,0:T(8,128)(2,1)S(1)}, u32[]{:S(2)}, u32[]{:S(2)}) collective-permute-start(bf16[8,128,128]{2,1,0:T(8,128)(2,1)S(1)} %get-tuple-element.61), channel_id=1, source_target_pairs={{1,3},{2,0},{5,7},{6,4},{9,11},{10,8},{13,15},{14,12},{17,19},{18,... | collective-permute-start | bytes 786440 | tf_op jit(solution)/shard_map/ppermute | solution.py:306
  85.8 20.0 %collective-permute-start.9 = (bf16[8,128,128]{2,1,0:T(8,128)(2,1)S(1)}, bf16[8,128,128]{2,1,0:T(8,128)(2,1)S(1)}, u32[]{:S(2)}, u32[]{:S(2)}) collective-permute-start(bf16[8,128,128]{2,1,0:T(8,128)(2,1)S(1)} %get-tuple-element.62), channel_id=1, source_target_pairs={{1,0},{2,3},{5,4},{6,7},{9,8},{10,11},{13,12},{14,15},{17,16},{18,... | collective-permute-start | bytes 786440 | tf_op jit(solution)/shard_map/ppermute | solution.py:306
  87.1 3.9 %collective-permute-start.21 = (f32[8,2,384]{2,1,0:T(2,128)S(1)}, f32[8,2,384]{2,1,0:T(2,128)S(1)}, u32[]{:S(2)}, u32[]{:S(2)}) collective-permute-start(f32[8,2,384]{2,1,0:T(2,128)S(1)} %add.117.refs_0_), channel_id=1, source_target_pairs={{0,16},{4,20},{8,24},{12,28},{16,0},{20,4},{24,8},{28,12},{1,17},{... | collective-permute-start | bytes 73736 | tf_op jit(solution)/shard_map/ppermute | solution.py:337
  87.4 3.8 %collective-permute-start.20 = (f32[8,2,384]{2,1,0:T(2,128)S(1)}, f32[8,2,384]{2,1,0:T(2,128)S(1)}, u32[]{:S(2)}, u32[]{:S(2)}) collective-permute-start(f32[8,2,384]{2,1,0:T(2,128)S(1)} %add.117.refs_0_), channel_id=1, source_target_pairs={{0,8},{4,12},{8,0},{12,4},{16,24},{20,28},{24,16},{28,20},{1,9},{5... | collective-permute-start | bytes 73736 | tf_op jit(solution)/shard_map/ppermute | solution.py:337
  92.0 5.6 %collective-permute-start.25 = (f32[2,384]{1,0:T(2,128)S(1)}, f32[2,384]{1,0:T(2,128)S(1)}, u32[]{:S(2)}, u32[]{:S(2)}) collective-permute-start(f32[2,384]{1,0:T(2,128)S(1)} %metric.1), channel_id=1, source_target_pairs={{0,1},{1,2},{2,3},{3,0},{4,5},{5,6},{6,7},{7,4},{8,9},{9,10},{10,1... | collective-permute-start | bytes 9224 | tf_op jit(solution)/shard_map/ppermute | solution.py:348
  94.7 9.2 %collective-permute-start.24 = (f32[2,384]{1,0:T(2,128)S(1)}, f32[2,384]{1,0:T(2,128)S(1)}, u32[]{:S(2)}, u32[]{:S(2)}) collective-permute-start(f32[2,384]{1,0:T(2,128)S(1)} %metric.1), channel_id=1, source_target_pairs={{0,2},{1,3},{2,0},{3,1},{4,6},{5,7},{6,4},{7,5},{8,10},{9,11},{10,... | collective-permute-start | bytes 9224 | tf_op jit(solution)/shard_map/ppermute | solution.py:348
  97.6 7.7 %collective-permute-start.23 = (f32[2,384]{1,0:T(2,128)S(1)}, f32[2,384]{1,0:T(2,128)S(1)}, u32[]{:S(2)}, u32[]{:S(2)}) collective-permute-start(f32[2,384]{1,0:T(2,128)S(1)} %metric.1), channel_id=1, source_target_pairs={{0,3},{1,0},{2,1},{3,2},{4,7},{5,4},{6,5},{7,6},{8,11},{9,8},{10,9... | collective-permute-start | bytes 9224 | tf_op jit(solution)/shard_map/ppermute | solution.py:348

commit v2 on v1

--- a/solution.py
+++ b/solution.py
@@ -42,63 +42,77 @@
     lax.fori_loop(0, trips, body, 0)
 
 
-def mid_kernel(slots, count_rows, group, plan, scal, keep, *refs):
+def cols(slot, width, blk):
+    return pl.ds(slot * blk, width * blk)
+
+
+def wide(ref, row, low, high, head, tail):
+    blk = ref.shape[1]
+    parts = [ref[row, :, cols(low, high - low, blk)]]
+    if head:
+        parts.insert(0, jnp.zeros((blk, head * blk), jnp.bfloat16))
+    if tail:
+        parts.append(jnp.zeros((blk, tail * blk), jnp.bfloat16))
+    return parts[0] if len(parts) == 1 else jnp.concatenate(parts, 1)
+
+
+def add_products(slots, total, lefts, left_row, right, right_row):
+    half, blk = slots // 2, right.shape[1]
+    for first in range(0, slots, 2):
+        rows, spans = [], []
+        for t in (first, first + 1):
+            low, high = max(0, t - half), min(slots - 1, slots - 1 + t - half)
+            spans.append((t, low, high))
+        start, stop = min(v[1] for v in spans), max(v[2] for v in spans)
+        for t, low, high in spans:
+            u = low - t + half
+            rows.append(
+                wide(right, right_row + t, u, u + high - low + 1, low - start, stop - high)
+            )
+        lhs = [left[left_row, :, cols(first, 2, blk)] for _, left in lefts]
+        lhs = lhs[0] if len(lhs) == 1 else jnp.concatenate(lhs, 0)
+        value = jnp.dot(lhs, jnp.concatenate(rows, 0), preferred_element_type=jnp.float32)
+        for index, (key, _) in enumerate(lefts):
+            for s in range(start, stop + 1):
+                part = value[index * blk : (index + 1) * blk, (s - start) * blk : (s - start + 1) * blk]
+                total[key, s] = total[key, s] + part if (key, s) in total else part
+
+
+def response_row(slots, keep, square, order, i, write):
+    half, blk = slots // 2, square.shape[1]
+    j = i + half
+    total = {}
+    add_products(slots, total, [("second", square)], j, order, i)
+    add_products(slots, total, [("second", order)], j, square, i)
+    for s in range(slots):
+        twice = 2.0 * order[j, :, cols(s, 1, blk)].astype(jnp.float32)
+        write(s, jnp.where(keep[j, s] != 0, twice - total["second", s], 0.0).astype(jnp.bfloat16))
+
+
+def place_of(slots, is_a, slot):
+    half = slots // 2
+    return jnp.where(is_a != 0, (slot - (half - 1)) % slots, (half - slot) % slots)
+
+
+def first_kernel(slots, count_rows, group, plan, scal, keep, *refs):
     half = slots // 2
     blk = refs[0].shape[-1]
     ins, rest = refs[: plan["inputs"]], refs[plan["inputs"] :]
-    outs, fits, dens, pert, square, order, sems = rest
-    mid_rows = count_rows + 2 * half - 1
+    square, order, fits, dens, pert, sems = rest
     middle, is_a, fit_row, owner = scal[0], scal[1], scal[2], scal[3]
-
-    def cols(slot, width=1):
-        return pl.ds(slot * blk, width * blk)
-
-    def wide(ref, row, low, high, head, tail):
-        parts = [ref[row, :, cols(low, high - low)]]
-        if head:
-            parts.insert(0, jnp.zeros((blk, head * blk), jnp.bfloat16))
-        if tail:
-            parts.append(jnp.zeros((blk, tail * blk), jnp.bfloat16))
-        return parts[0] if len(parts) == 1 else jnp.concatenate(parts, 1)
-
-    def add_products(total, lefts, left_row, right, right_row):
-        for first in range(0, slots, 2):
-            rows, spans = [], []
-            for t in (first, first + 1):
-                low, high = max(0, t - half), min(slots - 1, slots - 1 + t - half)
-                spans.append((t, low, high))
-            start, stop = min(v[1] for v in spans), max(v[2] for v in spans)
-            for t, low, high in spans:
-                u = low - t + half
-                rows.append(
-                    wide(right, right_row + t, u, u + high - low + 1, low - start, stop - high)
-                )
-            lhs = [left[left_row, :, cols(first, 2)] for _, left in lefts]
-            lhs = lhs[0] if len(lhs) == 1 else jnp.concatenate(lhs, 0)
-            value = jnp.dot(lhs, jnp.concatenate(rows, 0), preferred_element_type=jnp.float32)
-            for index, (key, _) in enumerate(lefts):
-                for s in range(start, stop + 1):
-                    part = value[index * blk : (index + 1) * blk, (s - start) * blk : (s - start + 1) * blk]
-                    total[key, s] = total[key, s] + part if (key, s) in total else part
 
     def first_step(j):
         total = {}
-        add_products(total, [("square", dens), ("order", pert)], j + half, dens, j)
-        add_products(total, [("order", dens)], j + half, pert, j)
+        add_products(slots, total, [("square", dens), ("order", pert)], j + half, dens, j)
+        add_products(slots, total, [("order", dens)], j + half, pert, j)
         for s in range(slots):
             kept = keep[j, s] != 0
-            square[j, :, cols(s)] = jnp.where(kept, total["square", s], 0.0).astype(jnp.bfloat16)
-            order[j, :, cols(s)] = jnp.where(kept, total["order", s], 0.0).astype(jnp.bfloat16)
-
-    def second_step(i):
-        j = i + half
-        total = {}
-        add_products(total, [("second", square)], j, order, i)
-        add_products(total, [("second", order)], j, square, i)
-        for s in range(slots):
-            twice = 2.0 * order[j, :, cols(s)].astype(jnp.float32)
-            value = jnp.where(keep[j, s] != 0, twice - total["second", s], 0.0).astype(jnp.bfloat16)
-            outs[jnp.where(is_a != 0, (s - (half - 1)) % slots, (half - s) % slots), i] = value
+            square[j, :, cols(s, 1, blk)] = jnp.where(kept, total["square", s], 0.0).astype(jnp.bfloat16)
+            order[j, :, cols(s, 1, blk)] = jnp.where(kept, total["order", s], 0.0).astype(jnp.bfloat16)
+
+    def write(s, value):
+        value = jnp.where(owner != 0, value, jnp.zeros_like(value))
+        fits[place_of(slots, is_a, s)] = value
 
     @pl.when(middle != 0)
     def _():
@@ -118,43 +132,91 @@
             copy.start()
         for copy in copies:
             copy.wait()
-        in_groups(mid_rows, group, first_step)
-        in_groups(count_rows, group, second_step)
-        for step in range(slots):
-            value = outs[step, fit_row].astype(jnp.float32)
-            fits[step] = jnp.where(owner != 0, value, 0.0).astype(jnp.bfloat16)
-
-    @pl.when(middle == 0)
+        in_groups(count_rows + 2 * half - 1, group, first_step)
+        response_row(slots, keep, square, order, fit_row, write)
+
+
+def second_kernel(slots, group, scal, keep, square, order, outs):
+    def step(i):
+        def write(s, value):
+            outs[place_of(slots, scal[1], s), i] = value
+
+        response_row(slots, keep, square, order, i, write)
+
+    @pl.when(scal[0] != 0)
     def _():
-        outs[...] = jnp.zeros_like(outs)
-        fits[...] = jnp.zeros_like(fits)
-
-
-def preload_kernel(steps, *refs):
-    count = len(refs) // 2
-    sources, targets, sems = refs[:count], refs[count : 2 * count], refs[2 * count]
-    copies = []
-    for source, target in zip(sources, targets):
-        height = source.shape[0] // steps
-        for step in range(steps):
-            rows = pl.ds(step * height, height)
-            copies.append(pltpu.make_async_copy(source.at[rows], target.at[rows], sems.at[len(copies)]))
+        in_groups(outs.shape[1], group, step)
+
+
+def pack_kernel(pattern, density_in, field_terms, near, far, flags, sems):
+    slots, rows = pattern.shape
+    half = slots // 2
+    my_slot = lax.axis_index("orb")
+    first_row = lax.axis_index("aux") * rows
+    near_field = jnp.where(my_slot < half, 0, 1)
+    copies = [
+        pltpu.make_async_copy(pattern, flags, sems.at[0]),
+        pltpu.make_async_copy(density_in.at[:, 0], near.at[pl.ds(0, rows)], sems.at[1]),
+        pltpu.make_async_copy(density_in.at[:, 0], far.at[pl.ds(0, rows)], sems.at[2]),
+        pltpu.make_async_copy(field_terms.at[near_field, :, 0], near.at[pl.ds(rows, rows)], sems.at[3]),
+        pltpu.make_async_copy(field_terms.at[1 - near_field, :, 0], far.at[pl.ds(rows, rows)], sems.at[4]),
+    ]
     for copy in copies:
         copy.start()
     for copy in copies:
         copy.wait()
-
-
-def sums_kernel(place, *refs):
-    pieces, (tensor, out) = refs[:-2], refs[-2:]
+    total_rows = lax.axis_size("aux") * rows
+    for row in range(rows):
+        column = first_row + row + my_slot - half
+        kept = (flags[my_slot, row] == 1) & (column >= 0) & (column < total_rows)
+
+        @pl.when(jnp.logical_not(kept))
+        def _(row=row):
+            for piece in (near, far):
+                for place in (row, rows + row):
+                    piece[place] = jnp.zeros_like(piece[place])
+
+
+def preload_kernel(parts, *refs):
+    refs, sems = refs[:-1], refs[-1]
+    copies = []
+    for source, row, rows, column, columns, target, target_row in parts:
+        copies.append(
+            pltpu.make_async_copy(
+                refs[source].at[pl.ds(row, rows), pl.ds(column, columns)],
+                refs[target].at[pl.ds(target_row, rows)],
+                sems.at[len(copies)],
+            )
+        )
+    for copy in copies:
+        copy.start()
+    for copy in copies:
+        copy.wait()
+
+
+def sums_kernel(pieces, place, *refs):
+    pieces, integrals, out = refs[:pieces], refs[pieces:-1], refs[-1]
     pairs = pieces[0][...]
     for piece in pieces[1:]:
         pairs = pairs + piece[...]
     out[...] = jnp.zeros_like(out)
-    flat = pairs.reshape(pairs.shape[0], -1)
-    out[place[0]] = lax.dot_general(
-        flat, tensor[...], (((1,), (1,)), ((), ())), preferred_element_type=jnp.float32
-    )
+    fields = pairs.shape[0]
+    flat = pairs.reshape(fields, -1)
+    start = 0
+    for part in integrals:
+        width = part.shape[1]
+        folds = flat.shape[1] // width
+        rows = part.shape[0] // folds
+        lhs = [flat[:, fold * width : (fold + 1) * width] for fold in range(folds)]
+        lhs = lhs[0] if folds == 1 else jnp.concatenate(lhs, 0)
+        value = lax.dot_general(
+            lhs, part[...], (((1,), (1,)), ((), ())), preferred_element_type=jnp.float32
+        )
+        total = value[:fields, :rows]
+        for fold in range(1, folds):
+            total = total + value[fold * fields : (fold + 1) * fields, fold * rows : (fold + 1) * rows]
+        out[place[0], :, start : start + rows] = total
+        start += rows
 
 
 def metric_kernel(*refs):
@@ -196,16 +258,20 @@
     forward = [(i, i + 1) for i in range(aux_count - 1)]
     backward = [(i + 1, i) for i in range(aux_count - 1)]
 
-    keep_rows = band_keep(band_pattern, first_row, total_rows)
-    keep_own = lax.dynamic_index_in_dim(keep_rows, my_slot, 1, keepdims=False)[:, None, None]
-    density = jnp.where(keep_own, density_in[:, 0], zero_half)
-
-    def with_field(index):
-        picked = lax.dynamic_index_in_dim(field_terms, index, 0, keepdims=False)[:, 0]
-        return jnp.concatenate([density, jnp.where(keep_own, picked, zero_half)], 0)
-
-    near = with_field(jnp.where(is_a, 0, 1))
-    far = with_field(jnp.where(is_a, 1, 0))
+    near, far = pl.pallas_call(
+        pack_kernel,
+        out_shape=[jax.ShapeDtypeStruct((2 * count_rows, blk, blk), jnp.bfloat16)] * 2,
+        in_specs=[pl.BlockSpec(memory_space=pltpu.HBM)] * 3,
+        out_specs=[VMEM] * 2,
+        scratch_shapes=[pltpu.SMEM((slots, count_rows), jnp.int32), pltpu.SemaphoreType.DMA((5,))],
+        compiler_params=pltpu.CompilerParams(vmem_limit_bytes=4 << 20),
+        name="pack",
+    )(
+        *(
+            pltpu.with_memory_space_constraint(value, pltpu.HBM)
+            for value in (band_pattern.T, density_in, field_terms)
+        ),
+    )
 
     inputs, moves = [], []
 
@@ -248,19 +314,52 @@
         [tensor, metric_inv] + [flag for group in wanted for flag in group]
     )
     wanted = [flags[index : index + slots] for index in range(0, len(flags), slots)]
-    held = (source.reshape(tensor.shape[1], -1), metric_source[0])
-    held = tuple(pltpu.with_memory_space_constraint(value, pltpu.HBM) for value in held)
-    steps = max(count for count in (1, 2, 4, 8) if held[0].shape[0] % (16 * count) == 0)
-    held = pl.pallas_call(
-        functools.partial(preload_kernel, steps),
-        out_shape=[jax.ShapeDtypeStruct(value.shape, value.dtype) for value in held],
-        in_specs=[pl.BlockSpec(memory_space=pltpu.HBM)] * 2,
-        out_specs=[VMEM] * 2,
-        scratch_shapes=[pltpu.SemaphoreType.DMA((2 * steps,))],
-        compiler_params=pltpu.CompilerParams(vmem_limit_bytes=4 << 20),
-        name="preload",
-    )(*held)
-    integrals, metric = (pltpu.with_memory_space_constraint(value, pltpu.VMEM) for value in held)
+    source, metric_source = (
+        pltpu.with_memory_space_constraint(value, pltpu.HBM)
+        for value in (source.reshape(tensor.shape[1], -1), metric_source[0])
+    )
+    aux_rows, length = source.shape
+    whole_rows = aux_rows // 256 * 256
+    rest_rows = aux_rows - whole_rows
+    folds = 2 if rest_rows <= 128 else 1
+
+    def preload(sources, shapes, parts):
+        held = pl.pallas_call(
+            functools.partial(preload_kernel, parts),
+            out_shape=shapes,
+            in_specs=[pl.BlockSpec(memory_space=pltpu.HBM)] * len(sources),
+            out_specs=[VMEM] * len(shapes),
+            scratch_shapes=[pltpu.SemaphoreType.DMA((len(parts),))],
+            compiler_params=pltpu.CompilerParams(vmem_limit_bytes=4 << 20),
+        )(*sources)
+        return [pltpu.with_memory_space_constraint(value, pltpu.VMEM) for value in held]
+
+    def strips(index, start, rows, column, columns, target, target_row):
+        count = max(count for count in (1, 2, 4, 8) if rows % (16 * count) == 0)
+        height = rows // count
+        return [
+            (index, start + strip * height, height, column, columns, target, target_row + strip * height)
+            for strip in range(count)
+        ]
+
+    integrals = []
+    if whole_rows:
+        integrals += preload(
+            [source],
+            [jax.ShapeDtypeStruct((whole_rows, length), source.dtype)],
+            strips(0, 0, whole_rows, 0, length, 1, 0),
+        )
+    (metric,) = preload(
+        [metric_source],
+        [jax.ShapeDtypeStruct(metric_source.shape, metric_source.dtype)],
+        strips(0, 0, metric_source.shape[0], 0, metric_source.shape[1], 1, 0),
+    )
+    if rest_rows:
+        width = length // folds
+        parts = []
+        for fold in range(folds):
+            parts += strips(0, whole_rows, rest_rows, fold * width, width, 1, fold * rest_rows)
+        integrals += preload([source], [jax.ShapeDtypeStruct((folds * rest_rows, width), source.dtype)], parts)
     pattern_low = low[-1, count_rows - half : count_rows, :slots].astype(jnp.int32)
     pattern_high = high[-1, : half - 1, :slots].astype(jnp.int32)
     for distance in range(1, half):
@@ -278,26 +377,28 @@
     wide_rows = count_rows + up_rows + down_rows
     mid_rows = count_rows + 2 * half - 1
     plan = {"inputs": len(inputs), "moves": tuple(moves)}
-    out_shape = [
-        jax.ShapeDtypeStruct((slots, count_rows, blk, blk), jnp.bfloat16),
-        jax.ShapeDtypeStruct((slots, blk, blk), jnp.bfloat16),
-    ]
-    blocks = 2 * (wide_rows + mid_rows) * slots + 2 * slots * (count_rows + 1)
-    parts, fit_parts = pl.pallas_call(
-        functools.partial(mid_kernel, slots, count_rows, 4 if slots <= 4 else 1, plan),
-        out_shape=out_shape,
+    group = 4 if slots <= 4 else 1
+    bands = jax.ShapeDtypeStruct((mid_rows, blk, slots * blk), jnp.bfloat16)
+    wide_band = pltpu.VMEM((wide_rows, blk, slots * blk), jnp.bfloat16)
+    blocks = 2 * wide_rows * slots
+    square, order, fit_parts = pl.pallas_call(
+        functools.partial(first_kernel, slots, count_rows, group, plan),
+        out_shape=[bands, bands, jax.ShapeDtypeStruct((slots, blk, blk), jnp.bfloat16)],
         in_specs=[SMEM, SMEM] + [ANY] * len(inputs),
-        out_specs=[VMEM] * 2,
-        scratch_shapes=[
-            pltpu.VMEM((wide_rows, blk, slots * blk), jnp.bfloat16),
-            pltpu.VMEM((wide_rows, blk, slots * blk), jnp.bfloat16),
-            pltpu.VMEM((mid_rows, blk, slots * blk), jnp.bfloat16),
-            pltpu.VMEM((mid_rows, blk, slots * blk), jnp.bfloat16),
-            pltpu.SemaphoreType.DMA((len(moves),)),
-        ],
+        out_specs=[VMEM] * 3,
+        scratch_shapes=[wide_band, wide_band, pltpu.SemaphoreType.DMA((len(moves),))],
         compiler_params=pltpu.CompilerParams(vmem_limit_bytes=blocks * blk * blk * 2 + (4 << 20)),
         name="mid_products",
     )(scal, keep_wide, *inputs)
+    square, order = (pltpu.with_memory_space_constraint(value, pltpu.VMEM) for value in (square, order))
+    parts = pl.pallas_call(
+        functools.partial(second_kernel, slots, group),
+        out_shape=jax.ShapeDtypeStruct((slots, count_rows, blk, blk), jnp.bfloat16),
+        in_specs=[SMEM, SMEM, VMEM, VMEM],
+        out_specs=VMEM,
+        compiler_params=pltpu.CompilerParams(vmem_limit_bytes=4 << 20),
+        name="mid_second",
+    )(scal, keep_wide, square, order)
 
     def scatter(blocks):
         got = [blocks[0]]
@@ -323,15 +424,14 @@
         lax.ppermute(fit_own, "aux", swap_pairs(aux_count, distance)) for distance in range(2, aux_count, 2)
     ]
 
-    aux_rows = integrals.shape[0]
     sums = pl.pallas_call(
-        sums_kernel,
+        functools.partial(sums_kernel, len(fit_pieces)),
         out_shape=jax.ShapeDtypeStruct((aux_count, fields, aux_rows), jnp.float32),
-        in_specs=[SMEM] + [VMEM] * (len(fit_pieces) + 1),
+        in_specs=[SMEM] + [VMEM] * (len(fit_pieces) + len(integrals)),
         out_specs=VMEM,
         compiler_params=pltpu.CompilerParams(vmem_limit_bytes=8 << 20),
         name="fit_sums",
-    )(my_aux.astype(jnp.int32)[None], *fit_pieces, integrals)
+    )(my_aux.astype(jnp.int32)[None], *fit_pieces, *integrals)
     sums = sums + lax.ppermute(sums, "aux", swap_pairs(aux_count, 1))
     pieces = [sums] + [
         lax.ppermute(sums, "aux", swap_pairs(aux_count, distance)) for distance in range(2, aux_count, 2)

time: 107 us -> 110 us (1.028)
  Pallas kernels: 11.2 us -> 15.2 us
  other arithmetic: 6.84 us -> 3.94 us
  local copies, waits for them, and re-layouts: 2.63 us -> 4.75 us
    ppermute x1, waiting for transfers between devices: 8.52 us -> 13.2 us  [on_device(): lax.ppermute(near, 'orb', [(side_a - distance, side_a), (side_b + distanc...]
    pallas_call x3 -> x7, Pallas kernels: 10.4 us -> 14.4 us  [the longest x3 8.13 us: preload(): pl.pallas_call(functools.partial(preload_kernel, parts), out_shape=shapes...]
    ppermute x6, waiting for transfers between devices: 12.1 us -> 8.49 us  [scatter(): got.append(lax.ppermute(blocks[step], 'orb', pairs))]
    unnamed x7 -> x17, local copies, waits for them, and re-layouts: 2.32 us -> 4.46 us
    ppermute x1, starting transfers between devices: 3.07 us -> 1.36 us  [on_device(): lax.ppermute(near, 'orb', [(side_a - distance, side_a), (side_b + distanc...]
    ppermute x2, starting transfers between devices: 6.68 us -> 8.39 us  [on_device(): lax.ppermute(far, 'orb', [(side_a - distance, side_b), (side_b + distance...]
    ppermute x3, waiting for transfers between devices: 2.36 us -> 1.03 us  [on_device(): lax.ppermute(sums, 'aux', swap_pairs(aux_count, distance))]
    ppermute x3, starting transfers between devices: 6.98 us -> 5.67 us  [on_device(): lax.ppermute(fit_own, 'aux', swap_pairs(aux_count, distance))]
  transfers between devices with their start and end apart: 26 -> 26, of which waited for: 11 -> 9; matrix products, arithmetic and copies ran while one was open for 3% -> 3% of each run, Pallas kernels for 6% -> 9%
where the time goes in v2:
time: 110 us; the launch traced here: 109 us
  starting transfers between devices  53 us (48%)
  waiting for transfers between devices  30.8 us (28%)
  Pallas kernels  15.2 us (14%)
  local copies, waits for them, and re-layouts  4.75 us (4%)
  other arithmetic  3.94 us (4%)
  between operations  1.87 us (2%)
    ppermute x1, waiting for transfers between devices, on_device(): lax.ppermute(near, 'orb', [(side_a - distance, side_a), (side_b + distanc...  13.2 us
    ppermute x3, starting transfers between devices, on_device(): lax.ppermute(part, 'orb', [(i, (i + step) % slots) for i in range(slots)])  10.2 us
    ppermute x3, starting transfers between devices, stage_rims(): low = lax.ppermute(jnp.concatenate(low, 0), 'aux', forward)  9.1 us
    ppermute x6, waiting for transfers between devices, scatter(): got.append(lax.ppermute(blocks[step], 'orb', pairs))  8.49 us
    ppermute x2, starting transfers between devices, on_device(): lax.ppermute(far, 'orb', [(side_a - distance, side_b), (side_b + distance...  8.39 us
    pallas_call x3, Pallas kernels, preload(): pl.pallas_call(functools.partial(preload_kernel, parts), out_shape=shapes...  8.13 us
    ppermute x6, starting transfers between devices, scatter(): got.append(lax.ppermute(blocks[step], 'orb', pairs))  6.5 us
    ppermute x3, starting transfers between devices, on_device(): lax.ppermute(fit_own, 'aux', swap_pairs(aux_count, distance))  5.67 us
  transfers between devices with their start and end apart: 26, of which 9 were waited for; matrix products, arithmetic and copies ran while one was open for 3% of the time, Pallas kernels for 9%

profile of v2, /device:TPU:0, one launch (start us, length us, event | category | flops | bytes accessed | tf_op | source)
XLA Modules:
  0.0 109.5 jit_solution(14020449679243190231)
XLA Ops:
  0.6 1.4 %pack.1 = (bf16[16,128,128]{2,1,0:T(8,128)(2,1)S(1)}, bf16[16,128,128]{2,1,0:T(8,128)(2,1)S(1)}) custom-call(s32[4,8]{1,0:T(4,128)} %bitcast.75, bf16[8,1,128,128]{3,2,1,0:T(8,128)(2,1)} %density_in.1, bf16[2,8,1,128,128]{4,3,2,1,0:T(8,128)(2,1)} %field_terms.1), custom_call_target="tpu_custom_call" | custom-call | tf_op jit(solution)/shard_map/pack/pallas_call | solution.py:261
  2.0 0.7 collective-permute-start.3
  2.7 7.7 %collective-permute-start.6 = (bf16[16,128,128]{2,1,0:T(8,128)(2,1)S(1)}, bf16[16,128,128]{2,1,0:T(8,128)(2,1)S(1)}, u32[]{:S(2)}, u32[]{:S(2)}) collective-permute-start(bf16[16,128,128]{2,1,0:T(8,128)(2,1)S(1)} %get-tuple-element.29), channel_id=1, source_target_pairs={{0,2},{3,1},{4,6},{7,5},{8,10},{11,9},{12,14},{15,13},{16,18},{19,... | collective-permute-start | bytes 1572872 | tf_op jit(solution)/shard_map/ppermute | solution.py:306
  10.4 1.4 %collective-permute-start.2 = (bf16[16,128,128]{2,1,0:T(8,128)(2,1)S(1)}, bf16[16,128,128]{2,1,0:T(8,128)(2,1)S(1)}, u32[]{:S(2)}, u32[]{:S(2)}) collective-permute-start(bf16[16,128,128]{2,1,0:T(8,128)(2,1)S(1)} %get-tuple-element.28.refs_2_), channel_id=1, source_target_pairs={{0,1},{3,2},{4,5},{7,6},{8,9},{11,10},{12,13},{15,14},{16,17},{19,... | collective-permute-start | bytes 1572872 | tf_op jit(solution)/shard_map/ppermute | solution.py:305
  11.8 0.7 convert_element_type.31
  12.6 1.3 %collective-permute-start.1 = (bf16[5,128,128]{2,1,0:T(8,128)(2,1)S(1)}, bf16[5,128,128]{2,1,0:T(8,128)(2,1)S(1)}, u32[]{:S(2)}, u32[]{:S(2)}) collective-permute-start(bf16[5,128,128]{2,1,0:T(8,128)(2,1)S(1)} %pad_maximum_fusion.4), channel_id=1, source_target_pairs={{4,0},{8,4},{12,8},{16,12},{20,16},{24,20},{28,24},{5,1},{9,5},{13... | collective-permute-start | bytes 491528 | tf_op jit(solution)/shard_map/ppermute | solution.py:285
  14.0 3.0 %collective-permute-start = (bf16[9,128,128]{2,1,0:T(8,128)(2,1)S(1)}, bf16[9,128,128]{2,1,0:T(8,128)(2,1)S(1)}, u32[]{:S(2)}, u32[]{:S(2)}) collective-permute-start(bf16[9,128,128]{2,1,0:T(8,128)(2,1)S(1)} %pad_maximum_fusion.1), channel_id=1, source_target_pairs={{0,4},{4,8},{8,12},{12,16},{16,20},{20,24},{24,28},{1,5},{5,9},{9,... | collective-permute-start | bytes 884744 | tf_op jit(solution)/shard_map/ppermute | solution.py:284
  18.3 0.8 copy.20
  19.2 13.2 %collective-permute-done.2.refs_5_ = bf16[16,128,128]{2,1,0:T(8,128)(2,1)S(1)} collective-permute-done((bf16[16,128,128]{2,1,0:T(8,128)(2,1)S(1)}, bf16[16,128,128]{2,1,0:T(8,128)(2,1)S(1)}, u32[]{:S(2)}, u32[]{:S(2)}) %collective-permute-start.2) | collective-permute-done | bytes 524320 | tf_op jit(solution)/shard_map/ppermute | solution.py:305
  32.5 1.3 %collective-permute-start.4 = (bf16[16,128,128]{2,1,0:T(8,128)(2,1)S(1)}, bf16[16,128,128]{2,1,0:T(8,128)(2,1)S(1)}, u32[]{:S(2)}, u32[]{:S(2)}) collective-permute-start(bf16[16,128,128]{2,1,0:T(8,128)(2,1)S(1)} %pad_maximum_fusion), channel_id=1, source_target_pairs={{0,4},{4,8},{8,12},{12,16},{16,20},{20,24},{24,28},{1,5},{5,9},{9,... | collective-permute-start | bytes 1572872 | tf_op jit(solution)/shard_map/ppermute | solution.py:284
  34.0 1.3 %collective-permute-start.5 = (bf16[8,128,128]{2,1,0:T(8,128)(2,1)S(1)}, bf16[8,128,128]{2,1,0:T(8,128)(2,1)S(1)}, u32[]{:S(2)}, u32[]{:S(2)}) collective-permute-start(bf16[8,128,128]{2,1,0:T(8,128)(2,1)S(1)} %pad_maximum_fusion.2), channel_id=1, source_target_pairs={{4,0},{8,4},{12,8},{16,12},{20,16},{24,20},{28,24},{5,1},{9,5},{13... | collective-permute-start | bytes 786440 | tf_op jit(solution)/shard_map/ppermute | solution.py:285
  35.3 4.7 %collective-permute-start.7 = (bf16[8,128,128]{2,1,0:T(8,128)(2,1)S(1)}, bf16[8,128,128]{2,1,0:T(8,128)(2,1)S(1)}, u32[]{:S(2)}, u32[]{:S(2)}) collective-permute-start(bf16[8,128,128]{2,1,0:T(8,128)(2,1)S(1)} %pad_maximum_fusion.3), channel_id=1, source_target_pairs={{0,4},{4,8},{8,12},{12,16},{16,20},{20,24},{24,28},{1,5},{5,9},{9,... | collective-permute-start | bytes 786440 | tf_op jit(solution)/shard_map/ppermute | solution.py:284
  40.1 1.3 %collective-permute-start.8 = (bf16[4,128,128]{2,1,0:T(8,128)(2,1)S(1)}, bf16[4,128,128]{2,1,0:T(8,128)(2,1)S(1)}, u32[]{:S(2)}, u32[]{:S(2)}) collective-permute-start(bf16[4,128,128]{2,1,0:T(8,128)(2,1)S(1)} %pad_maximum_fusion.5), channel_id=1, source_target_pairs={{4,0},{8,4},{12,8},{16,12},{20,16},{24,20},{28,24},{5,1},{9,5},{13... | collective-permute-start | bytes 393224 | tf_op jit(solution)/shard_map/ppermute | solution.py:285
  41.5 3.1 %collective-permute-done.8.refs_8_ = bf16[4,128,128]{2,1,0:T(8,128)(2,1)S(1)} collective-permute-done((bf16[4,128,128]{2,1,0:T(8,128)(2,1)S(1)}, bf16[4,128,128]{2,1,0:T(8,128)(2,1)S(1)}, u32[]{:S(2)}, u32[]{:S(2)}) %collective-permute-start.8) | collective-permute-done | bytes 131104 | tf_op jit(solution)/shard_map/ppermute | solution.py:285
  44.6 1.0 copy-done.3
  45.6 0.9 copy-done.5
  46.5 0.9 mid_products.1
  47.4 1.1 %copy-done = bf16[11,128,512]{2,1,0:T(8,128)(2,1)} copy-done((bf16[11,128,512]{2,1,0:T(8,128)(2,1)}, bf16[11,128,512]{2,1,0:T(8,128)(2,1)S(1)}, u32[]{:S(2)}) %copy-start) | copy-done | bytes 1441816
  48.5 0.7 copy-done.6
  49.2 1.3 %collective-permute-start.12 = (bf16[128,128]{1,0:T(8,128)(2,1)S(1)}, bf16[128,128]{1,0:T(8,128)(2,1)S(1)}, u32[]{:S(2)}, u32[]{:S(2)}) collective-permute-start(bf16[128,128]{1,0:T(8,128)(2,1)S(1)} %get-tuple-element.85), channel_id=1, source_target_pairs={{1,0},{2,3},{5,4},{6,7},{9,8},{10,11},{13,12},{14,15},{17,16},{18,... | collective-permute-start | bytes 98312 | tf_op jit(solution)/shard_map/ppermute | solution.py:407
  50.5 1.3 %collective-permute-start.13 = (bf16[128,128]{1,0:T(8,128)(2,1)S(1)}, bf16[128,128]{1,0:T(8,128)(2,1)S(1)}, u32[]{:S(2)}, u32[]{:S(2)}) collective-permute-start(bf16[128,128]{1,0:T(8,128)(2,1)S(1)} %get-tuple-element.84), channel_id=1, source_target_pairs={{1,3},{2,0},{5,7},{6,4},{9,11},{10,8},{13,15},{14,12},{17,19},{18,... | collective-permute-start | bytes 98312 | tf_op jit(solution)/shard_map/ppermute | solution.py:407
  51.8 0.7 collective-permute-start.14
  52.6 6.2 %collective-permute-done.12 = bf16[128,128]{1,0:T(8,128)(2,1)S(1)} collective-permute-done((bf16[128,128]{1,0:T(8,128)(2,1)S(1)}, bf16[128,128]{1,0:T(8,128)(2,1)S(1)}, u32[]{:S(2)}, u32[]{:S(2)}) %collective-permute-start.12) | collective-permute-done | bytes 32800 | tf_op jit(solution)/shard_map/ppermute | solution.py:407
  58.8 2.3 %collective-permute-done.13 = bf16[128,128]{1,0:T(8,128)(2,1)S(1)} collective-permute-done((bf16[128,128]{1,0:T(8,128)(2,1)S(1)}, bf16[128,128]{1,0:T(8,128)(2,1)S(1)}, u32[]{:S(2)}, u32[]{:S(2)}) %collective-permute-start.13) | collective-permute-done | bytes 32800 | tf_op jit(solution)/shard_map/ppermute | solution.py:407
  61.1 0.8 fusion.2
  61.9 4.1 %collective-permute-start.15 = (bf16[2,128,128]{2,1,0:T(8,128)(2,1)S(1)}, bf16[2,128,128]{2,1,0:T(8,128)(2,1)S(1)}, u32[]{:S(2)}, u32[]{:S(2)}) collective-permute-start(bf16[2,128,128]{2,1,0:T(8,128)(2,1)S(1)} %pad_maximum_fusion.6), channel_id=1, source_target_pairs={{0,4},{4,0},{8,12},{12,8},{16,20},{20,16},{24,28},{28,24},{1,5},{5... | collective-permute-start | bytes 196616 | tf_op jit(solution)/shard_map/ppermute | solution.py:422
  66.0 0.9 collective-permute-done.15
  66.9 3.2 %collective-permute-start.16 = (bf16[2,128,128]{2,1,0:T(8,128)(2,1)S(1)}, bf16[2,128,128]{2,1,0:T(8,128)(2,1)S(1)}, u32[]{:S(2)}, u32[]{:S(2)}) collective-permute-start(bf16[2,128,128]{2,1,0:T(8,128)(2,1)S(1)} %fusion.13.refs_0_), channel_id=1, source_target_pairs={{0,8},{4,12},{8,0},{12,4},{16,24},{20,28},{24,16},{28,20},{1,9},{5... | collective-permute-start | bytes 196616 | tf_op jit(solution)/shard_map/ppermute | solution.py:424
  70.1 1.2 %collective-permute-start.17 = (bf16[2,128,128]{2,1,0:T(8,128)(2,1)S(1)}, bf16[2,128,128]{2,1,0:T(8,128)(2,1)S(1)}, u32[]{:S(2)}, u32[]{:S(2)}) collective-permute-start(bf16[2,128,128]{2,1,0:T(8,128)(2,1)S(1)} %fusion.13.refs_0_), channel_id=1, source_target_pairs={{0,16},{4,20},{8,24},{12,28},{16,0},{20,4},{24,8},{28,12},{1,17},{... | collective-permute-start | bytes 196616 | tf_op jit(solution)/shard_map/ppermute | solution.py:424
  71.4 1.2 %collective-permute-start.18 = (bf16[2,128,128]{2,1,0:T(8,128)(2,1)S(1)}, bf16[2,128,128]{2,1,0:T(8,128)(2,1)S(1)}, u32[]{:S(2)}, u32[]{:S(2)}) collective-permute-start(bf16[2,128,128]{2,1,0:T(8,128)(2,1)S(1)} %fusion.13.refs_0_), channel_id=1, source_target_pairs={{0,24},{4,28},{8,16},{12,20},{16,8},{20,12},{24,0},{28,4},{1,25},{... | collective-permute-start | bytes 196616 | tf_op jit(solution)/shard_map/ppermute | solution.py:424
  72.6 3.5 %shard_map.77.refs_4_ = bf16[256,16384]{1,0:T(8,128)(2,1)S(1)} custom-call(bf16[384,16384]{1,0:T(8,128)(2,1)} %bitcast.72), custom_call_target="tpu_custom_call" | custom-call | tf_op jit(solution)/shard_map/pallas_call | solution.py:327
  76.1 2.3 %shard_map.78.refs_5_ = bf16[256,8192]{1,0:T(8,128)(2,1)S(1)} custom-call(bf16[384,16384]{1,0:T(8,128)(2,1)} %bitcast.73), custom_call_target="tpu_custom_call" | custom-call | tf_op jit(solution)/shard_map/pallas_call | solution.py:327
  78.4 3.4 %fit_sums.1 = f32[8,2,384]{2,1,0:T(2,128)S(1)} custom-call(s32[1]{0:T(128)} %bitcast.17.place, bf16[2,128,128]{2,1,0:T(8,128)(2,1)S(1)} %fusion.13.refs_0_, bf16[2,128,128]{2,1,0:T(8,128)(2,1)S(1)} %collective-permute-done.16.refs_1_, bf16[2,128,128]{2,1,0:T(8,128)(2,1)S(1)} %collective-permute-done.17.refs_2_, ...), custom_call_target="tpu_custom_call" | custom-call | tf_op jit(solution)/shard_map/fit_sums/pallas_call | solution.py:427
  81.8 0.7 mid_second.1
  83.0 1.1 %collective-permute-start.20 = (f32[8,2,384]{2,1,0:T(2,128)S(1)}, f32[8,2,384]{2,1,0:T(2,128)S(1)}, u32[]{:S(2)}, u32[]{:S(2)}) collective-permute-start(f32[8,2,384]{2,1,0:T(2,128)S(1)} %add.79.refs_0_), channel_id=1, source_target_pairs={{0,8},{4,12},{8,0},{12,4},{16,24},{20,28},{24,16},{28,20},{1,9},{5... | collective-permute-start | bytes 73736 | tf_op jit(solution)/shard_map/ppermute | solution.py:437
  84.2 1.3 %collective-permute-start.9 = (bf16[8,128,128]{2,1,0:T(8,128)(2,1)S(1)}, bf16[8,128,128]{2,1,0:T(8,128)(2,1)S(1)}, u32[]{:S(2)}, u32[]{:S(2)}) collective-permute-start(bf16[8,128,128]{2,1,0:T(8,128)(2,1)S(1)} %get-tuple-element.64), channel_id=1, source_target_pairs={{1,0},{2,3},{5,4},{6,7},{9,8},{10,11},{13,12},{14,15},{17,16},{18,... | collective-permute-start | bytes 786440 | tf_op jit(solution)/shard_map/ppermute | solution.py:407
  85.5 1.3 %collective-permute-start.10 = (bf16[8,128,128]{2,1,0:T(8,128)(2,1)S(1)}, bf16[8,128,128]{2,1,0:T(8,128)(2,1)S(1)}, u32[]{:S(2)}, u32[]{:S(2)}) collective-permute-start(bf16[8,128,128]{2,1,0:T(8,128)(2,1)S(1)} %get-tuple-element.63), channel_id=1, source_target_pairs={{1,3},{2,0},{5,7},{6,4},{9,11},{10,8},{13,15},{14,12},{17,19},{18,... | collective-permute-start | bytes 786440 | tf_op jit(solution)/shard_map/ppermute | solution.py:407
  86.8 0.7 collective-permute-start.11
  87.5 1.3 %collective-permute-start.21 = (f32[8,2,384]{2,1,0:T(2,128)S(1)}, f32[8,2,384]{2,1,0:T(2,128)S(1)}, u32[]{:S(2)}, u32[]{:S(2)}) collective-permute-start(f32[8,2,384]{2,1,0:T(2,128)S(1)} %add.79.refs_0_), channel_id=1, source_target_pairs={{0,16},{4,20},{8,24},{12,28},{16,0},{20,4},{24,8},{28,12},{1,17},{... | collective-permute-start | bytes 73736 | tf_op jit(solution)/shard_map/ppermute | solution.py:437
  88.7 1.3 %collective-permute-start.22 = (f32[8,2,384]{2,1,0:T(2,128)S(1)}, f32[8,2,384]{2,1,0:T(2,128)S(1)}, u32[]{:S(2)}, u32[]{:S(2)}) collective-permute-start(f32[8,2,384]{2,1,0:T(2,128)S(1)} %add.79.refs_0_), channel_id=1, source_target_pairs={{0,24},{4,28},{8,16},{12,20},{16,8},{20,12},{24,0},{28,4},{1,25},{... | collective-permute-start | bytes 73736 | tf_op jit(solution)/shard_map/ppermute | solution.py:437
  90.0 2.4 %shard_map.79.refs_4_ = f32[384,3072]{1,0:T(8,128)S(1)} custom-call(f32[384,3072]{1,0:T(8,128)} %bitcast.74), custom_call_target="tpu_custom_call" | custom-call | tf_op jit(solution)/shard_map/pallas_call | solution.py:327
  92.4 1.0 collective-permute-done.22.refs_3_
  93.5 0.8 metric.1
  94.2 1.3 %collective-permute-start.23 = (f32[2,384]{1,0:T(2,128)S(1)}, f32[2,384]{1,0:T(2,128)S(1)}, u32[]{:S(2)}, u32[]{:S(2)}) collective-permute-start(f32[2,384]{1,0:T(2,128)S(1)} %metric.1), channel_id=1, source_target_pairs={{0,3},{1,0},{2,1},{3,2},{4,7},{5,4},{6,5},{7,6},{8,11},{9,8},{10,9... | collective-permute-start | bytes 9224 | tf_op jit(solution)/shard_map/ppermute | solution.py:448
  95.5 6.9 %collective-permute-start.24 = (f32[2,384]{1,0:T(2,128)S(1)}, f32[2,384]{1,0:T(2,128)S(1)}, u32[]{:S(2)}, u32[]{:S(2)}) collective-permute-start(f32[2,384]{1,0:T(2,128)S(1)} %metric.1), channel_id=1, source_target_pairs={{0,2},{1,3},{2,0},{3,1},{4,6},{5,7},{6,4},{7,5},{8,10},{9,11},{10,... | collective-permute-start | bytes 9224 | tf_op jit(solution)/shard_map/ppermute | solution.py:448
  102.6 2.0 %collective-permute-start.25 = (f32[2,384]{1,0:T(2,128)S(1)}, f32[2,384]{1,0:T(2,128)S(1)}, u32[]{:S(2)}, u32[]{:S(2)}) collective-permute-start(f32[2,384]{1,0:T(2,128)S(1)} %metric.1), channel_id=1, source_target_pairs={{0,1},{1,2},{2,3},{3,0},{4,5},{5,6},{6,7},{7,4},{8,9},{9,10},{10,1... | collective-permute-start | bytes 9224 | tf_op jit(solution)/shard_map/ppermute | solution.py:448
  104.6 3.4 %collective-permute-done.25 = f32[2,384]{1,0:T(2,128)S(1)} collective-permute-done((f32[2,384]{1,0:T(2,128)S(1)}, f32[2,384]{1,0:T(2,128)S(1)}, u32[]{:S(2)}, u32[]{:S(2)}) %collective-permute-start.25) | collective-permute-done | bytes 3104 | tf_op jit(solution)/shard_map/ppermute | solution.py:448
  108.6 0.8 maximum_bitcast_fusion
  (60 shorter events, 2.6 us)
Async XLA Ops:
  2.0 17.2 %collective-permute-start.3 = (bf16[16,128,128]{2,1,0:T(8,128)(2,1)S(1)}, bf16[16,128,128]{2,1,0:T(8,128)(2,1)S(1)}, u32[]{:S(2)}, u32[]{:S(2)}) collective-permute-start(bf16[16,128,128]{2,1,0:T(8,128)(2,1)S(1)} %get-tuple-element.29), channel_id=1, source_target_pairs={{1,2},{2,1},{5,6},{6,5},{9,10},{10,9},{13,14},{14,13},{17,18},{18,... | collective-permute-start | bytes 1572872 | tf_op jit(solution)/shard_map/ppermute | solution.py:306
  2.7 32.6 %collective-permute-start.6 = (bf16[16,128,128]{2,1,0:T(8,128)(2,1)S(1)}, bf16[16,128,128]{2,1,0:T(8,128)(2,1)S(1)}, u32[]{:S(2)}, u32[]{:S(2)}) collective-permute-start(bf16[16,128,128]{2,1,0:T(8,128)(2,1)S(1)} %get-tuple-element.29), channel_id=1, source_target_pairs={{0,2},{3,1},{4,6},{7,5},{8,10},{11,9},{12,14},{15,13},{16,18},{19,... | collective-permute-start | bytes 1572872 | tf_op jit(solution)/shard_map/ppermute | solution.py:306
  10.4 22.1 %collective-permute-start.2 = (bf16[16,128,128]{2,1,0:T(8,128)(2,1)S(1)}, bf16[16,128,128]{2,1,0:T(8,128)(2,1)S(1)}, u32[]{:S(2)}, u32[]{:S(2)}) collective-permute-start(bf16[16,128,128]{2,1,0:T(8,128)(2,1)S(1)} %get-tuple-element.28.refs_2_), channel_id=1, source_target_pairs={{0,1},{3,2},{4,5},{7,6},{8,9},{11,10},{12,13},{15,14},{16,17},{19,... | collective-permute-start | bytes 1572872 | tf_op jit(solution)/shard_map/ppermute | solution.py:305
  12.6 6.5 %collective-permute-start.1 = (bf16[5,128,128]{2,1,0:T(8,128)(2,1)S(1)}, bf16[5,128,128]{2,1,0:T(8,128)(2,1)S(1)}, u32[]{:S(2)}, u32[]{:S(2)}) collective-permute-start(bf16[5,128,128]{2,1,0:T(8,128)(2,1)S(1)} %pad_maximum_fusion.4), channel_id=1, source_target_pairs={{4,0},{8,4},{12,8},{16,12},{20,16},{24,20},{28,24},{5,1},{9,5},{13... | collective-permute-start | bytes 491528 | tf_op jit(solution)/shard_map/ppermute | solution.py:285
  14.0 5.2 %collective-permute-start = (bf16[9,128,128]{2,1,0:T(8,128)(2,1)S(1)}, bf16[9,128,128]{2,1,0:T(8,128)(2,1)S(1)}, u32[]{:S(2)}, u32[]{:S(2)}) collective-permute-start(bf16[9,128,128]{2,1,0:T(8,128)(2,1)S(1)} %pad_maximum_fusion.1), channel_id=1, source_target_pairs={{0,4},{4,8},{8,12},{12,16},{16,20},{20,24},{24,28},{1,5},{5,9},{9,... | collective-permute-start | bytes 884744 | tf_op jit(solution)/shard_map/ppermute | solution.py:284
  19.0 22.4 %copy-start.7 = (s32[11]{0:T(128)S(1)}, s32[11]{0:T(128)}, u32[]{:S(2)}) copy-start(s32[11]{0:T(128)} %iota_add_fusion) | copy-start | bytes 136
  19.1 25.5 %copy-start.4 = (bf16[5,128,128]{2,1,0:T(8,128)(2,1)}, bf16[5,128,128]{2,1,0:T(8,128)(2,1)S(1)}, u32[]{:S(2)}) copy-start(bf16[5,128,128]{2,1,0:T(8,128)(2,1)S(1)} %collective-permute-done.1.refs_1_) | copy-start | bytes 491524
  19.1 25.5 %copy-start.2 = (bf16[9,128,128]{2,1,0:T(8,128)(2,1)}, bf16[9,128,128]{2,1,0:T(8,128)(2,1)S(1)}, u32[]{:S(2)}) copy-start(bf16[9,128,128]{2,1,0:T(8,128)(2,1)S(1)} %collective-permute-done.refs_0_) | copy-start | bytes 884740
  32.5 12.1 %collective-permute-start.4 = (bf16[16,128,128]{2,1,0:T(8,128)(2,1)S(1)}, bf16[16,128,128]{2,1,0:T(8,128)(2,1)S(1)}, u32[]{:S(2)}, u32[]{:S(2)}) collective-permute-start(bf16[16,128,128]{2,1,0:T(8,128)(2,1)S(1)} %pad_maximum_fusion), channel_id=1, source_target_pairs={{0,4},{4,8},{8,12},{12,16},{16,20},{20,24},{24,28},{1,5},{5,9},{9,... | collective-permute-start | bytes 1572872 | tf_op jit(solution)/shard_map/ppermute | solution.py:284
  34.0 10.6 %collective-permute-start.5 = (bf16[8,128,128]{2,1,0:T(8,128)(2,1)S(1)}, bf16[8,128,128]{2,1,0:T(8,128)(2,1)S(1)}, u32[]{:S(2)}, u32[]{:S(2)}) collective-permute-start(bf16[8,128,128]{2,1,0:T(8,128)(2,1)S(1)} %pad_maximum_fusion.2), channel_id=1, source_target_pairs={{4,0},{8,4},{12,8},{16,12},{20,16},{24,20},{28,24},{5,1},{9,5},{13... | collective-permute-start | bytes 786440 | tf_op jit(solution)/shard_map/ppermute | solution.py:285
  35.3 9.3 %collective-permute-start.7 = (bf16[8,128,128]{2,1,0:T(8,128)(2,1)S(1)}, bf16[8,128,128]{2,1,0:T(8,128)(2,1)S(1)}, u32[]{:S(2)}, u32[]{:S(2)}) collective-permute-start(bf16[8,128,128]{2,1,0:T(8,128)(2,1)S(1)} %pad_maximum_fusion.3), channel_id=1, source_target_pairs={{0,4},{4,8},{8,12},{12,16},{16,20},{20,24},{24,28},{1,5},{5,9},{9,... | collective-permute-start | bytes 786440 | tf_op jit(solution)/shard_map/ppermute | solution.py:284
  40.1 4.5 %collective-permute-start.8 = (bf16[4,128,128]{2,1,0:T(8,128)(2,1)S(1)}, bf16[4,128,128]{2,1,0:T(8,128)(2,1)S(1)}, u32[]{:S(2)}, u32[]{:S(2)}) collective-permute-start(bf16[4,128,128]{2,1,0:T(8,128)(2,1)S(1)} %pad_maximum_fusion.5), channel_id=1, source_target_pairs={{4,0},{8,4},{12,8},{16,12},{20,16},{24,20},{28,24},{5,1},{9,5},{13... | collective-permute-start | bytes 393224 | tf_op jit(solution)/shard_map/ppermute | solution.py:285
  44.6 1.0 copy-start.3
  45.6 0.9 copy-start.5
  47.4 1.2 %copy-start = (bf16[11,128,512]{2,1,0:T(8,128)(2,1)}, bf16[11,128,512]{2,1,0:T(8,128)(2,1)S(1)}, u32[]{:S(2)}) copy-start(bf16[11,128,512]{2,1,0:T(8,128)(2,1)S(1)} %get-tuple-element.31.order) | copy-start | bytes 4325380
  48.5 0.7 copy-start.6
  49.2 9.6 %collective-permute-start.12 = (bf16[128,128]{1,0:T(8,128)(2,1)S(1)}, bf16[128,128]{1,0:T(8,128)(2,1)S(1)}, u32[]{:S(2)}, u32[]{:S(2)}) collective-permute-start(bf16[128,128]{1,0:T(8,128)(2,1)S(1)} %get-tuple-element.85), channel_id=1, source_target_pairs={{1,0},{2,3},{5,4},{6,7},{9,8},{10,11},{13,12},{14,15},{17,16},{18,... | collective-permute-start | bytes 98312 | tf_op jit(solution)/shard_map/ppermute | solution.py:407
  50.5 10.6 %collective-permute-start.13 = (bf16[128,128]{1,0:T(8,128)(2,1)S(1)}, bf16[128,128]{1,0:T(8,128)(2,1)S(1)}, u32[]{:S(2)}, u32[]{:S(2)}) collective-permute-start(bf16[128,128]{1,0:T(8,128)(2,1)S(1)} %get-tuple-element.84), channel_id=1, source_target_pairs={{1,3},{2,0},{5,7},{6,4},{9,11},{10,8},{13,15},{14,12},{17,19},{18,... | collective-permute-start | bytes 98312 | tf_op jit(solution)/shard_map/ppermute | solution.py:407
  51.8 9.3 %collective-permute-start.14 = (bf16[128,128]{1,0:T(8,128)(2,1)S(1)}, bf16[128,128]{1,0:T(8,128)(2,1)S(1)}, u32[]{:S(2)}, u32[]{:S(2)}) collective-permute-start(bf16[128,128]{1,0:T(8,128)(2,1)S(1)} %get-tuple-element.83), channel_id=1, source_target_pairs={{1,2},{2,1},{5,6},{6,5},{9,10},{10,9},{13,14},{14,13},{17,18},{18,... | collective-permute-start | bytes 98312 | tf_op jit(solution)/shard_map/ppermute | solution.py:407
  61.9 5.0 %collective-permute-start.15 = (bf16[2,128,128]{2,1,0:T(8,128)(2,1)S(1)}, bf16[2,128,128]{2,1,0:T(8,128)(2,1)S(1)}, u32[]{:S(2)}, u32[]{:S(2)}) collective-permute-start(bf16[2,128,128]{2,1,0:T(8,128)(2,1)S(1)} %pad_maximum_fusion.6), channel_id=1, source_target_pairs={{0,4},{4,0},{8,12},{12,8},{16,20},{20,16},{24,28},{28,24},{1,5},{5... | collective-permute-start | bytes 196616 | tf_op jit(solution)/shard_map/ppermute | solution.py:422
  66.9 11.4 %collective-permute-start.16 = (bf16[2,128,128]{2,1,0:T(8,128)(2,1)S(1)}, bf16[2,128,128]{2,1,0:T(8,128)(2,1)S(1)}, u32[]{:S(2)}, u32[]{:S(2)}) collective-permute-start(bf16[2,128,128]{2,1,0:T(8,128)(2,1)S(1)} %fusion.13.refs_0_), channel_id=1, source_target_pairs={{0,8},{4,12},{8,0},{12,4},{16,24},{20,28},{24,16},{28,20},{1,9},{5... | collective-permute-start | bytes 196616 | tf_op jit(solution)/shard_map/ppermute | solution.py:424
  70.1 8.2 %collective-permute-start.17 = (bf16[2,128,128]{2,1,0:T(8,128)(2,1)S(1)}, bf16[2,128,128]{2,1,0:T(8,128)(2,1)S(1)}, u32[]{:S(2)}, u32[]{:S(2)}) collective-permute-start(bf16[2,128,128]{2,1,0:T(8,128)(2,1)S(1)} %fusion.13.refs_0_), channel_id=1, source_target_pairs={{0,16},{4,20},{8,24},{12,28},{16,0},{20,4},{24,8},{28,12},{1,17},{... | collective-permute-start | bytes 196616 | tf_op jit(solution)/shard_map/ppermute | solution.py:424
  71.4 7.0 %collective-permute-start.18 = (bf16[2,128,128]{2,1,0:T(8,128)(2,1)S(1)}, bf16[2,128,128]{2,1,0:T(8,128)(2,1)S(1)}, u32[]{:S(2)}, u32[]{:S(2)}) collective-permute-start(bf16[2,128,128]{2,1,0:T(8,128)(2,1)S(1)} %fusion.13.refs_0_), channel_id=1, source_target_pairs={{0,24},{4,28},{8,16},{12,20},{16,8},{20,12},{24,0},{28,4},{1,25},{... | collective-permute-start | bytes 196616 | tf_op jit(solution)/shard_map/ppermute | solution.py:424
  78.4 3.4 %copy-start.1 = (bf16[11,128,512]{2,1,0:T(8,128)(2,1)S(1)}, bf16[11,128,512]{2,1,0:T(8,128)(2,1)}, u32[]{:S(2)}) copy-start(bf16[11,128,512]{2,1,0:T(8,128)(2,1)} %copy-done) | copy-start | bytes 4325380
  81.8 1.2 %collective-permute-start.19 = (f32[8,2,384]{2,1,0:T(2,128)S(1)}, f32[8,2,384]{2,1,0:T(2,128)S(1)}, u32[]{:S(2)}, u32[]{:S(2)}) collective-permute-start(f32[8,2,384]{2,1,0:T(2,128)S(1)} %fit_sums.1), channel_id=1, source_target_pairs={{0,4},{4,0},{8,12},{12,8},{16,20},{20,16},{24,28},{28,24},{1,5},{5... | collective-permute-start | bytes 73736 | tf_op jit(solution)/shard_map/ppermute | solution.py:435
  83.0 5.8 %collective-permute-start.20 = (f32[8,2,384]{2,1,0:T(2,128)S(1)}, f32[8,2,384]{2,1,0:T(2,128)S(1)}, u32[]{:S(2)}, u32[]{:S(2)}) collective-permute-start(f32[8,2,384]{2,1,0:T(2,128)S(1)} %add.79.refs_0_), channel_id=1, source_target_pairs={{0,8},{4,12},{8,0},{12,4},{16,24},{20,28},{24,16},{28,20},{1,9},{5... | collective-permute-start | bytes 73736 | tf_op jit(solution)/shard_map/ppermute | solution.py:437
  84.2 24.4 %collective-permute-start.9 = (bf16[8,128,128]{2,1,0:T(8,128)(2,1)S(1)}, bf16[8,128,128]{2,1,0:T(8,128)(2,1)S(1)}, u32[]{:S(2)}, u32[]{:S(2)}) collective-permute-start(bf16[8,128,128]{2,1,0:T(8,128)(2,1)S(1)} %get-tuple-element.64), channel_id=1, source_target_pairs={{1,0},{2,3},{5,4},{6,7},{9,8},{10,11},{13,12},{14,15},{17,16},{18,... | collective-permute-start | bytes 786440 | tf_op jit(solution)/shard_map/ppermute | solution.py:407
  85.5 23.1 %collective-permute-start.10 = (bf16[8,128,128]{2,1,0:T(8,128)(2,1)S(1)}, bf16[8,128,128]{2,1,0:T(8,128)(2,1)S(1)}, u32[]{:S(2)}, u32[]{:S(2)}) collective-permute-start(bf16[8,128,128]{2,1,0:T(8,128)(2,1)S(1)} %get-tuple-element.63), channel_id=1, source_target_pairs={{1,3},{2,0},{5,7},{6,4},{9,11},{10,8},{13,15},{14,12},{17,19},{18,... | collective-permute-start | bytes 786440 | tf_op jit(solution)/shard_map/ppermute | solution.py:407
  86.8 21.8 %collective-permute-start.11 = (bf16[8,128,128]{2,1,0:T(8,128)(2,1)S(1)}, bf16[8,128,128]{2,1,0:T(8,128)(2,1)S(1)}, u32[]{:S(2)}, u32[]{:S(2)}) collective-permute-start(bf16[8,128,128]{2,1,0:T(8,128)(2,1)S(1)} %get-tuple-element.62), channel_id=1, source_target_pairs={{1,2},{2,1},{5,6},{6,5},{9,10},{10,9},{13,14},{14,13},{17,18},{18,... | collective-permute-start | bytes 786440 | tf_op jit(solution)/shard_map/ppermute | solution.py:407
  87.5 5.0 %collective-permute-start.21 = (f32[8,2,384]{2,1,0:T(2,128)S(1)}, f32[8,2,384]{2,1,0:T(2,128)S(1)}, u32[]{:S(2)}, u32[]{:S(2)}) collective-permute-start(f32[8,2,384]{2,1,0:T(2,128)S(1)} %add.79.refs_0_), channel_id=1, source_target_pairs={{0,16},{4,20},{8,24},{12,28},{16,0},{20,4},{24,8},{28,12},{1,17},{... | collective-permute-start | bytes 73736 | tf_op jit(solution)/shard_map/ppermute | solution.py:437
  88.7 4.7 %collective-permute-start.22 = (f32[8,2,384]{2,1,0:T(2,128)S(1)}, f32[8,2,384]{2,1,0:T(2,128)S(1)}, u32[]{:S(2)}, u32[]{:S(2)}) collective-permute-start(f32[8,2,384]{2,1,0:T(2,128)S(1)} %add.79.refs_0_), channel_id=1, source_target_pairs={{0,24},{4,28},{8,16},{12,20},{16,8},{20,12},{24,0},{28,4},{1,25},{... | collective-permute-start | bytes 73736 | tf_op jit(solution)/shard_map/ppermute | solution.py:437
  94.2 8.3 %collective-permute-start.23 = (f32[2,384]{1,0:T(2,128)S(1)}, f32[2,384]{1,0:T(2,128)S(1)}, u32[]{:S(2)}, u32[]{:S(2)}) collective-permute-start(f32[2,384]{1,0:T(2,128)S(1)} %metric.1), channel_id=1, source_target_pairs={{0,3},{1,0},{2,1},{3,2},{4,7},{5,4},{6,5},{7,6},{8,11},{9,8},{10,9... | collective-permute-start | bytes 9224 | tf_op jit(solution)/shard_map/ppermute | solution.py:448
  95.5 9.0 %collective-permute-start.24 = (f32[2,384]{1,0:T(2,128)S(1)}, f32[2,384]{1,0:T(2,128)S(1)}, u32[]{:S(2)}, u32[]{:S(2)}) collective-permute-start(f32[2,384]{1,0:T(2,128)S(1)} %metric.1), channel_id=1, source_target_pairs={{0,2},{1,3},{2,0},{3,1},{4,6},{5,7},{6,4},{7,5},{8,10},{9,11},{10,... | collective-permute-start | bytes 9224 | tf_op jit(solution)/shard_map/ppermute | solution.py:448
  102.6 5.4 %collective-permute-start.25 = (f32[2,384]{1,0:T(2,128)S(1)}, f32[2,384]{1,0:T(2,128)S(1)}, u32[]{:S(2)}, u32[]{:S(2)}) collective-permute-start(f32[2,384]{1,0:T(2,128)S(1)} %metric.1), channel_id=1, source_target_pairs={{0,1},{1,2},{2,3},{3,0},{4,5},{5,6},{6,7},{7,4},{8,9},{9,10},{10,1... | collective-permute-start | bytes 9224 | tf_op jit(solution)/shard_map/ppermute | solution.py:448

commit v3 on v2

--- a/solution.py
+++ b/solution.py
@@ -296,7 +296,7 @@
         return low, high
 
     wanted = [(my_slot - side_a) % slots, (side_b - my_slot) % slots]
-    wanted += [(my_slot - plane) % slots for plane in range(slots)]
+    wanted += [my_slot ^ plane for plane in range(slots)]
     wanted = [[index == step for step in range(slots)] for index in wanted]
 
     near_got, far_got = {0: near}, {}
@@ -377,7 +377,7 @@
     wide_rows = count_rows + up_rows + down_rows
     mid_rows = count_rows + 2 * half - 1
     plan = {"inputs": len(inputs), "moves": tuple(moves)}
-    group = 4 if slots <= 4 else 1
+    group = mid_rows if slots <= 4 else 1
     bands = jax.ShapeDtypeStruct((mid_rows, blk, slots * blk), jnp.bfloat16)
     wide_band = pltpu.VMEM((wide_rows, blk, slots * blk), jnp.bfloat16)
     blocks = 2 * wide_rows * slots
@@ -444,14 +444,14 @@
         compiler_params=pltpu.CompilerParams(vmem_limit_bytes=8 << 20),
         name="metric",
     )(*pieces, metric)
-    got = [part] + [
-        lax.ppermute(part, "orb", [(i, (i + step) % slots) for i in range(slots)]) for step in range(1, slots)
-    ]
+    got = [part] * slots
+    for distance in range(slots - 1, 0, -1):
+        got[distance] = lax.ppermute(part, "orb", swap_pairs(slots, distance))
     coefficients = None
     for plane in range(slots):
         value = got[0]
-        for step in range(1, slots):
-            value = jnp.where(wanted[fields + plane][step], got[step], value)
+        for distance in range(1, slots):
+            value = jnp.where(wanted[fields + plane][distance], got[distance], value)
         coefficients = value if coefficients is None else coefficients + value
     return (response, coefficients[None])
 

time: 110 us -> 108 us (0.982)
  waiting for transfers between devices: 30.8 us -> 28.4 us
    ppermute x3, waiting for transfers between devices: 3.49 us -> 1.58 us  [on_device(): got[distance] = lax.ppermute(part, 'orb', swap_pairs(slots, distance))]
  transfers between devices with their start and end apart: 26 -> 26, of which waited for: 9 -> 8; matrix products, arithmetic and copies ran while one was open for 3% -> 3% of each run, Pallas kernels for 9% -> 9%
where the time goes in v3:
time: 108 us; the launch traced here: 107 us
  starting transfers between devices  52.9 us (49%)
  waiting for transfers between devices  28.4 us (26%)
  Pallas kernels  15.2 us (14%)
  local copies, waits for them, and re-layouts  4.75 us (4%)
  other arithmetic  3.94 us (4%)
  between operations  1.84 us (2%)
    ppermute x1, waiting for transfers between devices, on_device(): lax.ppermute(near, 'orb', [(side_a - distance, side_a), (side_b + distanc...  13.2 us
    ppermute x3, starting transfers between devices, on_device(): got[distance] = lax.ppermute(part, 'orb', swap_pairs(slots, distance))  10.2 us
    ppermute x3, starting transfers between devices, stage_rims(): low = lax.ppermute(jnp.concatenate(low, 0), 'aux', forward)  9.1 us
    ppermute x2, starting transfers between devices, on_device(): lax.ppermute(far, 'orb', [(side_a - distance, side_b), (side_b + distance...  8.39 us
    pallas_call x3, Pallas kernels, preload(): pl.pallas_call(functools.partial(preload_kernel, parts), out_shape=shapes...  8.13 us
    ppermute x6, waiting for transfers between devices, scatter(): got.append(lax.ppermute(blocks[step], 'orb', pairs))  8.01 us
    ppermute x6, starting transfers between devices, scatter(): got.append(lax.ppermute(blocks[step], 'orb', pairs))  6.5 us
    ppermute x3, starting transfers between devices, on_device(): lax.ppermute(fit_own, 'aux', swap_pairs(aux_count, distance))  5.67 us
  transfers between devices with their start and end apart: 26, of which 8 were waited for; matrix products, arithmetic and copies ran while one was open for 3% of the time, Pallas kernels for 9%

profile of v3, /device:TPU:0, one launch (start us, length us, event | category | flops | bytes accessed | tf_op | source)
XLA Modules:
  0.0 107.0 jit_solution(5839715245799352483)
XLA Ops:
  0.6 1.4 %pack.1 = (bf16[16,128,128]{2,1,0:T(8,128)(2,1)S(1)}, bf16[16,128,128]{2,1,0:T(8,128)(2,1)S(1)}) custom-call(s32[4,8]{1,0:T(4,128)} %bitcast.75, bf16[8,1,128,128]{3,2,1,0:T(8,128)(2,1)} %density_in.1, bf16[2,8,1,128,128]{4,3,2,1,0:T(8,128)(2,1)} %field_terms.1), custom_call_target="tpu_custom_call" | custom-call | tf_op jit(solution)/shard_map/pack/pallas_call | solution.py:261
  2.0 0.7 collective-permute-start.3
  2.7 7.7 %collective-permute-start.6 = (bf16[16,128,128]{2,1,0:T(8,128)(2,1)S(1)}, bf16[16,128,128]{2,1,0:T(8,128)(2,1)S(1)}, u32[]{:S(2)}, u32[]{:S(2)}) collective-permute-start(bf16[16,128,128]{2,1,0:T(8,128)(2,1)S(1)} %get-tuple-element.29), channel_id=1, source_target_pairs={{0,2},{3,1},{4,6},{7,5},{8,10},{11,9},{12,14},{15,13},{16,18},{19,... | collective-permute-start | bytes 1572872 | tf_op jit(solution)/shard_map/ppermute | solution.py:306
  10.4 1.4 %collective-permute-start.2 = (bf16[16,128,128]{2,1,0:T(8,128)(2,1)S(1)}, bf16[16,128,128]{2,1,0:T(8,128)(2,1)S(1)}, u32[]{:S(2)}, u32[]{:S(2)}) collective-permute-start(bf16[16,128,128]{2,1,0:T(8,128)(2,1)S(1)} %get-tuple-element.28.refs_2_), channel_id=1, source_target_pairs={{0,1},{3,2},{4,5},{7,6},{8,9},{11,10},{12,13},{15,14},{16,17},{19,... | collective-permute-start | bytes 1572872 | tf_op jit(solution)/shard_map/ppermute | solution.py:305
  11.8 0.7 convert_element_type.31
  12.6 1.3 %collective-permute-start.1 = (bf16[5,128,128]{2,1,0:T(8,128)(2,1)S(1)}, bf16[5,128,128]{2,1,0:T(8,128)(2,1)S(1)}, u32[]{:S(2)}, u32[]{:S(2)}) collective-permute-start(bf16[5,128,128]{2,1,0:T(8,128)(2,1)S(1)} %pad_maximum_fusion.4), channel_id=1, source_target_pairs={{4,0},{8,4},{12,8},{16,12},{20,16},{24,20},{28,24},{5,1},{9,5},{13... | collective-permute-start | bytes 491528 | tf_op jit(solution)/shard_map/ppermute | solution.py:285
  14.0 3.0 %collective-permute-start = (bf16[9,128,128]{2,1,0:T(8,128)(2,1)S(1)}, bf16[9,128,128]{2,1,0:T(8,128)(2,1)S(1)}, u32[]{:S(2)}, u32[]{:S(2)}) collective-permute-start(bf16[9,128,128]{2,1,0:T(8,128)(2,1)S(1)} %pad_maximum_fusion.1), channel_id=1, source_target_pairs={{0,4},{4,8},{8,12},{12,16},{16,20},{20,24},{24,28},{1,5},{5,9},{9,... | collective-permute-start | bytes 884744 | tf_op jit(solution)/shard_map/ppermute | solution.py:284
  18.3 0.8 copy.20
  19.2 13.2 %collective-permute-done.2.refs_5_ = bf16[16,128,128]{2,1,0:T(8,128)(2,1)S(1)} collective-permute-done((bf16[16,128,128]{2,1,0:T(8,128)(2,1)S(1)}, bf16[16,128,128]{2,1,0:T(8,128)(2,1)S(1)}, u32[]{:S(2)}, u32[]{:S(2)}) %collective-permute-start.2) | collective-permute-done | bytes 524320 | tf_op jit(solution)/shard_map/ppermute | solution.py:305
  32.5 1.3 %collective-permute-start.4 = (bf16[16,128,128]{2,1,0:T(8,128)(2,1)S(1)}, bf16[16,128,128]{2,1,0:T(8,128)(2,1)S(1)}, u32[]{:S(2)}, u32[]{:S(2)}) collective-permute-start(bf16[16,128,128]{2,1,0:T(8,128)(2,1)S(1)} %pad_maximum_fusion), channel_id=1, source_target_pairs={{0,4},{4,8},{8,12},{12,16},{16,20},{20,24},{24,28},{1,5},{5,9},{9,... | collective-permute-start | bytes 1572872 | tf_op jit(solution)/shard_map/ppermute | solution.py:284
  34.0 1.3 %collective-permute-start.5 = (bf16[8,128,128]{2,1,0:T(8,128)(2,1)S(1)}, bf16[8,128,128]{2,1,0:T(8,128)(2,1)S(1)}, u32[]{:S(2)}, u32[]{:S(2)}) collective-permute-start(bf16[8,128,128]{2,1,0:T(8,128)(2,1)S(1)} %pad_maximum_fusion.2), channel_id=1, source_target_pairs={{4,0},{8,4},{12,8},{16,12},{20,16},{24,20},{28,24},{5,1},{9,5},{13... | collective-permute-start | bytes 786440 | tf_op jit(solution)/shard_map/ppermute | solution.py:285
  35.3 4.7 %collective-permute-start.7 = (bf16[8,128,128]{2,1,0:T(8,128)(2,1)S(1)}, bf16[8,128,128]{2,1,0:T(8,128)(2,1)S(1)}, u32[]{:S(2)}, u32[]{:S(2)}) collective-permute-start(bf16[8,128,128]{2,1,0:T(8,128)(2,1)S(1)} %pad_maximum_fusion.3), channel_id=1, source_target_pairs={{0,4},{4,8},{8,12},{12,16},{16,20},{20,24},{24,28},{1,5},{5,9},{9,... | collective-permute-start | bytes 786440 | tf_op jit(solution)/shard_map/ppermute | solution.py:284
  40.1 1.3 %collective-permute-start.8 = (bf16[4,128,128]{2,1,0:T(8,128)(2,1)S(1)}, bf16[4,128,128]{2,1,0:T(8,128)(2,1)S(1)}, u32[]{:S(2)}, u32[]{:S(2)}) collective-permute-start(bf16[4,128,128]{2,1,0:T(8,128)(2,1)S(1)} %pad_maximum_fusion.5), channel_id=1, source_target_pairs={{4,0},{8,4},{12,8},{16,12},{20,16},{24,20},{28,24},{5,1},{9,5},{13... | collective-permute-start | bytes 393224 | tf_op jit(solution)/shard_map/ppermute | solution.py:285
  41.5 3.1 %collective-permute-done.8.refs_8_ = bf16[4,128,128]{2,1,0:T(8,128)(2,1)S(1)} collective-permute-done((bf16[4,128,128]{2,1,0:T(8,128)(2,1)S(1)}, bf16[4,128,128]{2,1,0:T(8,128)(2,1)S(1)}, u32[]{:S(2)}, u32[]{:S(2)}) %collective-permute-start.8) | collective-permute-done | bytes 131104 | tf_op jit(solution)/shard_map/ppermute | solution.py:285
  44.6 1.0 copy-done.3
  45.6 0.9 copy-done.5
  46.5 0.9 mid_products.1
  47.4 1.1 %copy-done = bf16[11,128,512]{2,1,0:T(8,128)(2,1)} copy-done((bf16[11,128,512]{2,1,0:T(8,128)(2,1)}, bf16[11,128,512]{2,1,0:T(8,128)(2,1)S(1)}, u32[]{:S(2)}) %copy-start) | copy-done | bytes 1441816
  48.5 0.7 copy-done.6
  49.2 1.3 %collective-permute-start.12 = (bf16[128,128]{1,0:T(8,128)(2,1)S(1)}, bf16[128,128]{1,0:T(8,128)(2,1)S(1)}, u32[]{:S(2)}, u32[]{:S(2)}) collective-permute-start(bf16[128,128]{1,0:T(8,128)(2,1)S(1)} %get-tuple-element.85), channel_id=1, source_target_pairs={{1,0},{2,3},{5,4},{6,7},{9,8},{10,11},{13,12},{14,15},{17,16},{18,... | collective-permute-start | bytes 98312 | tf_op jit(solution)/shard_map/ppermute | solution.py:407
  50.5 1.3 %collective-permute-start.13 = (bf16[128,128]{1,0:T(8,128)(2,1)S(1)}, bf16[128,128]{1,0:T(8,128)(2,1)S(1)}, u32[]{:S(2)}, u32[]{:S(2)}) collective-permute-start(bf16[128,128]{1,0:T(8,128)(2,1)S(1)} %get-tuple-element.84), channel_id=1, source_target_pairs={{1,3},{2,0},{5,7},{6,4},{9,11},{10,8},{13,15},{14,12},{17,19},{18,... | collective-permute-start | bytes 98312 | tf_op jit(solution)/shard_map/ppermute | solution.py:407
  51.8 0.7 collective-permute-start.14
  52.5 5.7 %collective-permute-done.12 = bf16[128,128]{1,0:T(8,128)(2,1)S(1)} collective-permute-done((bf16[128,128]{1,0:T(8,128)(2,1)S(1)}, bf16[128,128]{1,0:T(8,128)(2,1)S(1)}, u32[]{:S(2)}, u32[]{:S(2)}) %collective-permute-start.12) | collective-permute-done | bytes 32800 | tf_op jit(solution)/shard_map/ppermute | solution.py:407
  58.3 2.3 %collective-permute-done.13 = bf16[128,128]{1,0:T(8,128)(2,1)S(1)} collective-permute-done((bf16[128,128]{1,0:T(8,128)(2,1)S(1)}, bf16[128,128]{1,0:T(8,128)(2,1)S(1)}, u32[]{:S(2)}, u32[]{:S(2)}) %collective-permute-start.13) | collective-permute-done | bytes 32800 | tf_op jit(solution)/shard_map/ppermute | solution.py:407
  60.5 0.8 fusion.2
  61.3 4.1 %collective-permute-start.15 = (bf16[2,128,128]{2,1,0:T(8,128)(2,1)S(1)}, bf16[2,128,128]{2,1,0:T(8,128)(2,1)S(1)}, u32[]{:S(2)}, u32[]{:S(2)}) collective-permute-start(bf16[2,128,128]{2,1,0:T(8,128)(2,1)S(1)} %pad_maximum_fusion.6), channel_id=1, source_target_pairs={{0,4},{4,0},{8,12},{12,8},{16,20},{20,16},{24,28},{28,24},{1,5},{5... | collective-permute-start | bytes 196616 | tf_op jit(solution)/shard_map/ppermute | solution.py:422
  65.5 0.9 collective-permute-done.15
  66.4 3.2 %collective-permute-start.16 = (bf16[2,128,128]{2,1,0:T(8,128)(2,1)S(1)}, bf16[2,128,128]{2,1,0:T(8,128)(2,1)S(1)}, u32[]{:S(2)}, u32[]{:S(2)}) collective-permute-start(bf16[2,128,128]{2,1,0:T(8,128)(2,1)S(1)} %fusion.13.refs_0_), channel_id=1, source_target_pairs={{0,8},{4,12},{8,0},{12,4},{16,24},{20,28},{24,16},{28,20},{1,9},{5... | collective-permute-start | bytes 196616 | tf_op jit(solution)/shard_map/ppermute | solution.py:424
  69.6 1.2 %collective-permute-start.17 = (bf16[2,128,128]{2,1,0:T(8,128)(2,1)S(1)}, bf16[2,128,128]{2,1,0:T(8,128)(2,1)S(1)}, u32[]{:S(2)}, u32[]{:S(2)}) collective-permute-start(bf16[2,128,128]{2,1,0:T(8,128)(2,1)S(1)} %fusion.13.refs_0_), channel_id=1, source_target_pairs={{0,16},{4,20},{8,24},{12,28},{16,0},{20,4},{24,8},{28,12},{1,17},{... | collective-permute-start | bytes 196616 | tf_op jit(solution)/shard_map/ppermute | solution.py:424
  70.8 1.2 %collective-permute-start.18 = (bf16[2,128,128]{2,1,0:T(8,128)(2,1)S(1)}, bf16[2,128,128]{2,1,0:T(8,128)(2,1)S(1)}, u32[]{:S(2)}, u32[]{:S(2)}) collective-permute-start(bf16[2,128,128]{2,1,0:T(8,128)(2,1)S(1)} %fusion.13.refs_0_), channel_id=1, source_target_pairs={{0,24},{4,28},{8,16},{12,20},{16,8},{20,12},{24,0},{28,4},{1,25},{... | collective-permute-start | bytes 196616 | tf_op jit(solution)/shard_map/ppermute | solution.py:424
  72.1 3.5 %shard_map.77.refs_4_ = bf16[256,16384]{1,0:T(8,128)(2,1)S(1)} custom-call(bf16[384,16384]{1,0:T(8,128)(2,1)} %bitcast.72), custom_call_target="tpu_custom_call" | custom-call | tf_op jit(solution)/shard_map/pallas_call | solution.py:327
  75.6 2.3 %shard_map.78.refs_5_ = bf16[256,8192]{1,0:T(8,128)(2,1)S(1)} custom-call(bf16[384,16384]{1,0:T(8,128)(2,1)} %bitcast.73), custom_call_target="tpu_custom_call" | custom-call | tf_op jit(solution)/shard_map/pallas_call | solution.py:327
  77.9 3.4 %fit_sums.1 = f32[8,2,384]{2,1,0:T(2,128)S(1)} custom-call(s32[1]{0:T(128)} %bitcast.17.place, bf16[2,128,128]{2,1,0:T(8,128)(2,1)S(1)} %fusion.13.refs_0_, bf16[2,128,128]{2,1,0:T(8,128)(2,1)S(1)} %collective-permute-done.16.refs_1_, bf16[2,128,128]{2,1,0:T(8,128)(2,1)S(1)} %collective-permute-done.17.refs_2_, ...), custom_call_target="tpu_custom_call" | custom-call | tf_op jit(solution)/shard_map/fit_sums/pallas_call | solution.py:427
  81.3 0.7 mid_second.1
  82.5 1.1 %collective-permute-start.20 = (f32[8,2,384]{2,1,0:T(2,128)S(1)}, f32[8,2,384]{2,1,0:T(2,128)S(1)}, u32[]{:S(2)}, u32[]{:S(2)}) collective-permute-start(f32[8,2,384]{2,1,0:T(2,128)S(1)} %add.64.refs_0_), channel_id=1, source_target_pairs={{0,8},{4,12},{8,0},{12,4},{16,24},{20,28},{24,16},{28,20},{1,9},{5... | collective-permute-start | bytes 73736 | tf_op jit(solution)/shard_map/ppermute | solution.py:437
  83.7 1.3 %collective-permute-start.9 = (bf16[8,128,128]{2,1,0:T(8,128)(2,1)S(1)}, bf16[8,128,128]{2,1,0:T(8,128)(2,1)S(1)}, u32[]{:S(2)}, u32[]{:S(2)}) collective-permute-start(bf16[8,128,128]{2,1,0:T(8,128)(2,1)S(1)} %get-tuple-element.64), channel_id=1, source_target_pairs={{1,0},{2,3},{5,4},{6,7},{9,8},{10,11},{13,12},{14,15},{17,16},{18,... | collective-permute-start | bytes 786440 | tf_op jit(solution)/shard_map/ppermute | solution.py:407
  85.0 1.3 %collective-permute-start.10 = (bf16[8,128,128]{2,1,0:T(8,128)(2,1)S(1)}, bf16[8,128,128]{2,1,0:T(8,128)(2,1)S(1)}, u32[]{:S(2)}, u32[]{:S(2)}) collective-permute-start(bf16[8,128,128]{2,1,0:T(8,128)(2,1)S(1)} %get-tuple-element.63), channel_id=1, source_target_pairs={{1,3},{2,0},{5,7},{6,4},{9,11},{10,8},{13,15},{14,12},{17,19},{18,... | collective-permute-start | bytes 786440 | tf_op jit(solution)/shard_map/ppermute | solution.py:407
  86.3 0.7 collective-permute-start.11
  86.9 1.3 %collective-permute-start.21 = (f32[8,2,384]{2,1,0:T(2,128)S(1)}, f32[8,2,384]{2,1,0:T(2,128)S(1)}, u32[]{:S(2)}, u32[]{:S(2)}) collective-permute-start(f32[8,2,384]{2,1,0:T(2,128)S(1)} %add.64.refs_0_), channel_id=1, source_target_pairs={{0,16},{4,20},{8,24},{12,28},{16,0},{20,4},{24,8},{28,12},{1,17},{... | collective-permute-start | bytes 73736 | tf_op jit(solution)/shard_map/ppermute | solution.py:437
  88.2 1.3 %collective-permute-start.22 = (f32[8,2,384]{2,1,0:T(2,128)S(1)}, f32[8,2,384]{2,1,0:T(2,128)S(1)}, u32[]{:S(2)}, u32[]{:S(2)}) collective-permute-start(f32[8,2,384]{2,1,0:T(2,128)S(1)} %add.64.refs_0_), channel_id=1, source_target_pairs={{0,24},{4,28},{8,16},{12,20},{16,8},{20,12},{24,0},{28,4},{1,25},{... | collective-permute-start | bytes 73736 | tf_op jit(solution)/shard_map/ppermute | solution.py:437
  89.5 2.4 %shard_map.79.refs_4_ = f32[384,3072]{1,0:T(8,128)S(1)} custom-call(f32[384,3072]{1,0:T(8,128)} %bitcast.74), custom_call_target="tpu_custom_call" | custom-call | tf_op jit(solution)/shard_map/pallas_call | solution.py:327
  91.9 1.0 collective-permute-done.22.refs_3_
  93.0 0.8 metric.1
  93.7 1.3 %collective-permute-start.23 = (f32[2,384]{1,0:T(2,128)S(1)}, f32[2,384]{1,0:T(2,128)S(1)}, u32[]{:S(2)}, u32[]{:S(2)}) collective-permute-start(f32[2,384]{1,0:T(2,128)S(1)} %metric.1), channel_id=1, source_target_pairs={{0,3},{1,2},{2,1},{3,0},{4,7},{5,6},{6,5},{7,4},{8,11},{9,10},{10,... | collective-permute-start | bytes 9224 | tf_op jit(solution)/shard_map/ppermute | solution.py:449
  95.0 6.7 %collective-permute-start.24 = (f32[2,384]{1,0:T(2,128)S(1)}, f32[2,384]{1,0:T(2,128)S(1)}, u32[]{:S(2)}, u32[]{:S(2)}) collective-permute-start(f32[2,384]{1,0:T(2,128)S(1)} %metric.1), channel_id=1, source_target_pairs={{0,2},{1,3},{2,0},{3,1},{4,6},{5,7},{6,4},{7,5},{8,10},{9,11},{10,... | collective-permute-start | bytes 9224 | tf_op jit(solution)/shard_map/ppermute | solution.py:449
  101.8 2.1 %collective-permute-start.25 = (f32[2,384]{1,0:T(2,128)S(1)}, f32[2,384]{1,0:T(2,128)S(1)}, u32[]{:S(2)}, u32[]{:S(2)}) collective-permute-start(f32[2,384]{1,0:T(2,128)S(1)} %metric.1), channel_id=1, source_target_pairs={{0,1},{1,0},{2,3},{3,2},{4,5},{5,4},{6,7},{7,6},{8,9},{9,8},{10,11... | collective-permute-start | bytes 9224 | tf_op jit(solution)/shard_map/ppermute | solution.py:449
  103.9 1.6 %collective-permute-done.25 = f32[2,384]{1,0:T(2,128)S(1)} collective-permute-done((f32[2,384]{1,0:T(2,128)S(1)}, f32[2,384]{1,0:T(2,128)S(1)}, u32[]{:S(2)}, u32[]{:S(2)}) %collective-permute-start.25) | collective-permute-done | bytes 3104 | tf_op jit(solution)/shard_map/ppermute | solution.py:449
  106.2 0.8 maximum_bitcast_fusion
  (60 shorter events, 2.5 us)
Async XLA Ops:
  2.0 17.2 %collective-permute-start.3 = (bf16[16,128,128]{2,1,0:T(8,128)(2,1)S(1)}, bf16[16,128,128]{2,1,0:T(8,128)(2,1)S(1)}, u32[]{:S(2)}, u32[]{:S(2)}) collective-permute-start(bf16[16,128,128]{2,1,0:T(8,128)(2,1)S(1)} %get-tuple-element.29), channel_id=1, source_target_pairs={{1,2},{2,1},{5,6},{6,5},{9,10},{10,9},{13,14},{14,13},{17,18},{18,... | collective-permute-start | bytes 1572872 | tf_op jit(solution)/shard_map/ppermute | solution.py:306
  2.7 32.6 %collective-permute-start.6 = (bf16[16,128,128]{2,1,0:T(8,128)(2,1)S(1)}, bf16[16,128,128]{2,1,0:T(8,128)(2,1)S(1)}, u32[]{:S(2)}, u32[]{:S(2)}) collective-permute-start(bf16[16,128,128]{2,1,0:T(8,128)(2,1)S(1)} %get-tuple-element.29), channel_id=1, source_target_pairs={{0,2},{3,1},{4,6},{7,5},{8,10},{11,9},{12,14},{15,13},{16,18},{19,... | collective-permute-start | bytes 1572872 | tf_op jit(solution)/shard_map/ppermute | solution.py:306
  10.4 22.1 %collective-permute-start.2 = (bf16[16,128,128]{2,1,0:T(8,128)(2,1)S(1)}, bf16[16,128,128]{2,1,0:T(8,128)(2,1)S(1)}, u32[]{:S(2)}, u32[]{:S(2)}) collective-permute-start(bf16[16,128,128]{2,1,0:T(8,128)(2,1)S(1)} %get-tuple-element.28.refs_2_), channel_id=1, source_target_pairs={{0,1},{3,2},{4,5},{7,6},{8,9},{11,10},{12,13},{15,14},{16,17},{19,... | collective-permute-start | bytes 1572872 | tf_op jit(solution)/shard_map/ppermute | solution.py:305
  12.6 6.5 %collective-permute-start.1 = (bf16[5,128,128]{2,1,0:T(8,128)(2,1)S(1)}, bf16[5,128,128]{2,1,0:T(8,128)(2,1)S(1)}, u32[]{:S(2)}, u32[]{:S(2)}) collective-permute-start(bf16[5,128,128]{2,1,0:T(8,128)(2,1)S(1)} %pad_maximum_fusion.4), channel_id=1, source_target_pairs={{4,0},{8,4},{12,8},{16,12},{20,16},{24,20},{28,24},{5,1},{9,5},{13... | collective-permute-start | bytes 491528 | tf_op jit(solution)/shard_map/ppermute | solution.py:285
  14.0 5.2 %collective-permute-start = (bf16[9,128,128]{2,1,0:T(8,128)(2,1)S(1)}, bf16[9,128,128]{2,1,0:T(8,128)(2,1)S(1)}, u32[]{:S(2)}, u32[]{:S(2)}) collective-permute-start(bf16[9,128,128]{2,1,0:T(8,128)(2,1)S(1)} %pad_maximum_fusion.1), channel_id=1, source_target_pairs={{0,4},{4,8},{8,12},{12,16},{16,20},{20,24},{24,28},{1,5},{5,9},{9,... | collective-permute-start | bytes 884744 | tf_op jit(solution)/shard_map/ppermute | solution.py:284
  19.0 22.4 %copy-start.7 = (s32[11]{0:T(128)S(1)}, s32[11]{0:T(128)}, u32[]{:S(2)}) copy-start(s32[11]{0:T(128)} %iota_add_fusion) | copy-start | bytes 136
  19.1 25.5 %copy-start.4 = (bf16[5,128,128]{2,1,0:T(8,128)(2,1)}, bf16[5,128,128]{2,1,0:T(8,128)(2,1)S(1)}, u32[]{:S(2)}) copy-start(bf16[5,128,128]{2,1,0:T(8,128)(2,1)S(1)} %collective-permute-done.1.refs_1_) | copy-start | bytes 491524
  19.1 25.5 %copy-start.2 = (bf16[9,128,128]{2,1,0:T(8,128)(2,1)}, bf16[9,128,128]{2,1,0:T(8,128)(2,1)S(1)}, u32[]{:S(2)}) copy-start(bf16[9,128,128]{2,1,0:T(8,128)(2,1)S(1)} %collective-permute-done.refs_0_) | copy-start | bytes 884740
  32.5 12.1 %collective-permute-start.4 = (bf16[16,128,128]{2,1,0:T(8,128)(2,1)S(1)}, bf16[16,128,128]{2,1,0:T(8,128)(2,1)S(1)}, u32[]{:S(2)}, u32[]{:S(2)}) collective-permute-start(bf16[16,128,128]{2,1,0:T(8,128)(2,1)S(1)} %pad_maximum_fusion), channel_id=1, source_target_pairs={{0,4},{4,8},{8,12},{12,16},{16,20},{20,24},{24,28},{1,5},{5,9},{9,... | collective-permute-start | bytes 1572872 | tf_op jit(solution)/shard_map/ppermute | solution.py:284
  34.0 10.6 %collective-permute-start.5 = (bf16[8,128,128]{2,1,0:T(8,128)(2,1)S(1)}, bf16[8,128,128]{2,1,0:T(8,128)(2,1)S(1)}, u32[]{:S(2)}, u32[]{:S(2)}) collective-permute-start(bf16[8,128,128]{2,1,0:T(8,128)(2,1)S(1)} %pad_maximum_fusion.2), channel_id=1, source_target_pairs={{4,0},{8,4},{12,8},{16,12},{20,16},{24,20},{28,24},{5,1},{9,5},{13... | collective-permute-start | bytes 786440 | tf_op jit(solution)/shard_map/ppermute | solution.py:285
  35.3 9.3 %collective-permute-start.7 = (bf16[8,128,128]{2,1,0:T(8,128)(2,1)S(1)}, bf16[8,128,128]{2,1,0:T(8,128)(2,1)S(1)}, u32[]{:S(2)}, u32[]{:S(2)}) collective-permute-start(bf16[8,128,128]{2,1,0:T(8,128)(2,1)S(1)} %pad_maximum_fusion.3), channel_id=1, source_target_pairs={{0,4},{4,8},{8,12},{12,16},{16,20},{20,24},{24,28},{1,5},{5,9},{9,... | collective-permute-start | bytes 786440 | tf_op jit(solution)/shard_map/ppermute | solution.py:284
  40.1 4.5 %collective-permute-start.8 = (bf16[4,128,128]{2,1,0:T(8,128)(2,1)S(1)}, bf16[4,128,128]{2,1,0:T(8,128)(2,1)S(1)}, u32[]{:S(2)}, u32[]{:S(2)}) collective-permute-start(bf16[4,128,128]{2,1,0:T(8,128)(2,1)S(1)} %pad_maximum_fusion.5), channel_id=1, source_target_pairs={{4,0},{8,4},{12,8},{16,12},{20,16},{24,20},{28,24},{5,1},{9,5},{13... | collective-permute-start | bytes 393224 | tf_op jit(solution)/shard_map/ppermute | solution.py:285
  44.6 1.0 copy-start.3
  45.6 0.9 copy-start.5
  47.4 1.2 %copy-start = (bf16[11,128,512]{2,1,0:T(8,128)(2,1)}, bf16[11,128,512]{2,1,0:T(8,128)(2,1)S(1)}, u32[]{:S(2)}) copy-start(bf16[11,128,512]{2,1,0:T(8,128)(2,1)S(1)} %get-tuple-element.31.order) | copy-start | bytes 4325380
  48.5 0.7 copy-start.6
  49.2 9.1 %collective-permute-start.12 = (bf16[128,128]{1,0:T(8,128)(2,1)S(1)}, bf16[128,128]{1,0:T(8,128)(2,1)S(1)}, u32[]{:S(2)}, u32[]{:S(2)}) collective-permute-start(bf16[128,128]{1,0:T(8,128)(2,1)S(1)} %get-tuple-element.85), channel_id=1, source_target_pairs={{1,0},{2,3},{5,4},{6,7},{9,8},{10,11},{13,12},{14,15},{17,16},{18,... | collective-permute-start | bytes 98312 | tf_op jit(solution)/shard_map/ppermute | solution.py:407
  50.5 10.0 %collective-permute-start.13 = (bf16[128,128]{1,0:T(8,128)(2,1)S(1)}, bf16[128,128]{1,0:T(8,128)(2,1)S(1)}, u32[]{:S(2)}, u32[]{:S(2)}) collective-permute-start(bf16[128,128]{1,0:T(8,128)(2,1)S(1)} %get-tuple-element.84), channel_id=1, source_target_pairs={{1,3},{2,0},{5,7},{6,4},{9,11},{10,8},{13,15},{14,12},{17,19},{18,... | collective-permute-start | bytes 98312 | tf_op jit(solution)/shard_map/ppermute | solution.py:407
  51.8 8.7 %collective-permute-start.14 = (bf16[128,128]{1,0:T(8,128)(2,1)S(1)}, bf16[128,128]{1,0:T(8,128)(2,1)S(1)}, u32[]{:S(2)}, u32[]{:S(2)}) collective-permute-start(bf16[128,128]{1,0:T(8,128)(2,1)S(1)} %get-tuple-element.83), channel_id=1, source_target_pairs={{1,2},{2,1},{5,6},{6,5},{9,10},{10,9},{13,14},{14,13},{17,18},{18,... | collective-permute-start | bytes 98312 | tf_op jit(solution)/shard_map/ppermute | solution.py:407
  61.3 5.0 %collective-permute-start.15 = (bf16[2,128,128]{2,1,0:T(8,128)(2,1)S(1)}, bf16[2,128,128]{2,1,0:T(8,128)(2,1)S(1)}, u32[]{:S(2)}, u32[]{:S(2)}) collective-permute-start(bf16[2,128,128]{2,1,0:T(8,128)(2,1)S(1)} %pad_maximum_fusion.6), channel_id=1, source_target_pairs={{0,4},{4,0},{8,12},{12,8},{16,20},{20,16},{24,28},{28,24},{1,5},{5... | collective-permute-start | bytes 196616 | tf_op jit(solution)/shard_map/ppermute | solution.py:422
  66.4 11.4 %collective-permute-start.16 = (bf16[2,128,128]{2,1,0:T(8,128)(2,1)S(1)}, bf16[2,128,128]{2,1,0:T(8,128)(2,1)S(1)}, u32[]{:S(2)}, u32[]{:S(2)}) collective-permute-start(bf16[2,128,128]{2,1,0:T(8,128)(2,1)S(1)} %fusion.13.refs_0_), channel_id=1, source_target_pairs={{0,8},{4,12},{8,0},{12,4},{16,24},{20,28},{24,16},{28,20},{1,9},{5... | collective-permute-start | bytes 196616 | tf_op jit(solution)/shard_map/ppermute | solution.py:424
  69.6 8.2 %collective-permute-start.17 = (bf16[2,128,128]{2,1,0:T(8,128)(2,1)S(1)}, bf16[2,128,128]{2,1,0:T(8,128)(2,1)S(1)}, u32[]{:S(2)}, u32[]{:S(2)}) collective-permute-start(bf16[2,128,128]{2,1,0:T(8,128)(2,1)S(1)} %fusion.13.refs_0_), channel_id=1, source_target_pairs={{0,16},{4,20},{8,24},{12,28},{16,0},{20,4},{24,8},{28,12},{1,17},{... | collective-permute-start | bytes 196616 | tf_op jit(solution)/shard_map/ppermute | solution.py:424
  70.8 7.0 %collective-permute-start.18 = (bf16[2,128,128]{2,1,0:T(8,128)(2,1)S(1)}, bf16[2,128,128]{2,1,0:T(8,128)(2,1)S(1)}, u32[]{:S(2)}, u32[]{:S(2)}) collective-permute-start(bf16[2,128,128]{2,1,0:T(8,128)(2,1)S(1)} %fusion.13.refs_0_), channel_id=1, source_target_pairs={{0,24},{4,28},{8,16},{12,20},{16,8},{20,12},{24,0},{28,4},{1,25},{... | collective-permute-start | bytes 196616 | tf_op jit(solution)/shard_map/ppermute | solution.py:424
  77.9 3.4 %copy-start.1 = (bf16[11,128,512]{2,1,0:T(8,128)(2,1)S(1)}, bf16[11,128,512]{2,1,0:T(8,128)(2,1)}, u32[]{:S(2)}) copy-start(bf16[11,128,512]{2,1,0:T(8,128)(2,1)} %copy-done) | copy-start | bytes 4325380
  81.2 1.2 %collective-permute-start.19 = (f32[8,2,384]{2,1,0:T(2,128)S(1)}, f32[8,2,384]{2,1,0:T(2,128)S(1)}, u32[]{:S(2)}, u32[]{:S(2)}) collective-permute-start(f32[8,2,384]{2,1,0:T(2,128)S(1)} %fit_sums.1), channel_id=1, source_target_pairs={{0,4},{4,0},{8,12},{12,8},{16,20},{20,16},{24,28},{28,24},{1,5},{5... | collective-permute-start | bytes 73736 | tf_op jit(solution)/shard_map/ppermute | solution.py:435
  82.5 5.7 %collective-permute-start.20 = (f32[8,2,384]{2,1,0:T(2,128)S(1)}, f32[8,2,384]{2,1,0:T(2,128)S(1)}, u32[]{:S(2)}, u32[]{:S(2)}) collective-permute-start(f32[8,2,384]{2,1,0:T(2,128)S(1)} %add.64.refs_0_), channel_id=1, source_target_pairs={{0,8},{4,12},{8,0},{12,4},{16,24},{20,28},{24,16},{28,20},{1,9},{5... | collective-permute-start | bytes 73736 | tf_op jit(solution)/shard_map/ppermute | solution.py:437
  83.7 22.4 %collective-permute-start.9 = (bf16[8,128,128]{2,1,0:T(8,128)(2,1)S(1)}, bf16[8,128,128]{2,1,0:T(8,128)(2,1)S(1)}, u32[]{:S(2)}, u32[]{:S(2)}) collective-permute-start(bf16[8,128,128]{2,1,0:T(8,128)(2,1)S(1)} %get-tuple-element.64), channel_id=1, source_target_pairs={{1,0},{2,3},{5,4},{6,7},{9,8},{10,11},{13,12},{14,15},{17,16},{18,... | collective-permute-start | bytes 786440 | tf_op jit(solution)/shard_map/ppermute | solution.py:407
  85.0 21.1 %collective-permute-start.10 = (bf16[8,128,128]{2,1,0:T(8,128)(2,1)S(1)}, bf16[8,128,128]{2,1,0:T(8,128)(2,1)S(1)}, u32[]{:S(2)}, u32[]{:S(2)}) collective-permute-start(bf16[8,128,128]{2,1,0:T(8,128)(2,1)S(1)} %get-tuple-element.63), channel_id=1, source_target_pairs={{1,3},{2,0},{5,7},{6,4},{9,11},{10,8},{13,15},{14,12},{17,19},{18,... | collective-permute-start | bytes 786440 | tf_op jit(solution)/shard_map/ppermute | solution.py:407
  86.3 19.8 %collective-permute-start.11 = (bf16[8,128,128]{2,1,0:T(8,128)(2,1)S(1)}, bf16[8,128,128]{2,1,0:T(8,128)(2,1)S(1)}, u32[]{:S(2)}, u32[]{:S(2)}) collective-permute-start(bf16[8,128,128]{2,1,0:T(8,128)(2,1)S(1)} %get-tuple-element.62), channel_id=1, source_target_pairs={{1,2},{2,1},{5,6},{6,5},{9,10},{10,9},{13,14},{14,13},{17,18},{18,... | collective-permute-start | bytes 786440 | tf_op jit(solution)/shard_map/ppermute | solution.py:407
  86.9 5.0 %collective-permute-start.21 = (f32[8,2,384]{2,1,0:T(2,128)S(1)}, f32[8,2,384]{2,1,0:T(2,128)S(1)}, u32[]{:S(2)}, u32[]{:S(2)}) collective-permute-start(f32[8,2,384]{2,1,0:T(2,128)S(1)} %add.64.refs_0_), channel_id=1, source_target_pairs={{0,16},{4,20},{8,24},{12,28},{16,0},{20,4},{24,8},{28,12},{1,17},{... | collective-permute-start | bytes 73736 | tf_op jit(solution)/shard_map/ppermute | solution.py:437
  88.2 4.7 %collective-permute-start.22 = (f32[8,2,384]{2,1,0:T(2,128)S(1)}, f32[8,2,384]{2,1,0:T(2,128)S(1)}, u32[]{:S(2)}, u32[]{:S(2)}) collective-permute-start(f32[8,2,384]{2,1,0:T(2,128)S(1)} %add.64.refs_0_), channel_id=1, source_target_pairs={{0,24},{4,28},{8,16},{12,20},{16,8},{20,12},{24,0},{28,4},{1,25},{... | collective-permute-start | bytes 73736 | tf_op jit(solution)/shard_map/ppermute | solution.py:437
  93.7 8.1 %collective-permute-start.23 = (f32[2,384]{1,0:T(2,128)S(1)}, f32[2,384]{1,0:T(2,128)S(1)}, u32[]{:S(2)}, u32[]{:S(2)}) collective-permute-start(f32[2,384]{1,0:T(2,128)S(1)} %metric.1), channel_id=1, source_target_pairs={{0,3},{1,2},{2,1},{3,0},{4,7},{5,6},{6,5},{7,4},{8,11},{9,10},{10,... | collective-permute-start | bytes 9224 | tf_op jit(solution)/shard_map/ppermute | solution.py:449
  95.0 8.9 %collective-permute-start.24 = (f32[2,384]{1,0:T(2,128)S(1)}, f32[2,384]{1,0:T(2,128)S(1)}, u32[]{:S(2)}, u32[]{:S(2)}) collective-permute-start(f32[2,384]{1,0:T(2,128)S(1)} %metric.1), channel_id=1, source_target_pairs={{0,2},{1,3},{2,0},{3,1},{4,6},{5,7},{6,4},{7,5},{8,10},{9,11},{10,... | collective-permute-start | bytes 9224 | tf_op jit(solution)/shard_map/ppermute | solution.py:449
  101.8 3.7 %collective-permute-start.25 = (f32[2,384]{1,0:T(2,128)S(1)}, f32[2,384]{1,0:T(2,128)S(1)}, u32[]{:S(2)}, u32[]{:S(2)}) collective-permute-start(f32[2,384]{1,0:T(2,128)S(1)} %metric.1), channel_id=1, source_target_pairs={{0,1},{1,0},{2,3},{3,2},{4,5},{5,4},{6,7},{7,6},{8,9},{9,8},{10,11... | collective-permute-start | bytes 9224 | tf_op jit(solution)/shard_map/ppermute | solution.py:449

commit v4 on v3

--- a/solution.py
+++ b/solution.py
@@ -255,8 +255,10 @@
     middle = (my_slot == side_a) | (my_slot == side_b)
     zero_half = jnp.zeros((), jnp.bfloat16)
     up_rows, down_rows = 2 * half, 2 * half - 2
-    forward = [(i, i + 1) for i in range(aux_count - 1)]
-    backward = [(i + 1, i) for i in range(aux_count - 1)]
+    forward = [
+        (i * slots + side, (i + 1) * slots + side) for i in range(aux_count - 1) for side in (side_a, side_b)
+    ]
+    backward = [(target, source) for source, target in forward]
 
     near, far = pl.pallas_call(
         pack_kernel,
@@ -281,8 +283,8 @@
         high = [part[:down_rows] for _, _, rows in pieces for part in split(rows)]
         if extra is not None:
             low, high = low + [extra], high + [extra]
-        low = lax.ppermute(jnp.concatenate(low, 0), "aux", forward)
-        high = lax.ppermute(jnp.concatenate(high, 0), "aux", backward)
+        low = lax.ppermute(jnp.concatenate(low, 0), ("aux", "orb"), forward)
+        high = lax.ppermute(jnp.concatenate(high, 0), ("aux", "orb"), backward)
         for source, size, row in ((low, up_rows, 0), (high, down_rows, up_rows + count_rows)):
             for index, (kind, distance, _) in enumerate(pieces):
                 for field in range(2):

time: 108 us -> 108 us (level)
  starting transfers between devices: 52.9 us -> 44 us
  waiting for transfers between devices: 28.4 us -> 37.3 us
    ppermute x6, waiting for transfers between devices: 8.01 us -> 17 us  [scatter(): got.append(lax.ppermute(blocks[step], 'orb', pairs))]
    ppermute x6, starting transfers between devices: 13 us -> 4.07 us  [the longest x3 2.05 us: stage_rims(): low = lax.ppermute(jnp.concatenate(low, 0), ('aux', 'orb'), forward)]
    ppermute x6, waiting for transfers between devices: 3.09 us -> 0.02 us  [the longest x3 0.01 us: stage_rims(): high = lax.ppermute(jnp.concatenate(high, 0), ('aux', 'orb'), backward)]
    ppermute x1, waiting for transfers between devices: 13.2 us -> 16.2 us  [on_device(): lax.ppermute(near, 'orb', [(side_a - distance, side_a), (side_b + distanc...]
  transfers between devices with their start and end apart: 26 -> 26, of which waited for: 8 -> 7; matrix products, arithmetic and copies ran while one was open for 3% -> 3% of each run, Pallas kernels for 9% -> 9%
where the time goes in v4:
time: 108 us; the launch traced here: 107 us
  starting transfers between devices  44 us (41%)
  waiting for transfers between devices  37.3 us (35%)
  Pallas kernels  15.2 us (14%)
  local copies, waits for them, and re-layouts  4.75 us (4%)
  other arithmetic  3.94 us (4%)
  between operations  1.86 us (2%)
    ppermute x6, waiting for transfers between devices, scatter(): got.append(lax.ppermute(blocks[step], 'orb', pairs))  17 us
    ppermute x1, waiting for transfers between devices, on_device(): lax.ppermute(near, 'orb', [(side_a - distance, side_a), (side_b + distanc...  16.2 us
    ppermute x3, starting transfers between devices, on_device(): got[distance] = lax.ppermute(part, 'orb', swap_pairs(slots, distance))  10.2 us
    ppermute x2, starting transfers between devices, on_device(): lax.ppermute(far, 'orb', [(side_a - distance, side_b), (side_b + distance...  8.39 us
    pallas_call x3, Pallas kernels, preload(): pl.pallas_call(functools.partial(preload_kernel, parts), out_shape=shapes...  8.13 us
    ppermute x6, starting transfers between devices, scatter(): got.append(lax.ppermute(blocks[step], 'orb', pairs))  6.5 us
    ppermute x3, starting transfers between devices, on_device(): lax.ppermute(fit_own, 'aux', swap_pairs(aux_count, distance))  5.67 us
    unnamed x17, local copies, waits for them, and re-layouts  4.46 us
  transfers between devices with their start and end apart: 26, of which 7 were waited for; matrix products, arithmetic and copies ran while one was open for 3% of the time, Pallas kernels for 9%

profile of v4, /device:TPU:0, one launch (start us, length us, event | category | flops | bytes accessed | tf_op | source)
XLA Modules:
  0.0 107.0 jit_solution(15405447175901937683)
XLA Ops:
  0.6 1.4 %pack.1 = (bf16[16,128,128]{2,1,0:T(8,128)(2,1)S(1)}, bf16[16,128,128]{2,1,0:T(8,128)(2,1)S(1)}) custom-call(s32[4,8]{1,0:T(4,128)} %bitcast.75, bf16[8,1,128,128]{3,2,1,0:T(8,128)(2,1)} %density_in.1, bf16[2,8,1,128,128]{4,3,2,1,0:T(8,128)(2,1)} %field_terms.1), custom_call_target="tpu_custom_call" | custom-call | tf_op jit(solution)/shard_map/pack/pallas_call | solution.py:263
  2.0 0.7 collective-permute-start.3
  2.7 7.7 %collective-permute-start.6 = (bf16[16,128,128]{2,1,0:T(8,128)(2,1)S(1)}, bf16[16,128,128]{2,1,0:T(8,128)(2,1)S(1)}, u32[]{:S(2)}, u32[]{:S(2)}) collective-permute-start(bf16[16,128,128]{2,1,0:T(8,128)(2,1)S(1)} %get-tuple-element.29), channel_id=1, source_target_pairs={{0,2},{3,1},{4,6},{7,5},{8,10},{11,9},{12,14},{15,13},{16,18},{19,... | collective-permute-start | bytes 1572872 | tf_op jit(solution)/shard_map/ppermute | solution.py:308
  10.4 1.4 %collective-permute-start.2 = (bf16[16,128,128]{2,1,0:T(8,128)(2,1)S(1)}, bf16[16,128,128]{2,1,0:T(8,128)(2,1)S(1)}, u32[]{:S(2)}, u32[]{:S(2)}) collective-permute-start(bf16[16,128,128]{2,1,0:T(8,128)(2,1)S(1)} %get-tuple-element.28.refs_2_), channel_id=1, source_target_pairs={{0,1},{3,2},{4,5},{7,6},{8,9},{11,10},{12,13},{15,14},{16,17},{19,... | collective-permute-start | bytes 1572872 | tf_op jit(solution)/shard_map/ppermute | solution.py:307
  11.8 0.7 convert_element_type.31
  12.6 0.7 collective-permute-start.1
  13.3 0.7 collective-permute-start
  15.3 0.8 copy.20
  16.2 16.2 %collective-permute-done.2.refs_5_ = bf16[16,128,128]{2,1,0:T(8,128)(2,1)S(1)} collective-permute-done((bf16[16,128,128]{2,1,0:T(8,128)(2,1)S(1)}, bf16[16,128,128]{2,1,0:T(8,128)(2,1)S(1)}, u32[]{:S(2)}, u32[]{:S(2)}) %collective-permute-start.2) | collective-permute-done | bytes 524320 | tf_op jit(solution)/shard_map/ppermute | solution.py:307
  32.5 0.7 collective-permute-start.4
  33.3 0.7 collective-permute-start.5
  34.1 0.7 collective-permute-start.7
  34.8 0.7 collective-permute-start.8
  35.7 1.0 copy-done.3
  36.6 0.9 copy-done.5
  37.5 0.9 mid_products.1
  38.4 1.1 %copy-done = bf16[11,128,512]{2,1,0:T(8,128)(2,1)} copy-done((bf16[11,128,512]{2,1,0:T(8,128)(2,1)}, bf16[11,128,512]{2,1,0:T(8,128)(2,1)S(1)}, u32[]{:S(2)}) %copy-start) | copy-done | bytes 1441816
  39.6 0.7 copy-done.6
  40.2 1.3 %collective-permute-start.12 = (bf16[128,128]{1,0:T(8,128)(2,1)S(1)}, bf16[128,128]{1,0:T(8,128)(2,1)S(1)}, u32[]{:S(2)}, u32[]{:S(2)}) collective-permute-start(bf16[128,128]{1,0:T(8,128)(2,1)S(1)} %get-tuple-element.85), channel_id=1, source_target_pairs={{1,0},{2,3},{5,4},{6,7},{9,8},{10,11},{13,12},{14,15},{17,16},{18,... | collective-permute-start | bytes 98312 | tf_op jit(solution)/shard_map/ppermute | solution.py:409
  41.5 1.3 %collective-permute-start.13 = (bf16[128,128]{1,0:T(8,128)(2,1)S(1)}, bf16[128,128]{1,0:T(8,128)(2,1)S(1)}, u32[]{:S(2)}, u32[]{:S(2)}) collective-permute-start(bf16[128,128]{1,0:T(8,128)(2,1)S(1)} %get-tuple-element.84), channel_id=1, source_target_pairs={{1,3},{2,0},{5,7},{6,4},{9,11},{10,8},{13,15},{14,12},{17,19},{18,... | collective-permute-start | bytes 98312 | tf_op jit(solution)/shard_map/ppermute | solution.py:409
  42.8 0.7 collective-permute-start.14
  43.6 14.7 %collective-permute-done.12 = bf16[128,128]{1,0:T(8,128)(2,1)S(1)} collective-permute-done((bf16[128,128]{1,0:T(8,128)(2,1)S(1)}, bf16[128,128]{1,0:T(8,128)(2,1)S(1)}, u32[]{:S(2)}, u32[]{:S(2)}) %collective-permute-start.12) | collective-permute-done | bytes 32800 | tf_op jit(solution)/shard_map/ppermute | solution.py:409
  58.3 2.3 %collective-permute-done.13 = bf16[128,128]{1,0:T(8,128)(2,1)S(1)} collective-permute-done((bf16[128,128]{1,0:T(8,128)(2,1)S(1)}, bf16[128,128]{1,0:T(8,128)(2,1)S(1)}, u32[]{:S(2)}, u32[]{:S(2)}) %collective-permute-start.13) | collective-permute-done | bytes 32800 | tf_op jit(solution)/shard_map/ppermute | solution.py:409
  60.5 0.8 fusion.2
  61.3 4.1 %collective-permute-start.15 = (bf16[2,128,128]{2,1,0:T(8,128)(2,1)S(1)}, bf16[2,128,128]{2,1,0:T(8,128)(2,1)S(1)}, u32[]{:S(2)}, u32[]{:S(2)}) collective-permute-start(bf16[2,128,128]{2,1,0:T(8,128)(2,1)S(1)} %pad_maximum_fusion.6), channel_id=1, source_target_pairs={{0,4},{4,0},{8,12},{12,8},{16,20},{20,16},{24,28},{28,24},{1,5},{5... | collective-permute-start | bytes 196616 | tf_op jit(solution)/shard_map/ppermute | solution.py:424
  65.5 0.9 collective-permute-done.15
  66.4 3.2 %collective-permute-start.16 = (bf16[2,128,128]{2,1,0:T(8,128)(2,1)S(1)}, bf16[2,128,128]{2,1,0:T(8,128)(2,1)S(1)}, u32[]{:S(2)}, u32[]{:S(2)}) collective-permute-start(bf16[2,128,128]{2,1,0:T(8,128)(2,1)S(1)} %fusion.13.refs_0_), channel_id=1, source_target_pairs={{0,8},{4,12},{8,0},{12,4},{16,24},{20,28},{24,16},{28,20},{1,9},{5... | collective-permute-start | bytes 196616 | tf_op jit(solution)/shard_map/ppermute | solution.py:426
  69.6 1.2 %collective-permute-start.17 = (bf16[2,128,128]{2,1,0:T(8,128)(2,1)S(1)}, bf16[2,128,128]{2,1,0:T(8,128)(2,1)S(1)}, u32[]{:S(2)}, u32[]{:S(2)}) collective-permute-start(bf16[2,128,128]{2,1,0:T(8,128)(2,1)S(1)} %fusion.13.refs_0_), channel_id=1, source_target_pairs={{0,16},{4,20},{8,24},{12,28},{16,0},{20,4},{24,8},{28,12},{1,17},{... | collective-permute-start | bytes 196616 | tf_op jit(solution)/shard_map/ppermute | solution.py:426
  70.8 1.2 %collective-permute-start.18 = (bf16[2,128,128]{2,1,0:T(8,128)(2,1)S(1)}, bf16[2,128,128]{2,1,0:T(8,128)(2,1)S(1)}, u32[]{:S(2)}, u32[]{:S(2)}) collective-permute-start(bf16[2,128,128]{2,1,0:T(8,128)(2,1)S(1)} %fusion.13.refs_0_), channel_id=1, source_target_pairs={{0,24},{4,28},{8,16},{12,20},{16,8},{20,12},{24,0},{28,4},{1,25},{... | collective-permute-start | bytes 196616 | tf_op jit(solution)/shard_map/ppermute | solution.py:426
  72.1 3.5 %shard_map.77.refs_4_ = bf16[256,16384]{1,0:T(8,128)(2,1)S(1)} custom-call(bf16[384,16384]{1,0:T(8,128)(2,1)} %bitcast.72), custom_call_target="tpu_custom_call" | custom-call | tf_op jit(solution)/shard_map/pallas_call | solution.py:329
  75.6 2.3 %shard_map.78.refs_5_ = bf16[256,8192]{1,0:T(8,128)(2,1)S(1)} custom-call(bf16[384,16384]{1,0:T(8,128)(2,1)} %bitcast.73), custom_call_target="tpu_custom_call" | custom-call | tf_op jit(solution)/shard_map/pallas_call | solution.py:329
  77.9 3.4 %fit_sums.1 = f32[8,2,384]{2,1,0:T(2,128)S(1)} custom-call(s32[1]{0:T(128)} %bitcast.17.place, bf16[2,128,128]{2,1,0:T(8,128)(2,1)S(1)} %fusion.13.refs_0_, bf16[2,128,128]{2,1,0:T(8,128)(2,1)S(1)} %collective-permute-done.16.refs_1_, bf16[2,128,128]{2,1,0:T(8,128)(2,1)S(1)} %collective-permute-done.17.refs_2_, ...), custom_call_target="tpu_custom_call" | custom-call | tf_op jit(solution)/shard_map/fit_sums/pallas_call | solution.py:429
  81.3 0.7 mid_second.1
  82.5 1.1 %collective-permute-start.20 = (f32[8,2,384]{2,1,0:T(2,128)S(1)}, f32[8,2,384]{2,1,0:T(2,128)S(1)}, u32[]{:S(2)}, u32[]{:S(2)}) collective-permute-start(f32[8,2,384]{2,1,0:T(2,128)S(1)} %add.64.refs_0_), channel_id=1, source_target_pairs={{0,8},{4,12},{8,0},{12,4},{16,24},{20,28},{24,16},{28,20},{1,9},{5... | collective-permute-start | bytes 73736 | tf_op jit(solution)/shard_map/ppermute | solution.py:439
  83.7 1.3 %collective-permute-start.9 = (bf16[8,128,128]{2,1,0:T(8,128)(2,1)S(1)}, bf16[8,128,128]{2,1,0:T(8,128)(2,1)S(1)}, u32[]{:S(2)}, u32[]{:S(2)}) collective-permute-start(bf16[8,128,128]{2,1,0:T(8,128)(2,1)S(1)} %get-tuple-element.64), channel_id=1, source_target_pairs={{1,0},{2,3},{5,4},{6,7},{9,8},{10,11},{13,12},{14,15},{17,16},{18,... | collective-permute-start | bytes 786440 | tf_op jit(solution)/shard_map/ppermute | solution.py:409
  85.0 1.3 %collective-permute-start.10 = (bf16[8,128,128]{2,1,0:T(8,128)(2,1)S(1)}, bf16[8,128,128]{2,1,0:T(8,128)(2,1)S(1)}, u32[]{:S(2)}, u32[]{:S(2)}) collective-permute-start(bf16[8,128,128]{2,1,0:T(8,128)(2,1)S(1)} %get-tuple-element.63), channel_id=1, source_target_pairs={{1,3},{2,0},{5,7},{6,4},{9,11},{10,8},{13,15},{14,12},{17,19},{18,... | collective-permute-start | bytes 786440 | tf_op jit(solution)/shard_map/ppermute | solution.py:409
  86.3 0.7 collective-permute-start.11
  86.9 1.3 %collective-permute-start.21 = (f32[8,2,384]{2,1,0:T(2,128)S(1)}, f32[8,2,384]{2,1,0:T(2,128)S(1)}, u32[]{:S(2)}, u32[]{:S(2)}) collective-permute-start(f32[8,2,384]{2,1,0:T(2,128)S(1)} %add.64.refs_0_), channel_id=1, source_target_pairs={{0,16},{4,20},{8,24},{12,28},{16,0},{20,4},{24,8},{28,12},{1,17},{... | collective-permute-start | bytes 73736 | tf_op jit(solution)/shard_map/ppermute | solution.py:439
  88.2 1.3 %collective-permute-start.22 = (f32[8,2,384]{2,1,0:T(2,128)S(1)}, f32[8,2,384]{2,1,0:T(2,128)S(1)}, u32[]{:S(2)}, u32[]{:S(2)}) collective-permute-start(f32[8,2,384]{2,1,0:T(2,128)S(1)} %add.64.refs_0_), channel_id=1, source_target_pairs={{0,24},{4,28},{8,16},{12,20},{16,8},{20,12},{24,0},{28,4},{1,25},{... | collective-permute-start | bytes 73736 | tf_op jit(solution)/shard_map/ppermute | solution.py:439
  89.5 2.4 %shard_map.79.refs_4_ = f32[384,3072]{1,0:T(8,128)S(1)} custom-call(f32[384,3072]{1,0:T(8,128)} %bitcast.74), custom_call_target="tpu_custom_call" | custom-call | tf_op jit(solution)/shard_map/pallas_call | solution.py:329
  91.9 1.0 collective-permute-done.22.refs_3_
  93.0 0.8 metric.1
  93.7 1.3 %collective-permute-start.23 = (f32[2,384]{1,0:T(2,128)S(1)}, f32[2,384]{1,0:T(2,128)S(1)}, u32[]{:S(2)}, u32[]{:S(2)}) collective-permute-start(f32[2,384]{1,0:T(2,128)S(1)} %metric.1), channel_id=1, source_target_pairs={{0,3},{1,2},{2,1},{3,0},{4,7},{5,6},{6,5},{7,4},{8,11},{9,10},{10,... | collective-permute-start | bytes 9224 | tf_op jit(solution)/shard_map/ppermute | solution.py:451
  95.0 6.7 %collective-permute-start.24 = (f32[2,384]{1,0:T(2,128)S(1)}, f32[2,384]{1,0:T(2,128)S(1)}, u32[]{:S(2)}, u32[]{:S(2)}) collective-permute-start(f32[2,384]{1,0:T(2,128)S(1)} %metric.1), channel_id=1, source_target_pairs={{0,2},{1,3},{2,0},{3,1},{4,6},{5,7},{6,4},{7,5},{8,10},{9,11},{10,... | collective-permute-start | bytes 9224 | tf_op jit(solution)/shard_map/ppermute | solution.py:451
  101.8 2.1 %collective-permute-start.25 = (f32[2,384]{1,0:T(2,128)S(1)}, f32[2,384]{1,0:T(2,128)S(1)}, u32[]{:S(2)}, u32[]{:S(2)}) collective-permute-start(f32[2,384]{1,0:T(2,128)S(1)} %metric.1), channel_id=1, source_target_pairs={{0,1},{1,0},{2,3},{3,2},{4,5},{5,4},{6,7},{7,6},{8,9},{9,8},{10,11... | collective-permute-start | bytes 9224 | tf_op jit(solution)/shard_map/ppermute | solution.py:451
  103.9 1.6 %collective-permute-done.25 = f32[2,384]{1,0:T(2,128)S(1)} collective-permute-done((f32[2,384]{1,0:T(2,128)S(1)}, f32[2,384]{1,0:T(2,128)S(1)}, u32[]{:S(2)}, u32[]{:S(2)}) %collective-permute-start.25) | collective-permute-done | bytes 3104 | tf_op jit(solution)/shard_map/ppermute | solution.py:451
  105.5 0.6 add_bitcast_fusion
  106.2 0.8 maximum_bitcast_fusion
  (60 shorter events, 1.9 us)
Async XLA Ops:
  2.0 14.2 %collective-permute-start.3 = (bf16[16,128,128]{2,1,0:T(8,128)(2,1)S(1)}, bf16[16,128,128]{2,1,0:T(8,128)(2,1)S(1)}, u32[]{:S(2)}, u32[]{:S(2)}) collective-permute-start(bf16[16,128,128]{2,1,0:T(8,128)(2,1)S(1)} %get-tuple-element.29), channel_id=1, source_target_pairs={{1,2},{2,1},{5,6},{6,5},{9,10},{10,9},{13,14},{14,13},{17,18},{18,... | collective-permute-start | bytes 1572872 | tf_op jit(solution)/shard_map/ppermute | solution.py:308
  2.7 31.3 %collective-permute-start.6 = (bf16[16,128,128]{2,1,0:T(8,128)(2,1)S(1)}, bf16[16,128,128]{2,1,0:T(8,128)(2,1)S(1)}, u32[]{:S(2)}, u32[]{:S(2)}) collective-permute-start(bf16[16,128,128]{2,1,0:T(8,128)(2,1)S(1)} %get-tuple-element.29), channel_id=1, source_target_pairs={{0,2},{3,1},{4,6},{7,5},{8,10},{11,9},{12,14},{15,13},{16,18},{19,... | collective-permute-start | bytes 1572872 | tf_op jit(solution)/shard_map/ppermute | solution.py:308
  10.4 22.1 %collective-permute-start.2 = (bf16[16,128,128]{2,1,0:T(8,128)(2,1)S(1)}, bf16[16,128,128]{2,1,0:T(8,128)(2,1)S(1)}, u32[]{:S(2)}, u32[]{:S(2)}) collective-permute-start(bf16[16,128,128]{2,1,0:T(8,128)(2,1)S(1)} %get-tuple-element.28.refs_2_), channel_id=1, source_target_pairs={{0,1},{3,2},{4,5},{7,6},{8,9},{11,10},{12,13},{15,14},{16,17},{19,... | collective-permute-start | bytes 1572872 | tf_op jit(solution)/shard_map/ppermute | solution.py:307
  12.6 3.5 %collective-permute-start.1 = (bf16[5,128,128]{2,1,0:T(8,128)(2,1)S(1)}, bf16[5,128,128]{2,1,0:T(8,128)(2,1)S(1)}, u32[]{:S(2)}, u32[]{:S(2)}) collective-permute-start(bf16[5,128,128]{2,1,0:T(8,128)(2,1)S(1)} %pad_maximum_fusion.4), channel_id=1, source_target_pairs={{5,1},{6,2},{9,5},{10,6},{13,9},{14,10},{17,13},{18,14},{21,17},{2... | collective-permute-start | bytes 491528 | tf_op jit(solution)/shard_map/ppermute | solution.py:287
  13.3 2.8 %collective-permute-start = (bf16[9,128,128]{2,1,0:T(8,128)(2,1)S(1)}, bf16[9,128,128]{2,1,0:T(8,128)(2,1)S(1)}, u32[]{:S(2)}, u32[]{:S(2)}) collective-permute-start(bf16[9,128,128]{2,1,0:T(8,128)(2,1)S(1)} %pad_maximum_fusion.1), channel_id=1, source_target_pairs={{1,5},{2,6},{5,9},{6,10},{9,13},{10,14},{13,17},{14,18},{17,21},{1... | collective-permute-start | bytes 884744 | tf_op jit(solution)/shard_map/ppermute | solution.py:286
  16.0 19.4 %copy-start.7 = (s32[11]{0:T(128)S(1)}, s32[11]{0:T(128)}, u32[]{:S(2)}) copy-start(s32[11]{0:T(128)} %iota_add_fusion) | copy-start | bytes 136
  16.1 19.5 %copy-start.4 = (bf16[5,128,128]{2,1,0:T(8,128)(2,1)}, bf16[5,128,128]{2,1,0:T(8,128)(2,1)S(1)}, u32[]{:S(2)}) copy-start(bf16[5,128,128]{2,1,0:T(8,128)(2,1)S(1)} %collective-permute-done.1.refs_1_) | copy-start | bytes 491524
  16.1 19.5 %copy-start.2 = (bf16[9,128,128]{2,1,0:T(8,128)(2,1)}, bf16[9,128,128]{2,1,0:T(8,128)(2,1)S(1)}, u32[]{:S(2)}) copy-start(bf16[9,128,128]{2,1,0:T(8,128)(2,1)S(1)} %collective-permute-done.refs_0_) | copy-start | bytes 884740
  32.5 3.1 %collective-permute-start.4 = (bf16[16,128,128]{2,1,0:T(8,128)(2,1)S(1)}, bf16[16,128,128]{2,1,0:T(8,128)(2,1)S(1)}, u32[]{:S(2)}, u32[]{:S(2)}) collective-permute-start(bf16[16,128,128]{2,1,0:T(8,128)(2,1)S(1)} %pad_maximum_fusion), channel_id=1, source_target_pairs={{1,5},{2,6},{5,9},{6,10},{9,13},{10,14},{13,17},{14,18},{17,21},{1... | collective-permute-start | bytes 1572872 | tf_op jit(solution)/shard_map/ppermute | solution.py:286
  33.3 2.3 %collective-permute-start.5 = (bf16[8,128,128]{2,1,0:T(8,128)(2,1)S(1)}, bf16[8,128,128]{2,1,0:T(8,128)(2,1)S(1)}, u32[]{:S(2)}, u32[]{:S(2)}) collective-permute-start(bf16[8,128,128]{2,1,0:T(8,128)(2,1)S(1)} %pad_maximum_fusion.2), channel_id=1, source_target_pairs={{5,1},{6,2},{9,5},{10,6},{13,9},{14,10},{17,13},{18,14},{21,17},{2... | collective-permute-start | bytes 786440 | tf_op jit(solution)/shard_map/ppermute | solution.py:287
  34.1 1.5 %collective-permute-start.7 = (bf16[8,128,128]{2,1,0:T(8,128)(2,1)S(1)}, bf16[8,128,128]{2,1,0:T(8,128)(2,1)S(1)}, u32[]{:S(2)}, u32[]{:S(2)}) collective-permute-start(bf16[8,128,128]{2,1,0:T(8,128)(2,1)S(1)} %pad_maximum_fusion.3), channel_id=1, source_target_pairs={{1,5},{2,6},{5,9},{6,10},{9,13},{10,14},{13,17},{14,18},{17,21},{1... | collective-permute-start | bytes 786440 | tf_op jit(solution)/shard_map/ppermute | solution.py:286
  34.8 0.8 collective-permute-start.8
  35.6 1.0 copy-start.3
  36.6 0.9 copy-start.5
  38.4 1.2 %copy-start = (bf16[11,128,512]{2,1,0:T(8,128)(2,1)}, bf16[11,128,512]{2,1,0:T(8,128)(2,1)S(1)}, u32[]{:S(2)}) copy-start(bf16[11,128,512]{2,1,0:T(8,128)(2,1)S(1)} %get-tuple-element.31.order) | copy-start | bytes 4325380
  39.6 0.7 copy-start.6
  40.2 18.0 %collective-permute-start.12 = (bf16[128,128]{1,0:T(8,128)(2,1)S(1)}, bf16[128,128]{1,0:T(8,128)(2,1)S(1)}, u32[]{:S(2)}, u32[]{:S(2)}) collective-permute-start(bf16[128,128]{1,0:T(8,128)(2,1)S(1)} %get-tuple-element.85), channel_id=1, source_target_pairs={{1,0},{2,3},{5,4},{6,7},{9,8},{10,11},{13,12},{14,15},{17,16},{18,... | collective-permute-start | bytes 98312 | tf_op jit(solution)/shard_map/ppermute | solution.py:409
  41.5 19.0 %collective-permute-start.13 = (bf16[128,128]{1,0:T(8,128)(2,1)S(1)}, bf16[128,128]{1,0:T(8,128)(2,1)S(1)}, u32[]{:S(2)}, u32[]{:S(2)}) collective-permute-start(bf16[128,128]{1,0:T(8,128)(2,1)S(1)} %get-tuple-element.84), channel_id=1, source_target_pairs={{1,3},{2,0},{5,7},{6,4},{9,11},{10,8},{13,15},{14,12},{17,19},{18,... | collective-permute-start | bytes 98312 | tf_op jit(solution)/shard_map/ppermute | solution.py:409
  42.8 17.7 %collective-permute-start.14 = (bf16[128,128]{1,0:T(8,128)(2,1)S(1)}, bf16[128,128]{1,0:T(8,128)(2,1)S(1)}, u32[]{:S(2)}, u32[]{:S(2)}) collective-permute-start(bf16[128,128]{1,0:T(8,128)(2,1)S(1)} %get-tuple-element.83), channel_id=1, source_target_pairs={{1,2},{2,1},{5,6},{6,5},{9,10},{10,9},{13,14},{14,13},{17,18},{18,... | collective-permute-start | bytes 98312 | tf_op jit(solution)/shard_map/ppermute | solution.py:409
  61.3 5.0 %collective-permute-start.15 = (bf16[2,128,128]{2,1,0:T(8,128)(2,1)S(1)}, bf16[2,128,128]{2,1,0:T(8,128)(2,1)S(1)}, u32[]{:S(2)}, u32[]{:S(2)}) collective-permute-start(bf16[2,128,128]{2,1,0:T(8,128)(2,1)S(1)} %pad_maximum_fusion.6), channel_id=1, source_target_pairs={{0,4},{4,0},{8,12},{12,8},{16,20},{20,16},{24,28},{28,24},{1,5},{5... | collective-permute-start | bytes 196616 | tf_op jit(solution)/shard_map/ppermute | solution.py:424
  66.4 11.4 %collective-permute-start.16 = (bf16[2,128,128]{2,1,0:T(8,128)(2,1)S(1)}, bf16[2,128,128]{2,1,0:T(8,128)(2,1)S(1)}, u32[]{:S(2)}, u32[]{:S(2)}) collective-permute-start(bf16[2,128,128]{2,1,0:T(8,128)(2,1)S(1)} %fusion.13.refs_0_), channel_id=1, source_target_pairs={{0,8},{4,12},{8,0},{12,4},{16,24},{20,28},{24,16},{28,20},{1,9},{5... | collective-permute-start | bytes 196616 | tf_op jit(solution)/shard_map/ppermute | solution.py:426
  69.6 8.2 %collective-permute-start.17 = (bf16[2,128,128]{2,1,0:T(8,128)(2,1)S(1)}, bf16[2,128,128]{2,1,0:T(8,128)(2,1)S(1)}, u32[]{:S(2)}, u32[]{:S(2)}) collective-permute-start(bf16[2,128,128]{2,1,0:T(8,128)(2,1)S(1)} %fusion.13.refs_0_), channel_id=1, source_target_pairs={{0,16},{4,20},{8,24},{12,28},{16,0},{20,4},{24,8},{28,12},{1,17},{... | collective-permute-start | bytes 196616 | tf_op jit(solution)/shard_map/ppermute | solution.py:426
  70.8 7.0 %collective-permute-start.18 = (bf16[2,128,128]{2,1,0:T(8,128)(2,1)S(1)}, bf16[2,128,128]{2,1,0:T(8,128)(2,1)S(1)}, u32[]{:S(2)}, u32[]{:S(2)}) collective-permute-start(bf16[2,128,128]{2,1,0:T(8,128)(2,1)S(1)} %fusion.13.refs_0_), channel_id=1, source_target_pairs={{0,24},{4,28},{8,16},{12,20},{16,8},{20,12},{24,0},{28,4},{1,25},{... | collective-permute-start | bytes 196616 | tf_op jit(solution)/shard_map/ppermute | solution.py:426
  77.9 3.4 %copy-start.1 = (bf16[11,128,512]{2,1,0:T(8,128)(2,1)S(1)}, bf16[11,128,512]{2,1,0:T(8,128)(2,1)}, u32[]{:S(2)}) copy-start(bf16[11,128,512]{2,1,0:T(8,128)(2,1)} %copy-done) | copy-start | bytes 4325380
  81.2 1.2 %collective-permute-start.19 = (f32[8,2,384]{2,1,0:T(2,128)S(1)}, f32[8,2,384]{2,1,0:T(2,128)S(1)}, u32[]{:S(2)}, u32[]{:S(2)}) collective-permute-start(f32[8,2,384]{2,1,0:T(2,128)S(1)} %fit_sums.1), channel_id=1, source_target_pairs={{0,4},{4,0},{8,12},{12,8},{16,20},{20,16},{24,28},{28,24},{1,5},{5... | collective-permute-start | bytes 73736 | tf_op jit(solution)/shard_map/ppermute | solution.py:437
  82.5 5.7 %collective-permute-start.20 = (f32[8,2,384]{2,1,0:T(2,128)S(1)}, f32[8,2,384]{2,1,0:T(2,128)S(1)}, u32[]{:S(2)}, u32[]{:S(2)}) collective-permute-start(f32[8,2,384]{2,1,0:T(2,128)S(1)} %add.64.refs_0_), channel_id=1, source_target_pairs={{0,8},{4,12},{8,0},{12,4},{16,24},{20,28},{24,16},{28,20},{1,9},{5... | collective-permute-start | bytes 73736 | tf_op jit(solution)/shard_map/ppermute | solution.py:439
  83.7 22.4 %collective-permute-start.9 = (bf16[8,128,128]{2,1,0:T(8,128)(2,1)S(1)}, bf16[8,128,128]{2,1,0:T(8,128)(2,1)S(1)}, u32[]{:S(2)}, u32[]{:S(2)}) collective-permute-start(bf16[8,128,128]{2,1,0:T(8,128)(2,1)S(1)} %get-tuple-element.64), channel_id=1, source_target_pairs={{1,0},{2,3},{5,4},{6,7},{9,8},{10,11},{13,12},{14,15},{17,16},{18,... | collective-permute-start | bytes 786440 | tf_op jit(solution)/shard_map/ppermute | solution.py:409
  85.0 21.1 %collective-permute-start.10 = (bf16[8,128,128]{2,1,0:T(8,128)(2,1)S(1)}, bf16[8,128,128]{2,1,0:T(8,128)(2,1)S(1)}, u32[]{:S(2)}, u32[]{:S(2)}) collective-permute-start(bf16[8,128,128]{2,1,0:T(8,128)(2,1)S(1)} %get-tuple-element.63), channel_id=1, source_target_pairs={{1,3},{2,0},{5,7},{6,4},{9,11},{10,8},{13,15},{14,12},{17,19},{18,... | collective-permute-start | bytes 786440 | tf_op jit(solution)/shard_map/ppermute | solution.py:409
  86.3 19.8 %collective-permute-start.11 = (bf16[8,128,128]{2,1,0:T(8,128)(2,1)S(1)}, bf16[8,128,128]{2,1,0:T(8,128)(2,1)S(1)}, u32[]{:S(2)}, u32[]{:S(2)}) collective-permute-start(bf16[8,128,128]{2,1,0:T(8,128)(2,1)S(1)} %get-tuple-element.62), channel_id=1, source_target_pairs={{1,2},{2,1},{5,6},{6,5},{9,10},{10,9},{13,14},{14,13},{17,18},{18,... | collective-permute-start | bytes 786440 | tf_op jit(solution)/shard_map/ppermute | solution.py:409
  86.9 5.0 %collective-permute-start.21 = (f32[8,2,384]{2,1,0:T(2,128)S(1)}, f32[8,2,384]{2,1,0:T(2,128)S(1)}, u32[]{:S(2)}, u32[]{:S(2)}) collective-permute-start(f32[8,2,384]{2,1,0:T(2,128)S(1)} %add.64.refs_0_), channel_id=1, source_target_pairs={{0,16},{4,20},{8,24},{12,28},{16,0},{20,4},{24,8},{28,12},{1,17},{... | collective-permute-start | bytes 73736 | tf_op jit(solution)/shard_map/ppermute | solution.py:439
  88.2 4.7 %collective-permute-start.22 = (f32[8,2,384]{2,1,0:T(2,128)S(1)}, f32[8,2,384]{2,1,0:T(2,128)S(1)}, u32[]{:S(2)}, u32[]{:S(2)}) collective-permute-start(f32[8,2,384]{2,1,0:T(2,128)S(1)} %add.64.refs_0_), channel_id=1, source_target_pairs={{0,24},{4,28},{8,16},{12,20},{16,8},{20,12},{24,0},{28,4},{1,25},{... | collective-permute-start | bytes 73736 | tf_op jit(solution)/shard_map/ppermute | solution.py:439
  93.7 8.1 %collective-permute-start.23 = (f32[2,384]{1,0:T(2,128)S(1)}, f32[2,384]{1,0:T(2,128)S(1)}, u32[]{:S(2)}, u32[]{:S(2)}) collective-permute-start(f32[2,384]{1,0:T(2,128)S(1)} %metric.1), channel_id=1, source_target_pairs={{0,3},{1,2},{2,1},{3,0},{4,7},{5,6},{6,5},{7,4},{8,11},{9,10},{10,... | collective-permute-start | bytes 9224 | tf_op jit(solution)/shard_map/ppermute | solution.py:451
  95.0 8.9 %collective-permute-start.24 = (f32[2,384]{1,0:T(2,128)S(1)}, f32[2,384]{1,0:T(2,128)S(1)}, u32[]{:S(2)}, u32[]{:S(2)}) collective-permute-start(f32[2,384]{1,0:T(2,128)S(1)} %metric.1), channel_id=1, source_target_pairs={{0,2},{1,3},{2,0},{3,1},{4,6},{5,7},{6,4},{7,5},{8,10},{9,11},{10,... | collective-permute-start | bytes 9224 | tf_op jit(solution)/shard_map/ppermute | solution.py:451
  101.8 3.7 %collective-permute-start.25 = (f32[2,384]{1,0:T(2,128)S(1)}, f32[2,384]{1,0:T(2,128)S(1)}, u32[]{:S(2)}, u32[]{:S(2)}) collective-permute-start(f32[2,384]{1,0:T(2,128)S(1)} %metric.1), channel_id=1, source_target_pairs={{0,1},{1,0},{2,3},{3,2},{4,5},{5,4},{6,7},{7,6},{8,9},{9,8},{10,11... | collective-permute-start | bytes 9224 | tf_op jit(solution)/shard_map/ppermute | solution.py:451

commit v5 on v4

--- a/solution.py
+++ b/solution.py
@@ -219,11 +219,11 @@
         start += rows
 
 
-def metric_kernel(*refs):
-    pieces, (metric, out) = refs[:-2], refs[-2:]
-    sums = pieces[0][...]
-    for piece in pieces[1:]:
-        sums = sums + piece[...]
+def metric_kernel(place, *refs):
+    pieces, (metric, out, sums) = refs[:-3], refs[-3:]
+    for index, piece in enumerate(pieces):
+        for core in range(2):
+            sums[jnp.bitwise_xor(place[0], 2 * index) + core] = piece[core]
     groups, fields, width = sums.shape
     lanes = 128
     totals = [jnp.zeros((out.shape[1], lanes), jnp.float32) for _ in range(fields)]
@@ -312,8 +312,9 @@
         band_pattern.astype(jnp.bfloat16), ((0, blk - count_rows), (0, blk - slots))
     )[None]
     low, high = stage_rims([("near", 0, near)], pattern)
-    source, metric_source, *flags = lax.optimization_barrier(
-        [tensor, metric_inv] + [flag for group in wanted for flag in group]
+    core = my_aux.astype(jnp.int32) % 2
+    source, metric_source, core, first_core, *flags = lax.optimization_barrier(
+        [tensor, metric_inv, core[None], (my_aux.astype(jnp.int32) - core)[None]] + [flag for group in wanted for flag in group]
     )
     wanted = [flags[index : index + slots] for index in range(0, len(flags), slots)]
     source, metric_source = (
@@ -428,12 +429,12 @@
 
     sums = pl.pallas_call(
         functools.partial(sums_kernel, len(fit_pieces)),
-        out_shape=jax.ShapeDtypeStruct((aux_count, fields, aux_rows), jnp.float32),
+        out_shape=jax.ShapeDtypeStruct((2, fields, aux_rows), jnp.float32),
         in_specs=[SMEM] + [VMEM] * (len(fit_pieces) + len(integrals)),
         out_specs=VMEM,
         compiler_params=pltpu.CompilerParams(vmem_limit_bytes=8 << 20),
         name="fit_sums",
-    )(my_aux.astype(jnp.int32)[None], *fit_pieces, *integrals)
+    )(core, *fit_pieces, *integrals)
     sums = sums + lax.ppermute(sums, "aux", swap_pairs(aux_count, 1))
     pieces = [sums] + [
         lax.ppermute(sums, "aux", swap_pairs(aux_count, distance)) for distance in range(2, aux_count, 2)
@@ -441,11 +442,12 @@
     part = pl.pallas_call(
         metric_kernel,
         out_shape=jax.ShapeDtypeStruct((fields, metric.shape[0]), jnp.float32),
-        in_specs=[VMEM] * (len(pieces) + 1),
+        in_specs=[SMEM] + [VMEM] * (len(pieces) + 1),
         out_specs=VMEM,
+        scratch_shapes=[pltpu.VMEM((aux_count, fields, aux_rows), jnp.float32)],
         compiler_params=pltpu.CompilerParams(vmem_limit_bytes=8 << 20),
         name="metric",
-    )(*pieces, metric)
+    )(first_core, *pieces, metric)
     got = [part] * slots
     for distance in range(slots - 1, 0, -1):
         got[distance] = lax.ppermute(part, "orb", swap_pairs(slots, distance))

time: 108 us -> 110 us (1.019)
  local copies, waits for them, and re-layouts: 4.75 us -> 6.1 us
    unnamed x17, local copies, waits for them, and re-layouts: 4.46 us -> 5.81 us
  transfers between devices with their start and end apart: 26 -> 26, of which waited for: 7 -> 7; matrix products, arithmetic and copies ran while one was open for 3% -> 3% of each run, Pallas kernels for 9% -> 12%
where the time goes in v5:
time: 110 us; the launch traced here: 109 us
  starting transfers between devices  44.4 us (40%)
  waiting for transfers between devices  37.8 us (34%)
  Pallas kernels  15.3 us (14%)
  local copies, waits for them, and re-layouts  6.1 us (6%)
  other arithmetic  3.93 us (4%)
  between operations  1.86 us (2%)
    ppermute x6, waiting for transfers between devices, scatter(): got.append(lax.ppermute(blocks[step], 'orb', pairs))  17 us
    ppermute x1, waiting for transfers between devices, on_device(): lax.ppermute(near, 'orb', [(side_a - distance, side_a), (side_b + distanc...  16.2 us
    ppermute x3, starting transfers between devices, on_device(): got[distance] = lax.ppermute(part, 'orb', swap_pairs(slots, distance))  10.7 us
    ppermute x2, starting transfers between devices, on_device(): lax.ppermute(far, 'orb', [(side_a - distance, side_b), (side_b + distance...  8.39 us
    pallas_call x3, Pallas kernels, preload(): pl.pallas_call(functools.partial(preload_kernel, parts), out_shape=shapes...  8.13 us
    ppermute x6, starting transfers between devices, scatter(): got.append(lax.ppermute(blocks[step], 'orb', pairs))  6.5 us
    unnamed x17, local copies, waits for them, and re-layouts  5.81 us
    ppermute x3, starting transfers between devices, on_device(): lax.ppermute(fit_own, 'aux', swap_pairs(aux_count, distance))  5.33 us
  transfers between devices with their start and end apart: 26, of which 7 were waited for; matrix products, arithmetic and copies ran while one was open for 3% of the time, Pallas kernels for 12%

profile of v5, /device:TPU:0, one launch (start us, length us, event | category | flops | bytes accessed | tf_op | source)
XLA Modules:
  0.0 109.4 jit_solution(11776557178564402878)
XLA Ops:
  0.6 1.4 %pack.1 = (bf16[16,128,128]{2,1,0:T(8,128)(2,1)S(1)}, bf16[16,128,128]{2,1,0:T(8,128)(2,1)S(1)}) custom-call(s32[4,8]{1,0:T(4,128)} %bitcast.76, bf16[8,1,128,128]{3,2,1,0:T(8,128)(2,1)} %density_in.1, bf16[2,8,1,128,128]{4,3,2,1,0:T(8,128)(2,1)} %field_terms.1), custom_call_target="tpu_custom_call" | custom-call | tf_op jit(solution)/shard_map/pack/pallas_call | solution.py:263
  2.0 0.7 collective-permute-start.3
  2.7 7.7 %collective-permute-start.6 = (bf16[16,128,128]{2,1,0:T(8,128)(2,1)S(1)}, bf16[16,128,128]{2,1,0:T(8,128)(2,1)S(1)}, u32[]{:S(2)}, u32[]{:S(2)}) collective-permute-start(bf16[16,128,128]{2,1,0:T(8,128)(2,1)S(1)} %get-tuple-element.31), channel_id=1, source_target_pairs={{0,2},{3,1},{4,6},{7,5},{8,10},{11,9},{12,14},{15,13},{16,18},{19,... | collective-permute-start | bytes 1572872 | tf_op jit(solution)/shard_map/ppermute | solution.py:308
  10.4 1.4 %collective-permute-start.2 = (bf16[16,128,128]{2,1,0:T(8,128)(2,1)S(1)}, bf16[16,128,128]{2,1,0:T(8,128)(2,1)S(1)}, u32[]{:S(2)}, u32[]{:S(2)}) collective-permute-start(bf16[16,128,128]{2,1,0:T(8,128)(2,1)S(1)} %get-tuple-element.30.refs_2_), channel_id=1, source_target_pairs={{0,1},{3,2},{4,5},{7,6},{8,9},{11,10},{12,13},{15,14},{16,17},{19,... | collective-permute-start | bytes 1572872 | tf_op jit(solution)/shard_map/ppermute | solution.py:307
  11.8 0.7 convert_element_type.31
  12.6 0.7 collective-permute-start.1
  13.3 0.7 collective-permute-start
  15.3 0.8 copy.20
  16.2 16.2 %collective-permute-done.2.refs_5_ = bf16[16,128,128]{2,1,0:T(8,128)(2,1)S(1)} collective-permute-done((bf16[16,128,128]{2,1,0:T(8,128)(2,1)S(1)}, bf16[16,128,128]{2,1,0:T(8,128)(2,1)S(1)}, u32[]{:S(2)}, u32[]{:S(2)}) %collective-permute-start.2) | collective-permute-done | bytes 524320 | tf_op jit(solution)/shard_map/ppermute | solution.py:307
  32.5 0.7 collective-permute-start.4
  33.3 0.7 collective-permute-start.5
  34.1 0.7 collective-permute-start.7
  34.8 0.7 collective-permute-start.8
  35.7 1.0 copy-done.3
  36.6 0.9 copy-done.5
  37.5 0.9 mid_products.1
  38.4 1.1 %copy-done = bf16[11,128,512]{2,1,0:T(8,128)(2,1)} copy-done((bf16[11,128,512]{2,1,0:T(8,128)(2,1)}, bf16[11,128,512]{2,1,0:T(8,128)(2,1)S(1)}, u32[]{:S(2)}) %copy-start) | copy-done | bytes 1441816
  39.6 0.7 copy-done.6
  40.2 1.3 %collective-permute-start.12 = (bf16[128,128]{1,0:T(8,128)(2,1)S(1)}, bf16[128,128]{1,0:T(8,128)(2,1)S(1)}, u32[]{:S(2)}, u32[]{:S(2)}) collective-permute-start(bf16[128,128]{1,0:T(8,128)(2,1)S(1)} %get-tuple-element.89), channel_id=1, source_target_pairs={{1,0},{2,3},{5,4},{6,7},{9,8},{10,11},{13,12},{14,15},{17,16},{18,... | collective-permute-start | bytes 98312 | tf_op jit(solution)/shard_map/ppermute | solution.py:410
  41.5 1.3 %collective-permute-start.13 = (bf16[128,128]{1,0:T(8,128)(2,1)S(1)}, bf16[128,128]{1,0:T(8,128)(2,1)S(1)}, u32[]{:S(2)}, u32[]{:S(2)}) collective-permute-start(bf16[128,128]{1,0:T(8,128)(2,1)S(1)} %get-tuple-element.88), channel_id=1, source_target_pairs={{1,3},{2,0},{5,7},{6,4},{9,11},{10,8},{13,15},{14,12},{17,19},{18,... | collective-permute-start | bytes 98312 | tf_op jit(solution)/shard_map/ppermute | solution.py:410
  42.8 0.7 collective-permute-start.14
  43.6 14.7 %collective-permute-done.12 = bf16[128,128]{1,0:T(8,128)(2,1)S(1)} collective-permute-done((bf16[128,128]{1,0:T(8,128)(2,1)S(1)}, bf16[128,128]{1,0:T(8,128)(2,1)S(1)}, u32[]{:S(2)}, u32[]{:S(2)}) %collective-permute-start.12) | collective-permute-done | bytes 32800 | tf_op jit(solution)/shard_map/ppermute | solution.py:410
  58.3 2.3 %collective-permute-done.13 = bf16[128,128]{1,0:T(8,128)(2,1)S(1)} collective-permute-done((bf16[128,128]{1,0:T(8,128)(2,1)S(1)}, bf16[128,128]{1,0:T(8,128)(2,1)S(1)}, u32[]{:S(2)}, u32[]{:S(2)}) %collective-permute-start.13) | collective-permute-done | bytes 32800 | tf_op jit(solution)/shard_map/ppermute | solution.py:410
  60.5 0.8 fusion.2
  61.3 4.1 %collective-permute-start.15 = (bf16[2,128,128]{2,1,0:T(8,128)(2,1)S(1)}, bf16[2,128,128]{2,1,0:T(8,128)(2,1)S(1)}, u32[]{:S(2)}, u32[]{:S(2)}) collective-permute-start(bf16[2,128,128]{2,1,0:T(8,128)(2,1)S(1)} %pad_maximum_fusion.6), channel_id=1, source_target_pairs={{0,4},{4,0},{8,12},{12,8},{16,20},{20,16},{24,28},{28,24},{1,5},{5... | collective-permute-start | bytes 196616 | tf_op jit(solution)/shard_map/ppermute | solution.py:425
  65.5 1.4 %copy-done.1 = bf16[11,128,512]{2,1,0:T(8,128)(2,1)S(1)} copy-done((bf16[11,128,512]{2,1,0:T(8,128)(2,1)S(1)}, bf16[11,128,512]{2,1,0:T(8,128)(2,1)}, u32[]{:S(2)}) %copy-start.1) | copy-done | bytes 1441816
  66.8 0.7 mid_second.1
  67.6 3.2 %collective-permute-start.16 = (bf16[2,128,128]{2,1,0:T(8,128)(2,1)S(1)}, bf16[2,128,128]{2,1,0:T(8,128)(2,1)S(1)}, u32[]{:S(2)}, u32[]{:S(2)}) collective-permute-start(bf16[2,128,128]{2,1,0:T(8,128)(2,1)S(1)} %fusion.13.refs_0_), channel_id=1, source_target_pairs={{0,8},{4,12},{8,0},{12,4},{16,24},{20,28},{24,16},{28,20},{1,9},{5... | collective-permute-start | bytes 196616 | tf_op jit(solution)/shard_map/ppermute | solution.py:427
  70.8 0.9 collective-permute-start.17
  71.7 1.2 %collective-permute-start.18 = (bf16[2,128,128]{2,1,0:T(8,128)(2,1)S(1)}, bf16[2,128,128]{2,1,0:T(8,128)(2,1)S(1)}, u32[]{:S(2)}, u32[]{:S(2)}) collective-permute-start(bf16[2,128,128]{2,1,0:T(8,128)(2,1)S(1)} %fusion.13.refs_0_), channel_id=1, source_target_pairs={{0,24},{4,28},{8,16},{12,20},{16,8},{20,12},{24,0},{28,4},{1,25},{... | collective-permute-start | bytes 196616 | tf_op jit(solution)/shard_map/ppermute | solution.py:427
  73.0 1.3 %collective-permute-start.9 = (bf16[8,128,128]{2,1,0:T(8,128)(2,1)S(1)}, bf16[8,128,128]{2,1,0:T(8,128)(2,1)S(1)}, u32[]{:S(2)}, u32[]{:S(2)}) collective-permute-start(bf16[8,128,128]{2,1,0:T(8,128)(2,1)S(1)} %get-tuple-element.68), channel_id=1, source_target_pairs={{1,0},{2,3},{5,4},{6,7},{9,8},{10,11},{13,12},{14,15},{17,16},{18,... | collective-permute-start | bytes 786440 | tf_op jit(solution)/shard_map/ppermute | solution.py:410
  74.3 1.3 %collective-permute-start.10 = (bf16[8,128,128]{2,1,0:T(8,128)(2,1)S(1)}, bf16[8,128,128]{2,1,0:T(8,128)(2,1)S(1)}, u32[]{:S(2)}, u32[]{:S(2)}) collective-permute-start(bf16[8,128,128]{2,1,0:T(8,128)(2,1)S(1)} %get-tuple-element.67), channel_id=1, source_target_pairs={{1,3},{2,0},{5,7},{6,4},{9,11},{10,8},{13,15},{14,12},{17,19},{18,... | collective-permute-start | bytes 786440 | tf_op jit(solution)/shard_map/ppermute | solution.py:410
  75.6 0.7 collective-permute-start.11
  76.3 3.5 %shard_map.77.refs_4_ = bf16[256,16384]{1,0:T(8,128)(2,1)S(1)} custom-call(bf16[384,16384]{1,0:T(8,128)(2,1)} %bitcast.73), custom_call_target="tpu_custom_call" | custom-call | tf_op jit(solution)/shard_map/pallas_call | solution.py:330
  79.8 2.3 %shard_map.78.refs_5_ = bf16[256,8192]{1,0:T(8,128)(2,1)S(1)} custom-call(bf16[384,16384]{1,0:T(8,128)(2,1)} %bitcast.74), custom_call_target="tpu_custom_call" | custom-call | tf_op jit(solution)/shard_map/pallas_call | solution.py:330
  82.1 3.4 %fit_sums.1 = f32[2,2,384]{2,1,0:T(2,128)S(1)} custom-call(s32[1]{0:T(128)} %bitcast.place, bf16[2,128,128]{2,1,0:T(8,128)(2,1)S(1)} %fusion.13.refs_0_, bf16[2,128,128]{2,1,0:T(8,128)(2,1)S(1)} %collective-permute-done.16.refs_1_, bf16[2,128,128]{2,1,0:T(8,128)(2,1)S(1)} %collective-permute-done.17.refs_2_, ...), custom_call_target="tpu_custom_call" | custom-call | tf_op jit(solution)/shard_map/fit_sums/pallas_call | solution.py:430
  85.4 1.2 %collective-permute-done.19 = f32[2,2,384]{2,1,0:T(2,128)S(1)} collective-permute-done((f32[2,2,384]{2,1,0:T(2,128)S(1)}, f32[2,2,384]{2,1,0:T(2,128)S(1)}, u32[]{:S(2)}, u32[]{:S(2)}) %collective-permute-start.19) | collective-permute-done | bytes 6176 | tf_op jit(solution)/shard_map/ppermute | solution.py:438
  86.6 1.4 %collective-permute-start.20 = (f32[2,2,384]{2,1,0:T(2,128)S(1)}, f32[2,2,384]{2,1,0:T(2,128)S(1)}, u32[]{:S(2)}, u32[]{:S(2)}) collective-permute-start(f32[2,2,384]{2,1,0:T(2,128)S(1)} %add.68.refs_0_), channel_id=1, source_target_pairs={{0,8},{4,12},{8,0},{12,4},{16,24},{20,28},{24,16},{28,20},{1,9},{5... | collective-permute-start | bytes 18440 | tf_op jit(solution)/shard_map/ppermute | solution.py:440
  88.0 0.9 collective-permute-start.21
  88.9 1.4 %collective-permute-done.20.refs_1_ = f32[2,2,384]{2,1,0:T(2,128)S(1)} collective-permute-done((f32[2,2,384]{2,1,0:T(2,128)S(1)}, f32[2,2,384]{2,1,0:T(2,128)S(1)}, u32[]{:S(2)}, u32[]{:S(2)}) %collective-permute-start.20) | collective-permute-done | bytes 6176 | tf_op jit(solution)/shard_map/ppermute | solution.py:440
  90.2 1.7 %collective-permute-start.22 = (f32[2,2,384]{2,1,0:T(2,128)S(1)}, f32[2,2,384]{2,1,0:T(2,128)S(1)}, u32[]{:S(2)}, u32[]{:S(2)}) collective-permute-start(f32[2,2,384]{2,1,0:T(2,128)S(1)} %add.68.refs_0_), channel_id=1, source_target_pairs={{0,24},{4,28},{8,16},{12,20},{16,8},{20,12},{24,0},{28,4},{1,25},{... | collective-permute-start | bytes 18440 | tf_op jit(solution)/shard_map/ppermute | solution.py:440
  91.9 2.4 %shard_map.79.refs_4_ = f32[384,3072]{1,0:T(8,128)S(1)} custom-call(f32[384,3072]{1,0:T(8,128)} %bitcast.75), custom_call_target="tpu_custom_call" | custom-call | tf_op jit(solution)/shard_map/pallas_call | solution.py:330
  94.8 0.9 metric.1
  95.6 1.5 %collective-permute-start.23 = (f32[2,384]{1,0:T(2,128)S(1)}, f32[2,384]{1,0:T(2,128)S(1)}, u32[]{:S(2)}, u32[]{:S(2)}) collective-permute-start(f32[2,384]{1,0:T(2,128)S(1)} %metric.1), channel_id=1, source_target_pairs={{0,3},{1,2},{2,1},{3,0},{4,7},{5,6},{6,5},{7,4},{8,11},{9,10},{10,... | collective-permute-start | bytes 9224 | tf_op jit(solution)/shard_map/ppermute | solution.py:453
  97.1 7.1 %collective-permute-start.24 = (f32[2,384]{1,0:T(2,128)S(1)}, f32[2,384]{1,0:T(2,128)S(1)}, u32[]{:S(2)}, u32[]{:S(2)}) collective-permute-start(f32[2,384]{1,0:T(2,128)S(1)} %metric.1), channel_id=1, source_target_pairs={{0,2},{1,3},{2,0},{3,1},{4,6},{5,7},{6,4},{7,5},{8,10},{9,11},{10,... | collective-permute-start | bytes 9224 | tf_op jit(solution)/shard_map/ppermute | solution.py:453
  104.2 2.1 %collective-permute-start.25 = (f32[2,384]{1,0:T(2,128)S(1)}, f32[2,384]{1,0:T(2,128)S(1)}, u32[]{:S(2)}, u32[]{:S(2)}) collective-permute-start(f32[2,384]{1,0:T(2,128)S(1)} %metric.1), channel_id=1, source_target_pairs={{0,1},{1,0},{2,3},{3,2},{4,5},{5,4},{6,7},{7,6},{8,9},{9,8},{10,11... | collective-permute-start | bytes 9224 | tf_op jit(solution)/shard_map/ppermute | solution.py:453
  106.3 1.6 %collective-permute-done.25 = f32[2,384]{1,0:T(2,128)S(1)} collective-permute-done((f32[2,384]{1,0:T(2,128)S(1)}, f32[2,384]{1,0:T(2,128)S(1)}, u32[]{:S(2)}, u32[]{:S(2)}) %collective-permute-start.25) | collective-permute-done | bytes 3104 | tf_op jit(solution)/shard_map/ppermute | solution.py:453
  108.5 0.8 maximum_bitcast_fusion
  (60 shorter events, 2.4 us)
Async XLA Ops:
  2.0 14.2 %collective-permute-start.3 = (bf16[16,128,128]{2,1,0:T(8,128)(2,1)S(1)}, bf16[16,128,128]{2,1,0:T(8,128)(2,1)S(1)}, u32[]{:S(2)}, u32[]{:S(2)}) collective-permute-start(bf16[16,128,128]{2,1,0:T(8,128)(2,1)S(1)} %get-tuple-element.31), channel_id=1, source_target_pairs={{1,2},{2,1},{5,6},{6,5},{9,10},{10,9},{13,14},{14,13},{17,18},{18,... | collective-permute-start | bytes 1572872 | tf_op jit(solution)/shard_map/ppermute | solution.py:308
  2.7 31.3 %collective-permute-start.6 = (bf16[16,128,128]{2,1,0:T(8,128)(2,1)S(1)}, bf16[16,128,128]{2,1,0:T(8,128)(2,1)S(1)}, u32[]{:S(2)}, u32[]{:S(2)}) collective-permute-start(bf16[16,128,128]{2,1,0:T(8,128)(2,1)S(1)} %get-tuple-element.31), channel_id=1, source_target_pairs={{0,2},{3,1},{4,6},{7,5},{8,10},{11,9},{12,14},{15,13},{16,18},{19,... | collective-permute-start | bytes 1572872 | tf_op jit(solution)/shard_map/ppermute | solution.py:308
  10.4 22.1 %collective-permute-start.2 = (bf16[16,128,128]{2,1,0:T(8,128)(2,1)S(1)}, bf16[16,128,128]{2,1,0:T(8,128)(2,1)S(1)}, u32[]{:S(2)}, u32[]{:S(2)}) collective-permute-start(bf16[16,128,128]{2,1,0:T(8,128)(2,1)S(1)} %get-tuple-element.30.refs_2_), channel_id=1, source_target_pairs={{0,1},{3,2},{4,5},{7,6},{8,9},{11,10},{12,13},{15,14},{16,17},{19,... | collective-permute-start | bytes 1572872 | tf_op jit(solution)/shard_map/ppermute | solution.py:307
  12.6 3.5 %collective-permute-start.1 = (bf16[5,128,128]{2,1,0:T(8,128)(2,1)S(1)}, bf16[5,128,128]{2,1,0:T(8,128)(2,1)S(1)}, u32[]{:S(2)}, u32[]{:S(2)}) collective-permute-start(bf16[5,128,128]{2,1,0:T(8,128)(2,1)S(1)} %pad_maximum_fusion.4), channel_id=1, source_target_pairs={{5,1},{6,2},{9,5},{10,6},{13,9},{14,10},{17,13},{18,14},{21,17},{2... | collective-permute-start | bytes 491528 | tf_op jit(solution)/shard_map/ppermute | solution.py:287
  13.3 2.8 %collective-permute-start = (bf16[9,128,128]{2,1,0:T(8,128)(2,1)S(1)}, bf16[9,128,128]{2,1,0:T(8,128)(2,1)S(1)}, u32[]{:S(2)}, u32[]{:S(2)}) collective-permute-start(bf16[9,128,128]{2,1,0:T(8,128)(2,1)S(1)} %pad_maximum_fusion.1), channel_id=1, source_target_pairs={{1,5},{2,6},{5,9},{6,10},{9,13},{10,14},{13,17},{14,18},{17,21},{1... | collective-permute-start | bytes 884744 | tf_op jit(solution)/shard_map/ppermute | solution.py:286
  16.0 19.4 %copy-start.7 = (s32[11]{0:T(128)S(1)}, s32[11]{0:T(128)}, u32[]{:S(2)}) copy-start(s32[11]{0:T(128)} %iota_add_fusion) | copy-start | bytes 136
  16.1 19.5 %copy-start.4 = (bf16[5,128,128]{2,1,0:T(8,128)(2,1)}, bf16[5,128,128]{2,1,0:T(8,128)(2,1)S(1)}, u32[]{:S(2)}) copy-start(bf16[5,128,128]{2,1,0:T(8,128)(2,1)S(1)} %collective-permute-done.1.refs_1_) | copy-start | bytes 491524
  16.1 19.5 %copy-start.2 = (bf16[9,128,128]{2,1,0:T(8,128)(2,1)}, bf16[9,128,128]{2,1,0:T(8,128)(2,1)S(1)}, u32[]{:S(2)}) copy-start(bf16[9,128,128]{2,1,0:T(8,128)(2,1)S(1)} %collective-permute-done.refs_0_) | copy-start | bytes 884740
  32.5 3.1 %collective-permute-start.4 = (bf16[16,128,128]{2,1,0:T(8,128)(2,1)S(1)}, bf16[16,128,128]{2,1,0:T(8,128)(2,1)S(1)}, u32[]{:S(2)}, u32[]{:S(2)}) collective-permute-start(bf16[16,128,128]{2,1,0:T(8,128)(2,1)S(1)} %pad_maximum_fusion), channel_id=1, source_target_pairs={{1,5},{2,6},{5,9},{6,10},{9,13},{10,14},{13,17},{14,18},{17,21},{1... | collective-permute-start | bytes 1572872 | tf_op jit(solution)/shard_map/ppermute | solution.py:286
  33.3 2.3 %collective-permute-start.5 = (bf16[8,128,128]{2,1,0:T(8,128)(2,1)S(1)}, bf16[8,128,128]{2,1,0:T(8,128)(2,1)S(1)}, u32[]{:S(2)}, u32[]{:S(2)}) collective-permute-start(bf16[8,128,128]{2,1,0:T(8,128)(2,1)S(1)} %pad_maximum_fusion.2), channel_id=1, source_target_pairs={{5,1},{6,2},{9,5},{10,6},{13,9},{14,10},{17,13},{18,14},{21,17},{2... | collective-permute-start | bytes 786440 | tf_op jit(solution)/shard_map/ppermute | solution.py:287
  34.1 1.5 %collective-permute-start.7 = (bf16[8,128,128]{2,1,0:T(8,128)(2,1)S(1)}, bf16[8,128,128]{2,1,0:T(8,128)(2,1)S(1)}, u32[]{:S(2)}, u32[]{:S(2)}) collective-permute-start(bf16[8,128,128]{2,1,0:T(8,128)(2,1)S(1)} %pad_maximum_fusion.3), channel_id=1, source_target_pairs={{1,5},{2,6},{5,9},{6,10},{9,13},{10,14},{13,17},{14,18},{17,21},{1... | collective-permute-start | bytes 786440 | tf_op jit(solution)/shard_map/ppermute | solution.py:286
  34.8 0.8 collective-permute-start.8
  35.6 1.0 copy-start.3
  36.6 0.9 copy-start.5
  38.4 1.2 %copy-start = (bf16[11,128,512]{2,1,0:T(8,128)(2,1)}, bf16[11,128,512]{2,1,0:T(8,128)(2,1)S(1)}, u32[]{:S(2)}) copy-start(bf16[11,128,512]{2,1,0:T(8,128)(2,1)S(1)} %get-tuple-element.33.order) | copy-start | bytes 4325380
  39.6 0.7 copy-start.6
  40.2 18.0 %collective-permute-start.12 = (bf16[128,128]{1,0:T(8,128)(2,1)S(1)}, bf16[128,128]{1,0:T(8,128)(2,1)S(1)}, u32[]{:S(2)}, u32[]{:S(2)}) collective-permute-start(bf16[128,128]{1,0:T(8,128)(2,1)S(1)} %get-tuple-element.89), channel_id=1, source_target_pairs={{1,0},{2,3},{5,4},{6,7},{9,8},{10,11},{13,12},{14,15},{17,16},{18,... | collective-permute-start | bytes 98312 | tf_op jit(solution)/shard_map/ppermute | solution.py:410
  41.5 19.0 %collective-permute-start.13 = (bf16[128,128]{1,0:T(8,128)(2,1)S(1)}, bf16[128,128]{1,0:T(8,128)(2,1)S(1)}, u32[]{:S(2)}, u32[]{:S(2)}) collective-permute-start(bf16[128,128]{1,0:T(8,128)(2,1)S(1)} %get-tuple-element.88), channel_id=1, source_target_pairs={{1,3},{2,0},{5,7},{6,4},{9,11},{10,8},{13,15},{14,12},{17,19},{18,... | collective-permute-start | bytes 98312 | tf_op jit(solution)/shard_map/ppermute | solution.py:410
  42.8 17.7 %collective-permute-start.14 = (bf16[128,128]{1,0:T(8,128)(2,1)S(1)}, bf16[128,128]{1,0:T(8,128)(2,1)S(1)}, u32[]{:S(2)}, u32[]{:S(2)}) collective-permute-start(bf16[128,128]{1,0:T(8,128)(2,1)S(1)} %get-tuple-element.87), channel_id=1, source_target_pairs={{1,2},{2,1},{5,6},{6,5},{9,10},{10,9},{13,14},{14,13},{17,18},{18,... | collective-permute-start | bytes 98312 | tf_op jit(solution)/shard_map/ppermute | solution.py:410
  61.3 6.2 %collective-permute-start.15 = (bf16[2,128,128]{2,1,0:T(8,128)(2,1)S(1)}, bf16[2,128,128]{2,1,0:T(8,128)(2,1)S(1)}, u32[]{:S(2)}, u32[]{:S(2)}) collective-permute-start(bf16[2,128,128]{2,1,0:T(8,128)(2,1)S(1)} %pad_maximum_fusion.6), channel_id=1, source_target_pairs={{0,4},{4,0},{8,12},{12,8},{16,20},{20,16},{24,28},{28,24},{1,5},{5... | collective-permute-start | bytes 196616 | tf_op jit(solution)/shard_map/ppermute | solution.py:425
  65.5 1.4 %copy-start.1 = (bf16[11,128,512]{2,1,0:T(8,128)(2,1)S(1)}, bf16[11,128,512]{2,1,0:T(8,128)(2,1)}, u32[]{:S(2)}) copy-start(bf16[11,128,512]{2,1,0:T(8,128)(2,1)} %copy-done) | copy-start | bytes 4325380
  67.6 8.0 %collective-permute-start.16 = (bf16[2,128,128]{2,1,0:T(8,128)(2,1)S(1)}, bf16[2,128,128]{2,1,0:T(8,128)(2,1)S(1)}, u32[]{:S(2)}, u32[]{:S(2)}) collective-permute-start(bf16[2,128,128]{2,1,0:T(8,128)(2,1)S(1)} %fusion.13.refs_0_), channel_id=1, source_target_pairs={{0,8},{4,12},{8,0},{12,4},{16,24},{20,28},{24,16},{28,20},{1,9},{5... | collective-permute-start | bytes 196616 | tf_op jit(solution)/shard_map/ppermute | solution.py:427
  70.8 11.2 %collective-permute-start.17 = (bf16[2,128,128]{2,1,0:T(8,128)(2,1)S(1)}, bf16[2,128,128]{2,1,0:T(8,128)(2,1)S(1)}, u32[]{:S(2)}, u32[]{:S(2)}) collective-permute-start(bf16[2,128,128]{2,1,0:T(8,128)(2,1)S(1)} %fusion.13.refs_0_), channel_id=1, source_target_pairs={{0,16},{4,20},{8,24},{12,28},{16,0},{20,4},{24,8},{28,12},{1,17},{... | collective-permute-start | bytes 196616 | tf_op jit(solution)/shard_map/ppermute | solution.py:427
  71.7 10.4 %collective-permute-start.18 = (bf16[2,128,128]{2,1,0:T(8,128)(2,1)S(1)}, bf16[2,128,128]{2,1,0:T(8,128)(2,1)S(1)}, u32[]{:S(2)}, u32[]{:S(2)}) collective-permute-start(bf16[2,128,128]{2,1,0:T(8,128)(2,1)S(1)} %fusion.13.refs_0_), channel_id=1, source_target_pairs={{0,24},{4,28},{8,16},{12,20},{16,8},{20,12},{24,0},{28,4},{1,25},{... | collective-permute-start | bytes 196616 | tf_op jit(solution)/shard_map/ppermute | solution.py:427
  73.0 35.5 %collective-permute-start.9 = (bf16[8,128,128]{2,1,0:T(8,128)(2,1)S(1)}, bf16[8,128,128]{2,1,0:T(8,128)(2,1)S(1)}, u32[]{:S(2)}, u32[]{:S(2)}) collective-permute-start(bf16[8,128,128]{2,1,0:T(8,128)(2,1)S(1)} %get-tuple-element.68), channel_id=1, source_target_pairs={{1,0},{2,3},{5,4},{6,7},{9,8},{10,11},{13,12},{14,15},{17,16},{18,... | collective-permute-start | bytes 786440 | tf_op jit(solution)/shard_map/ppermute | solution.py:410
  74.3 34.2 %collective-permute-start.10 = (bf16[8,128,128]{2,1,0:T(8,128)(2,1)S(1)}, bf16[8,128,128]{2,1,0:T(8,128)(2,1)S(1)}, u32[]{:S(2)}, u32[]{:S(2)}) collective-permute-start(bf16[8,128,128]{2,1,0:T(8,128)(2,1)S(1)} %get-tuple-element.67), channel_id=1, source_target_pairs={{1,3},{2,0},{5,7},{6,4},{9,11},{10,8},{13,15},{14,12},{17,19},{18,... | collective-permute-start | bytes 786440 | tf_op jit(solution)/shard_map/ppermute | solution.py:410
  75.6 32.9 %collective-permute-start.11 = (bf16[8,128,128]{2,1,0:T(8,128)(2,1)S(1)}, bf16[8,128,128]{2,1,0:T(8,128)(2,1)S(1)}, u32[]{:S(2)}, u32[]{:S(2)}) collective-permute-start(bf16[8,128,128]{2,1,0:T(8,128)(2,1)S(1)} %get-tuple-element.66), channel_id=1, source_target_pairs={{1,2},{2,1},{5,6},{6,5},{9,10},{10,9},{13,14},{14,13},{17,18},{18,... | collective-permute-start | bytes 786440 | tf_op jit(solution)/shard_map/ppermute | solution.py:410
  85.4 1.2 %collective-permute-start.19 = (f32[2,2,384]{2,1,0:T(2,128)S(1)}, f32[2,2,384]{2,1,0:T(2,128)S(1)}, u32[]{:S(2)}, u32[]{:S(2)}) collective-permute-start(f32[2,2,384]{2,1,0:T(2,128)S(1)} %fit_sums.1), channel_id=1, source_target_pairs={{0,4},{4,0},{8,12},{12,8},{16,20},{20,16},{24,28},{28,24},{1,5},{5... | collective-permute-start | bytes 18440 | tf_op jit(solution)/shard_map/ppermute | solution.py:438
  86.6 3.6 %collective-permute-start.20 = (f32[2,2,384]{2,1,0:T(2,128)S(1)}, f32[2,2,384]{2,1,0:T(2,128)S(1)}, u32[]{:S(2)}, u32[]{:S(2)}) collective-permute-start(f32[2,2,384]{2,1,0:T(2,128)S(1)} %add.68.refs_0_), channel_id=1, source_target_pairs={{0,8},{4,12},{8,0},{12,4},{16,24},{20,28},{24,16},{28,20},{1,9},{5... | collective-permute-start | bytes 18440 | tf_op jit(solution)/shard_map/ppermute | solution.py:440
  88.0 6.3 %collective-permute-start.21 = (f32[2,2,384]{2,1,0:T(2,128)S(1)}, f32[2,2,384]{2,1,0:T(2,128)S(1)}, u32[]{:S(2)}, u32[]{:S(2)}) collective-permute-start(f32[2,2,384]{2,1,0:T(2,128)S(1)} %add.68.refs_0_), channel_id=1, source_target_pairs={{0,16},{4,20},{8,24},{12,28},{16,0},{20,4},{24,8},{28,12},{1,17},{... | collective-permute-start | bytes 18440 | tf_op jit(solution)/shard_map/ppermute | solution.py:440
  90.2 4.5 %collective-permute-start.22 = (f32[2,2,384]{2,1,0:T(2,128)S(1)}, f32[2,2,384]{2,1,0:T(2,128)S(1)}, u32[]{:S(2)}, u32[]{:S(2)}) collective-permute-start(f32[2,2,384]{2,1,0:T(2,128)S(1)} %add.68.refs_0_), channel_id=1, source_target_pairs={{0,24},{4,28},{8,16},{12,20},{16,8},{20,12},{24,0},{28,4},{1,25},{... | collective-permute-start | bytes 18440 | tf_op jit(solution)/shard_map/ppermute | solution.py:440
  95.6 8.5 %collective-permute-start.23 = (f32[2,384]{1,0:T(2,128)S(1)}, f32[2,384]{1,0:T(2,128)S(1)}, u32[]{:S(2)}, u32[]{:S(2)}) collective-permute-start(f32[2,384]{1,0:T(2,128)S(1)} %metric.1), channel_id=1, source_target_pairs={{0,3},{1,2},{2,1},{3,0},{4,7},{5,6},{6,5},{7,4},{8,11},{9,10},{10,... | collective-permute-start | bytes 9224 | tf_op jit(solution)/shard_map/ppermute | solution.py:453
  97.1 9.2 %collective-permute-start.24 = (f32[2,384]{1,0:T(2,128)S(1)}, f32[2,384]{1,0:T(2,128)S(1)}, u32[]{:S(2)}, u32[]{:S(2)}) collective-permute-start(f32[2,384]{1,0:T(2,128)S(1)} %metric.1), channel_id=1, source_target_pairs={{0,2},{1,3},{2,0},{3,1},{4,6},{5,7},{6,4},{7,5},{8,10},{9,11},{10,... | collective-permute-start | bytes 9224 | tf_op jit(solution)/shard_map/ppermute | solution.py:453
  104.2 3.7 %collective-permute-start.25 = (f32[2,384]{1,0:T(2,128)S(1)}, f32[2,384]{1,0:T(2,128)S(1)}, u32[]{:S(2)}, u32[]{:S(2)}) collective-permute-start(f32[2,384]{1,0:T(2,128)S(1)} %metric.1), channel_id=1, source_target_pairs={{0,1},{1,0},{2,3},{3,2},{4,5},{5,4},{6,7},{7,6},{8,9},{9,8},{10,11... | collective-permute-start | bytes 9224 | tf_op jit(solution)/shard_map/ppermute | solution.py:453
